TPU v7x, 128 devices: a whole 4x4x4 slice. The times are simulated.
128 devices in a mesh: row: 8 (over y, x_hi), col: 16 (over z, x_lo, core).
Axes of the slice: x: 4 (x_hi: 2, x_lo: 2; x = x_hi * 2 + x_lo), y: 4, z: 4, core: 2. Of those that a mesh axis runs over, the one named last changes fastest.
Arguments:
- object_tiles: float32 [2, 2, 2048, 4096], P(None, None, 'row', 'col'), may hold values from -5 to 5
- probe_modes: float32 [2, 4, 128, 128], replicated, may hold values from -6 to 6
- offsets: int32 [8, 16, 3, 2], P('row', 'col'), may hold values from 0 to 192
- amplitude: float32 [8, 16, 3, 128, 128], P('row', 'col'), may hold values from 0.2 to 3
Outputs:
- object_grad: float32 [2, 2, 2048, 4096], P(None, None, 'row', 'col')
- probe_new: float32 [2, 4, 128, 128], replicated
All inputs are finite; a program needn't handle non-finite values.
Results may differ from a plain program's by a relative error of at most 0.0003.
Values sent between devices are 32-bit elements; how exact they have to be, the bound alone decides.
No kernel may reach another device: no remote copies, remote signals or barrier semaphores. Data moves between devices by JAX's collectives and lax.ppermute only.
A program may use at most 64 MiB of HBM per device.

v0:
```python
import jax
import jax.numpy as jnp
from jax import lax
from jax.sharding import PartitionSpec as P

HALO = 32
WIN = 128
MODES = 4
SLICES = 2


PROP = 0.002
SHIFT_AMP = 0.5
STEP_SIZE = 0.5
EPSILON = 1e-06
HIGH = lax.Precision.HIGHEST


def padded(cells, sides, width):
    for axis, dim in sides:
        count = lax.axis_size(axis)
        head = lax.slice_in_dim(cells, 0, width, axis=dim)
        tail = lax.slice_in_dim(cells, cells.shape[dim] - width, cells.shape[dim], axis=dim)
        cells = jnp.concatenate(
            [
                lax.ppermute(tail, axis, [(i, (i + 1) % count) for i in range(count)]),
                cells,
                lax.ppermute(head, axis, [((i + 1) % count, i) for i in range(count)]),
            ],
            axis=dim,
        )
    return cells


def shifted(block, axis, distance):
    devices = range(lax.axis_size(axis))
    route = [((i - distance) % len(devices), i) for i in devices]
    return lax.ppermute(block, axis, route)


def tables():
    counter = jnp.arange(WIN, dtype=jnp.int32)
    product = counter[:, None] * counter[None, :] % WIN
    angles = product.astype(jnp.float32) * (2.0 * jnp.pi / WIN)
    scale_factor = 1.0 / jnp.sqrt(jnp.float32(WIN))
    cos_table = jnp.cos(angles) * scale_factor
    sin_table = jnp.sin(angles) * scale_factor
    frequency = ((counter + WIN // 2) % WIN - WIN // 2).astype(jnp.float32)
    phase_map = -PROP * (frequency[:, None] ** 2 + frequency[None, :] ** 2)
    return (cos_table, sin_table, jnp.cos(phase_map), jnp.sin(phase_map))


def matprod(left_op, right_op):
    return jnp.matmul(left_op, right_op, precision=HIGH)


def transform(wave_real, wave_imag, sign_value, cos_table, sin_table):
    first_real = matprod(cos_table, wave_real) + sign_value * matprod(sin_table, wave_imag)
    first_imag = matprod(cos_table, wave_imag) - sign_value * matprod(sin_table, wave_real)
    second_real = matprod(first_real, cos_table) + sign_value * matprod(first_imag, sin_table)
    second_imag = matprod(first_imag, cos_table) - sign_value * matprod(first_real, sin_table)
    return (second_real, second_imag)


def position_loss(window, probe_field, measured, table_set):
    cos_table, sin_table, prop_cos, prop_sin = table_set
    probe_real = probe_field[0]
    probe_imag = probe_field[1]
    wave_real = probe_real * window[0, 0] - probe_imag * window[1, 0]
    wave_imag = probe_real * window[1, 0] + probe_imag * window[0, 0]
    wave_real, wave_imag = transform(wave_real, wave_imag, 1.0, cos_table, sin_table)
    turned_real = wave_real * prop_cos - wave_imag * prop_sin
    turned_imag = wave_real * prop_sin + wave_imag * prop_cos
    wave_real, wave_imag = transform(turned_real, turned_imag, -1.0, cos_table, sin_table)
    slice_real = window[0, 1]
    slice_imag = window[1, 1]
    wave_real, wave_imag = (
        wave_real * slice_real - wave_imag * slice_imag,
        wave_real * slice_imag + wave_imag * slice_real,
    )
    far_real, far_imag = transform(wave_real, wave_imag, 1.0, cos_table, sin_table)
    intensity = jnp.sum(far_real * far_real + far_imag * far_imag, axis=0)
    return jnp.sum((jnp.sqrt(intensity + SHIFT_AMP) - measured) ** 2)


def on_device(object_tiles, probe_modes, offsets, amplitude):
    table_set = tables()
    tile_size = object_tiles.shape[2]
    extended = padded(object_tiles, (("row", 2), ("col", 3)), HALO)

    def local_loss(ext_tiles, probe_field):
        loss_sum = jnp.zeros((), jnp.float32)
        anchor = jnp.zeros((), jnp.int32)
        for scan_no in range(offsets.shape[2]):
            row_start = offsets[0, 0, scan_no, 0]
            col_start = offsets[0, 0, scan_no, 1]
            window = lax.dynamic_slice(
                ext_tiles, (anchor, anchor, row_start, col_start), (2, SLICES, WIN, WIN)
            )
            loss_sum = loss_sum + position_loss(
                window, probe_field, amplitude[0, 0, scan_no], table_set
            )
        return loss_sum

    loss_value, pullback = jax.vjp(local_loss, extended, probe_modes)
    grad_ext, grad_probe = pullback(jnp.ones_like(loss_value))
    top_rim = grad_ext[:, :, :HALO]
    bottom_rim = grad_ext[:, :, tile_size + HALO :]
    middle = grad_ext[:, :, HALO : tile_size + HALO]
    from_below = shifted(top_rim, "row", -1)
    from_above = shifted(bottom_rim, "row", 1)
    middle = middle.at[:, :, tile_size - HALO :].add(from_below)
    middle = middle.at[:, :, :HALO].add(from_above)
    left_rim = middle[:, :, :, :HALO]
    right_rim = middle[:, :, :, tile_size + HALO :]
    center = middle[:, :, :, HALO : tile_size + HALO]
    from_right = shifted(left_rim, "col", -1)
    from_left = shifted(right_rim, "col", 1)
    center = center.at[:, :, :, tile_size - HALO :].add(from_right)
    object_grad = center.at[:, :, :, :HALO].add(from_left)
    entries = 2 * MODES * WIN * WIN
    grad_total = lax.psum(grad_probe, ("row", "col"))
    mean_square = jnp.sum(grad_total * grad_total) / entries
    probe_new = probe_modes - STEP_SIZE * grad_total / jnp.sqrt(mean_square + EPSILON)
    return (object_grad, probe_new)


def solution(mesh):
    placed = (
        P(None, None, "row", "col"),
        P(),
        P("row", "col", None, None),
        P("row", "col", None, None, None),
    )
    return jax.shard_map(
        on_device,
        mesh=mesh,
        in_specs=placed,
        out_specs=(P(None, None, "row", "col"), P()),
        check_vma=False,
    )
```

profile of v0, /device:TPU:1, one launch (start us, length us, event | category | flops | bytes accessed | tf_op | source)
XLA Modules:
  0.0 350.5 jit_solution(5730426143015588015)
XLA Ops:
  7.2 1.6 copy.175
  8.8 1.1 fusion.1090
  10.0 3.6 %collective-permute-start = (f32[2,2,32,256]{2,3,1,0:T(8,128)}, f32[2,2,32,256]{2,3,1,0:T(8,128)S(1)}, u32[]{:S(2)}, u32[]{:S(2)}) collective-permute-start(f32[2,2,32,256]{2,3,1,0:T(8,128)} %get-tuple-element.108), channel_id=1, source_target_pairs={{0,16},{16,32},{32,48},{48,64},{64,80},{80,96},{96,112},{112,0},{1... | collective-permute-start | bytes 393224 | tf_op jit(solution)/shard_map/ppermute | solution.py:26
  13.5 2.5 collective-permute-start.1
  28.1 9.4 %collective-permute-done.1 = f32[2,2,32,256]{2,3,1,0:T(8,128)S(1)} collective-permute-done((f32[2,2,32,256]{2,3,1,0:T(8,128)}, f32[2,2,32,256]{2,3,1,0:T(8,128)S(1)}, u32[]{:S(2)}, u32[]{:S(2)}) %collective-permute-start.1) | collective-permute-done | bytes 131104 | tf_op jit(solution)/shard_map/ppermute | solution.py:28
  37.8 2.7 collective-permute-start.2
  41.2 1.8 collective-permute-done.2
  43.1 4.2 %collective-permute-done.3 = f32[2,2,320,32]{2,3,1,0:T(8,128)S(1)} collective-permute-done((f32[2,2,320,32]{2,3,1,0:T(8,128)S(1)}, f32[2,2,320,32]{2,3,1,0:T(8,128)S(1)}, u32[]{:S(2)}, u32[]{:S(2)}) %collective-permute-start.3) | collective-permute-done | bytes 163872 | tf_op jit(solution)/shard_map/ppermute | solution.py:28
  47.8 1.0 dynamic-slice_bitcast_fusion.5
  60.9 0.9 fusion.300
  67.0 1.4 fusion.296
  68.4 0.9 copy.213
  69.3 0.9 copy.214
  71.6 1.6 fusion.41
  75.1 1.4 fusion.284
  76.4 1.4 fusion.288
  79.2 0.9 fusion.64
  83.3 1.4 fusion.333
  84.7 1.4 fusion.337
  86.1 0.9 copy.184
  87.1 1.6 fusion.61
  89.3 1.6 fusion.63
  97.5 1.1 fusion.34
  110.9 1.6 multiply_reduce_fusion.15
  119.5 0.7 fusion.82
  124.2 0.8 fusion.54
  125.7 1.4 multiply_reduce_fusion.23
  134.1 0.7 fusion.98
  137.5 1.1 fusion.78
  140.5 1.4 multiply_reduce_fusion.7
  149.0 0.7 fusion.66
  151.1 0.7 fusion.23
  151.8 0.9 fusion.22
  154.0 0.7 fusion.1
  154.7 0.7 fusion
  155.4 0.7 fusion.44
  156.2 2.1 add_bitcast_fusion.5
  158.7 0.7 copy.237
  160.9 0.7 copy.234
  161.8 0.7 copy.264
  162.9 3.1 dynamic_update_slice.11
  166.0 1.0 add_bitcast_fusion.8
  167.0 1.1 add_add_fusion.1
  168.1 3.1 add_any.542
  171.2 1.0 add_bitcast_fusion.6
  172.3 3.1 add_any.583
  175.4 0.8 fusion.1088
  176.8 4.6 %collective-permute-start.4 = (f32[2,2,32,320]{3,2,1,0:T(8,128)}, f32[2,2,32,320]{3,2,1,0:T(8,128)}, u32[]{:S(2)}, u32[]{:S(2)}) collective-permute-start(f32[2,2,32,320]{3,2,1,0:T(8,128)} %get-tuple-element.93), channel_id=1, source_target_pairs={{16,0},{32,16},{48,32},{64,48},{80,64},{96,80},{112,96},{0,112},{1... | collective-permute-start | bytes 491528 | tf_op jit(solution)/shard_map/ppermute | solution.py:38
  181.4 1.5 slice.268
  183.0 0.9 pad_add_fusion
  183.9 2.4 collective-permute-done.4
  186.4 1.0 fusion.118
  187.4 6.5 %collective-permute-done.5 = f32[2,2,32,320]{3,2,1,0:T(8,128)S(1)} collective-permute-done((f32[2,2,32,320]{3,2,1,0:T(8,128)S(1)}, f32[2,2,32,320]{3,2,1,0:T(8,128)S(1)}, u32[]{:S(2)}, u32[]{:S(2)}) %collective-permute-start.5) | collective-permute-done | bytes 163872 | tf_op jit(solution)/shard_map/ppermute | solution.py:38
  194.3 1.1 fusion.1089
  195.4 0.8 collective-permute-start.7
  196.2 132.9 %all-reduce.26.cloned.1.call-done = f32[2,4,128,128]{2,3,1,0:T(8,128)} async-done(((f32[2,4,128,128]{2,3,1,0:T(8,128)}), f32[2,4,128,128]{2,3,1,0:T(8,128)}) %all-reduce.26.cloned.1.call-update) | async-done | bytes 524304 | tf_op jit(solution)/shard_map/psum | solution.py:122
  329.2 1.8 multiply_reduce_fusion
  331.6 1.9 divide_subtract_fusion
  333.5 2.0 copy.270
  335.6 1.1 slice_add_fusion.1
  336.7 2.4 scatter-add.16
  339.1 1.1 slice_add_fusion
  340.2 2.3 scatter-add.19
  342.5 1.0 copy-done.1
  (187 shorter events, 82.5 us)
Async XLA Ops:
  7.2 8.8 %copy-start.17 = (s32[1,1,3,2]{2,3,1,0:T(2,128)S(1)}, s32[1,1,3,2]{2,3,1,0:T(2,128)}, u32[]{:S(2)}) copy-start(s32[1,1,3,2]{2,3,1,0:T(2,128)} %param.14) | copy-start | bytes 76
  7.2 17.0 %copy-start.8 = (f32[2,4,128,128]{3,2,1,0:T(8,128)S(1)}, f32[2,4,128,128]{3,2,1,0:T(8,128)}, u32[]{:S(2)}) copy-start(f32[2,4,128,128]{3,2,1,0:T(8,128)} %param.13) | copy-start | bytes 1572868
  7.2 322.0 %all-reduce.26.cloned.1.call-start = ((), (), s32[]{:S(2)}) async-start(), calls=%async_computation | async-start | bytes 1048576 | tf_op jit(solution)/shard_map/psum | solution.py:122
  10.0 18.2 %collective-permute-start = (f32[2,2,32,256]{2,3,1,0:T(8,128)}, f32[2,2,32,256]{2,3,1,0:T(8,128)S(1)}, u32[]{:S(2)}, u32[]{:S(2)}) collective-permute-start(f32[2,2,32,256]{2,3,1,0:T(8,128)} %get-tuple-element.108), channel_id=1, source_target_pairs={{0,16},{16,32},{32,48},{48,64},{64,80},{80,96},{96,112},{112,0},{1... | collective-permute-start | bytes 393224 | tf_op jit(solution)/shard_map/ppermute | solution.py:26
  13.5 24.0 %collective-permute-start.1 = (f32[2,2,32,256]{2,3,1,0:T(8,128)}, f32[2,2,32,256]{2,3,1,0:T(8,128)S(1)}, u32[]{:S(2)}, u32[]{:S(2)}) collective-permute-start(f32[2,2,32,256]{2,3,1,0:T(8,128)} %get-tuple-element.109), channel_id=1, source_target_pairs={{16,0},{32,16},{48,32},{64,48},{80,64},{96,80},{112,96},{0,112},{1... | collective-permute-start | bytes 393224 | tf_op jit(solution)/shard_map/ppermute | solution.py:28
  37.8 5.3 %collective-permute-start.2 = (f32[2,2,320,32]{2,3,1,0:T(8,128)S(1)}, f32[2,2,320,32]{2,3,1,0:T(8,128)S(1)}, u32[]{:S(2)}, u32[]{:S(2)}) collective-permute-start(f32[2,2,320,32]{2,3,1,0:T(8,128)S(1)} %get-tuple-element.90), channel_id=1, source_target_pairs={{0,1},{1,2},{2,3},{3,4},{4,5},{5,6},{6,7},{7,8},{8,9},{9,10},{10,1... | collective-permute-start | bytes 491528 | tf_op jit(solution)/shard_map/ppermute | solution.py:26
  40.5 6.8 %collective-permute-start.3 = (f32[2,2,320,32]{2,3,1,0:T(8,128)S(1)}, f32[2,2,320,32]{2,3,1,0:T(8,128)S(1)}, u32[]{:S(2)}, u32[]{:S(2)}) collective-permute-start(f32[2,2,320,32]{2,3,1,0:T(8,128)S(1)} %get-tuple-element.91), channel_id=1, source_target_pairs={{1,0},{2,1},{3,2},{4,3},{5,4},{6,5},{7,6},{8,7},{9,8},{10,9},{11,1... | collective-permute-start | bytes 491528 | tf_op jit(solution)/shard_map/ppermute | solution.py:28
  81.4 4.7 %copy-start.9 = (f32[128,128]{0,1:T(8,128)S(1)}, f32[128,128]{0,1:T(8,128)}, u32[]{:S(2)}) copy-start(f32[128,128]{0,1:T(8,128)} %get-tuple-element.100) | copy-start | bytes 196612
  94.2 3.3 copy-start.3
  95.5 3.7 %copy-start.2 = (f32[128,4,128]{2,0,1:T(8,128)S(1)}, f32[128,4,128]{2,0,1:T(8,128)}, u32[]{:S(2)}) copy-start(f32[128,4,128]{2,0,1:T(8,128)} %fusion.288) | copy-start | bytes 786436
  103.8 2.5 copy-start.15
  156.1 6.5 %copy-start.11 = (f32[128,128]{1,0:T(8,128)S(1)}, f32[128,128]{1,0:T(8,128)}, u32[]{:S(2)}) copy-start(f32[128,128]{1,0:T(8,128)} %get-tuple-element.86) | copy-start | bytes 196612
  156.2 6.5 %copy-start.12 = (f32[128,128]{1,0:T(8,128)S(1)}, f32[128,128]{1,0:T(8,128)}, u32[]{:S(2)}) copy-start(f32[128,128]{1,0:T(8,128)} %get-tuple-element.87) | copy-start | bytes 196612
  156.2 6.5 %copy-start.13 = (f32[128,128]{1,0:T(8,128)S(1)}, f32[128,128]{1,0:T(8,128)}, u32[]{:S(2)}) copy-start(f32[128,128]{1,0:T(8,128)} %get-tuple-element.88) | copy-start | bytes 196612
  156.2 6.5 %copy-start.14 = (f32[128,128]{1,0:T(8,128)S(1)}, f32[128,128]{1,0:T(8,128)}, u32[]{:S(2)}) copy-start(f32[128,128]{1,0:T(8,128)} %get-tuple-element.89) | copy-start | bytes 196612
  162.7 9.4 %copy-start.10 = (f32[128,128]{1,0:T(8,128)S(1)}, f32[128,128]{1,0:T(8,128)}, u32[]{:S(2)}) copy-start(f32[128,128]{1,0:T(8,128)} %copy.264) | copy-start | bytes 196612
  175.4 1.4 copy-start
  175.4 7.5 %copy-start.4 = (f32[1,4,128,128]{2,3,1,0:T(8,128)S(1)}, f32[1,4,128,128]{2,3,1,0:T(8,128)}, u32[]{:S(2)}) copy-start(f32[1,4,128,128]{2,3,1,0:T(8,128)} %get-tuple-element.128) | copy-start | bytes 786436
  175.4 7.5 %copy-start.5 = (f32[1,4,128,128]{2,3,1,0:T(8,128)S(1)}, f32[1,4,128,128]{2,3,1,0:T(8,128)}, u32[]{:S(2)}) copy-start(f32[1,4,128,128]{2,3,1,0:T(8,128)} %get-tuple-element.129) | copy-start | bytes 786436
  175.4 7.5 %copy-start.6 = (f32[1,4,128,128]{2,3,1,0:T(8,128)S(1)}, f32[1,4,128,128]{2,3,1,0:T(8,128)}, u32[]{:S(2)}) copy-start(f32[1,4,128,128]{2,3,1,0:T(8,128)} %get-tuple-element.130) | copy-start | bytes 786436
  175.4 7.5 %copy-start.7 = (f32[1,4,128,128]{2,3,1,0:T(8,128)S(1)}, f32[1,4,128,128]{2,3,1,0:T(8,128)}, u32[]{:S(2)}) copy-start(f32[1,4,128,128]{2,3,1,0:T(8,128)} %get-tuple-element.131) | copy-start | bytes 786436
  176.8 9.5 %collective-permute-start.4 = (f32[2,2,32,320]{3,2,1,0:T(8,128)}, f32[2,2,32,320]{3,2,1,0:T(8,128)}, u32[]{:S(2)}, u32[]{:S(2)}) collective-permute-start(f32[2,2,32,320]{3,2,1,0:T(8,128)} %get-tuple-element.93), channel_id=1, source_target_pairs={{16,0},{32,16},{48,32},{64,48},{80,64},{96,80},{112,96},{0,112},{1... | collective-permute-start | bytes 491528 | tf_op jit(solution)/shard_map/ppermute | solution.py:38
  182.9 1.0 copy-start.16
  183.9 10.0 %collective-permute-start.5 = (f32[2,2,32,320]{3,2,1,0:T(8,128)S(1)}, f32[2,2,32,320]{3,2,1,0:T(8,128)S(1)}, u32[]{:S(2)}, u32[]{:S(2)}) collective-permute-start(f32[2,2,32,320]{3,2,1,0:T(8,128)S(1)} %copy-done.16), channel_id=1, source_target_pairs={{112,0},{0,16},{16,32},{32,48},{48,64},{64,80},{80,96},{96,112},{1... | collective-permute-start | bytes 491528 | tf_op jit(solution)/shard_map/ppermute | solution.py:38
  195.4 143.7 %collective-permute-start.7 = (f32[2,2,256,32]{3,2,1,0:T(8,128)}, f32[2,2,256,32]{3,2,1,0:T(8,128)}, u32[]{:S(2)}, u32[]{:S(2)}) collective-permute-start(f32[2,2,256,32]{3,2,1,0:T(8,128)} %get-tuple-element.106), channel_id=1, source_target_pairs={{15,0},{0,1},{1,2},{2,3},{3,4},{4,5},{5,6},{6,7},{7,8},{8,9},{9,10... | collective-permute-start | bytes 393224 | tf_op jit(solution)/shard_map/ppermute | solution.py:38
  196.2 139.4 %collective-permute-start.6 = (f32[2,2,256,32]{3,2,1,0:T(8,128)}, f32[2,2,256,32]{3,2,1,0:T(8,128)}, u32[]{:S(2)}, u32[]{:S(2)}) collective-permute-start(f32[2,2,256,32]{3,2,1,0:T(8,128)} %get-tuple-element.107), channel_id=1, source_target_pairs={{1,0},{2,1},{3,2},{4,3},{5,4},{6,5},{7,6},{8,7},{9,8},{10,9},{11,1... | collective-permute-start | bytes 393224 | tf_op jit(solution)/shard_map/ppermute | solution.py:38
  342.5 1.0 copy-start.1
Sparse Core Ops, SparseCore 0:
  184.0 145.1 all-reduce.25
where the time goes:
time: 354 us; the launch traced here: 350 us
  waiting for transfers between devices  157 us (44%)
  matrix products  105 us (30%)
  local copies, waits for them, and re-layouts  33.4 us (9%)
  between operations  27.7 us (8%)
  starting transfers between devices  14.7 us (4%)
  other arithmetic  12.2 us (3%)
    psum x1, waiting for transfers between devices, on_device(): grad_total = lax.psum(grad_probe, ('row', 'col'))  133 us
    dot_general x144, matrix products, matprod(): return jnp.matmul(left_op, right_op, precision=HIGH)  105 us
    ppermute x2, waiting for transfers between devices, padded(): lax.ppermute(head, axis, [((i + 1) % count, i) for i in range(count)])  13.6 us
    ppermute x4, waiting for transfers between devices, shifted(): return lax.ppermute(block, axis, route)  8.92 us
  transfers between devices with their start and end apart: 9, of which 6 were waited for; matrix products, arithmetic and copies ran while one was open for 4% of the time, Pallas kernels for 0%

commit v1 on v0

v1 whole, which is shorter than its diff:
```python
import functools

import jax
import jax.numpy as jnp
import numpy as np
from jax import lax
from jax.experimental import pallas as pl
from jax.experimental.pallas import tpu as pltpu
from jax.sharding import PartitionSpec as P

HALO = 32
WIN = 128
MODES = 4
PLANES = 4
LANES = 128
PROP = 0.002
SHIFT_AMP = 0.5
STEP_SIZE = 0.5
EPSILON = 1e-06
BOTH = ("row", "col")


def matrices():
    k = np.arange(WIN)
    c = np.exp(-2j * np.pi * (np.outer(k, k) % WIN) / WIN) / np.sqrt(WIN)
    f = ((k + WIN // 2) % WIN - WIN // 2).astype(np.float64)
    g = c.conj() @ np.diag(np.exp(-1j * PROP * f * f)) @ c
    stack = []
    for m in (c, c.conj(), g, g.conj()):
        w = np.block([[m.real, m.imag], [-m.imag, m.real]]).astype(np.float32)
        high = w.astype(jnp.bfloat16)
        low = (w - high.astype(np.float32)).astype(jnp.bfloat16)
        stack.append(np.stack([high, low]))
    return np.stack(stack)


C, C_CONJ, G, G_CONJ = range(4)


def lane_iota(rows):
    return lax.broadcasted_iota(jnp.int32, (rows, LANES), 1)


def pack_kernel(tile_ref, north_ref, south_ref, east_ref, west_ref):
    def strip(src, lo, rows):
        lane = lane_iota(rows)
        east = jnp.zeros((rows, LANES), jnp.float32)
        west = jnp.zeros((rows, LANES), jnp.float32)
        for p in range(PLANES):
            here = (lane >= p * HALO) & (lane < (p + 1) * HALO)
            right = src[p, :, LANES : 2 * LANES]
            left = src[p, :, 0:LANES]
            shift = (p * HALO - 3 * HALO) % LANES
            right = pltpu.roll(right, shift, 1) if shift else right
            left = pltpu.roll(left, p * HALO, 1) if p else left
            east = jnp.where(here, right, east)
            west = jnp.where(here, left, west)
        east_ref[lo : lo + rows, :] = east
        west_ref[lo : lo + rows, :] = west

    strip(north_ref, 0, HALO)
    strip(tile_ref, HALO, tile_ref.shape[1])
    strip(south_ref, HALO + tile_ref.shape[1], HALO)


def split(value):
    high = value.astype(jnp.bfloat16)
    return high, (value - high.astype(jnp.float32)).astype(jnp.bfloat16)


def dot(left, right):
    return jnp.dot(left, right, preferred_element_type=jnp.float32)


def main_kernel(
    offsets_ref, tile_ref, north_ref, south_ref, from_west_ref, from_east_ref, probe_ref, amp_ref, mat_ref,
    probe_grad_ref, core_grad_ref, east_rim_ref, west_rim_ref,
    ext, grad, rh, rl, lh, ll, field, d_keep,
):
    rows = tile_ref.shape[1]
    ext_rows = rows + 2 * HALO
    lane_all = lane_iota(ext_rows)
    for p in range(PLANES):
        for q in range(2):
            cols = slice(q * LANES, (q + 1) * LANES)
            ext[p, q, 0:HALO, :] = north_ref[p, :, cols]
            ext[p, q, HALO : HALO + rows, :] = tile_ref[p, :, cols]
            ext[p, q, HALO + rows : ext_rows, :] = south_ref[p, :, cols]
        right = from_east_ref[...]
        left = from_west_ref[...]
        right = pltpu.roll(right, (-p * HALO) % LANES, 1) if p else right
        shift = (3 * HALO - p * HALO) % LANES
        left = pltpu.roll(left, shift, 1) if shift else left
        ext[p, 2, :, :] = jnp.where(lane_all < 2 * HALO, right, left)
        ext[p, 3, :, :] = ext[p, 0, :, :]
    grad[...] = jnp.zeros_like(grad)
    probe_grad_ref[...] = jnp.zeros_like(probe_grad_ref)

    lane = lane_iota(WIN)
    half = WIN

    def put_r(m, real, imag):
        h, l = split(real)
        rh[m * WIN : (m + 1) * WIN, 0:half] = h
        rl[m * WIN : (m + 1) * WIN, 0:half] = l
        h, l = split(imag)
        rh[m * WIN : (m + 1) * WIN, half:] = h
        rl[m * WIN : (m + 1) * WIN, half:] = l

    def put_l(m, real, imag):
        h, l = split(real)
        lh[0:half, m * WIN : (m + 1) * WIN] = h
        ll[0:half, m * WIN : (m + 1) * WIN] = l
        h, l = split(imag)
        lh[half:, m * WIN : (m + 1) * WIN] = h
        ll[half:, m * WIN : (m + 1) * WIN] = l

    def from_right(which):
        high, low = mat_ref[which, 0], mat_ref[which, 1]
        out = dot(rh[...], high) + dot(rl[...], high) + dot(rh[...], low)
        return [
            (out[m * WIN : (m + 1) * WIN, 0:half], out[m * WIN : (m + 1) * WIN, half:]) for m in range(MODES)
        ]

    def from_left(which):
        high, low = mat_ref[which ^ 1, 0], mat_ref[which ^ 1, 1]
        out = dot(high, lh[...]) + dot(high, ll[...]) + dot(low, lh[...])
        return [
            (out[0:half, m * WIN : (m + 1) * WIN], out[half:, m * WIN : (m + 1) * WIN]) for m in range(MODES)
        ]

    def scan_step(s, carry):
        row = offsets_ref[2 * s]
        start = lax.rem(offsets_ref[2 * s + 1] + (3 * LANES - HALO), 3 * LANES)
        q = lax.div(start, LANES)
        shift = lax.rem(start, LANES)
        back = lax.rem(LANES - shift, LANES)

        def window(p):
            a = pltpu.roll(ext[p, q, pl.ds(row, WIN), :], back, 1)
            b = pltpu.roll(ext[p, q + 1, pl.ds(row, WIN), :], back, 1)
            return jnp.where(lane < LANES - shift, a, b)

        def scatter(p, value):
            moved = pltpu.roll(value, shift, 1)
            grad[p, q, pl.ds(row, WIN), :] += jnp.where(lane >= shift, moved, 0.0)
            q2 = lax.rem(q + 1, 3)
            grad[p, q2, pl.ds(row, WIN), :] += jnp.where(lane < shift, moved, 0.0)

        first_r, second_r, first_i, second_i = (window(p) for p in range(PLANES))
        for m in range(MODES):
            pr, pi = probe_ref[0, m], probe_ref[1, m]
            put_r(m, pr * first_r - pi * first_i, pr * first_i + pi * first_r)
        for m, (real, imag) in enumerate(from_right(G)):
            put_l(m, real, imag)
        for m, (real, imag) in enumerate(from_left(G)):
            d_keep[0, m] = real
            d_keep[1, m] = imag
            put_l(m, real * second_r - imag * second_i, real * second_i + imag * second_r)
        for m, (real, imag) in enumerate(from_left(C)):
            put_r(m, real, imag)
        intensity = jnp.full((WIN, WIN), SHIFT_AMP, jnp.float32)
        for m, (real, imag) in enumerate(from_right(C)):
            field[0, m] = real
            field[1, m] = imag
            intensity = intensity + (real * real + imag * imag)
        factor = 2.0 - 2.0 * amp_ref[s] / jnp.sqrt(intensity)
        for m in range(MODES):
            put_r(m, field[0, m] * factor, field[1, m] * factor)
        for m, (real, imag) in enumerate(from_right(C_CONJ)):
            put_l(m, real, imag)
        sum_r = jnp.zeros((WIN, WIN), jnp.float32)
        sum_i = jnp.zeros((WIN, WIN), jnp.float32)
        for m, (real, imag) in enumerate(from_left(C_CONJ)):
            dr, di = d_keep[0, m], d_keep[1, m]
            sum_r = sum_r + (dr * real + di * imag)
            sum_i = sum_i + (dr * imag - di * real)
            put_l(m, second_r * real + second_i * imag, second_r * imag - second_i * real)
        scatter(1, sum_r)
        scatter(3, sum_i)
        for m, (real, imag) in enumerate(from_left(G_CONJ)):
            put_r(m, real, imag)
        sum_r = jnp.zeros((WIN, WIN), jnp.float32)
        sum_i = jnp.zeros((WIN, WIN), jnp.float32)
        for m, (real, imag) in enumerate(from_right(G_CONJ)):
            pr, pi = probe_ref[0, m], probe_ref[1, m]
            sum_r = sum_r + (pr * real + pi * imag)
            sum_i = sum_i + (pr * imag - pi * real)
            probe_grad_ref[0, m] += first_r * real + first_i * imag
            probe_grad_ref[1, m] += first_r * imag - first_i * real
        scatter(0, sum_r)
        scatter(2, sum_i)
        return carry

    lax.fori_loop(0, amp_ref.shape[0], scan_step, 0)

    east = jnp.zeros((ext_rows, LANES), jnp.float32)
    west = jnp.zeros((ext_rows, LANES), jnp.float32)
    for p in range(PLANES):
        core_grad_ref[p] = grad[p, 0:2]
        third = grad[p, 2]
        here = (lane_all >= p * HALO) & (lane_all < (p + 1) * HALO)
        shift = (p * HALO - 3 * HALO) % LANES
        east = jnp.where(here, pltpu.roll(third, p * HALO, 1) if p else third, east)
        west = jnp.where(here, pltpu.roll(third, shift, 1) if shift else third, west)
    east_rim_ref[...] = east
    west_rim_ref[...] = west


def middle_kernel(
    core_ref, from_west_ref, from_east_ref, parts_ref, north_ref, south_ref, center_ref, share_ref
):
    share = jnp.sum(parts_ref[...], axis=0)
    share_ref[...] = jnp.broadcast_to(share[None], share_ref.shape)
    ext_rows = core_ref.shape[2]
    rows = ext_rows - 2 * HALO
    lane = lane_iota(ext_rows)
    for p in range(PLANES):
        left = from_west_ref[...]
        right = from_east_ref[...]
        left = pltpu.roll(left, (-p * HALO) % LANES, 1) if p else left
        shift = (3 * HALO - p * HALO) % LANES
        right = pltpu.roll(right, shift, 1) if shift else right
        cols = (
            core_ref[p, 0] + jnp.where(lane < HALO, left, 0.0),
            core_ref[p, 1] + jnp.where(lane >= LANES - HALO, right, 0.0),
        )
        for q in range(2):
            at = slice(q * LANES, (q + 1) * LANES)
            north_ref[p, :, at] = cols[q][0:HALO]
            center_ref[p, :, at] = cols[q][HALO : HALO + rows]
            south_ref[p, :, at] = cols[q][HALO + rows :]


def final_kernel(center_ref, from_north_ref, from_south_ref, total_ref, probe_ref, object_ref, probe_new_ref):
    rows = center_ref.shape[1]
    object_ref[:, HALO : rows - HALO, :] = center_ref[:, HALO : rows - HALO, :]
    object_ref[:, 0:HALO, :] = center_ref[:, 0:HALO, :] + from_north_ref[...]
    object_ref[:, rows - HALO :, :] = center_ref[:, rows - HALO :, :] + from_south_ref[...]
    total = total_ref[...]
    squares = jnp.sum(total * total, axis=0, keepdims=True)
    mean = jnp.sum(squares, axis=1, keepdims=True) / (total.shape[0] * total.shape[1])
    probe_new_ref[...] = probe_ref[...] - total * (STEP_SIZE / jnp.sqrt(mean + EPSILON))


def vmem(count):
    return [pl.BlockSpec(memory_space=pltpu.VMEM)] * count


def f32(*shape):
    return jax.ShapeDtypeStruct(shape, jnp.float32)


def moved(block, axis, distance):
    count = lax.axis_size(axis)
    return lax.ppermute(block, axis, [(i, (i + distance) % count) for i in range(count)])


LIMIT = pltpu.CompilerParams(vmem_limit_bytes=40 * 2**20)


def on_device(object_tiles, probe_modes, offsets, amplitude):
    rows, cols = object_tiles.shape[2:]
    ext_rows = rows + 2 * HALO
    scans = offsets.shape[2]
    tile = object_tiles.reshape(PLANES, rows, cols)
    flat_offsets = offsets.reshape(2 * scans)
    amp = amplitude.reshape(scans, WIN, WIN)

    north = moved(tile[:, rows - HALO :], "row", 1)
    south = moved(tile[:, :HALO], "row", -1)
    east_send, west_send = pl.pallas_call(
        pack_kernel,
        out_shape=[f32(ext_rows, LANES)] * 2,
        in_specs=vmem(3),
        out_specs=vmem(2),
    )(tile, north, south)
    from_west = moved(east_send, "col", 1)
    from_east = moved(west_send, "col", -1)

    probe_grad, core_grad, east_rim, west_rim = pl.pallas_call(
        main_kernel,
        out_shape=[f32(2, MODES, WIN, WIN), f32(PLANES, 2, ext_rows, LANES), f32(ext_rows, LANES), f32(ext_rows, LANES)],
        in_specs=[pl.BlockSpec(memory_space=pltpu.SMEM)] + vmem(8),
        out_specs=vmem(4),
        scratch_shapes=[
            pltpu.VMEM((PLANES, 4, ext_rows, LANES), jnp.float32),
            pltpu.VMEM((PLANES, 3, ext_rows, LANES), jnp.float32),
            pltpu.VMEM((MODES * WIN, 2 * WIN), jnp.bfloat16),
            pltpu.VMEM((MODES * WIN, 2 * WIN), jnp.bfloat16),
            pltpu.VMEM((2 * WIN, MODES * WIN), jnp.bfloat16),
            pltpu.VMEM((2 * WIN, MODES * WIN), jnp.bfloat16),
            pltpu.VMEM((2, MODES, WIN, WIN), jnp.float32),
            pltpu.VMEM((2, MODES, WIN, WIN), jnp.float32),
        ],
        compiler_params=LIMIT,
    )(flat_offsets, tile, north, south, from_west, from_east, probe_modes, amp, jnp.asarray(matrices()))

    rim_from_west = moved(east_rim, "col", 1)
    rim_from_east = moved(west_rim, "col", -1)
    devices = lax.axis_size("row") * lax.axis_size("col")
    parts = probe_grad.reshape(devices, -1, LANES)
    parts = lax.all_to_all(parts, BOTH, 0, 0, tiled=True)
    north_rim, south_rim, center, share = pl.pallas_call(
        middle_kernel,
        out_shape=[f32(PLANES, HALO, cols), f32(PLANES, HALO, cols), f32(PLANES, rows, cols), f32(*parts.shape)],
        in_specs=vmem(4),
        out_specs=vmem(4),
    )(core_grad, rim_from_west, rim_from_east, parts)
    from_south = moved(north_rim, "row", -1)
    from_north = moved(south_rim, "row", 1)
    total = lax.all_to_all(share, BOTH, 0, 0, tiled=True)
    object_grad, probe_new = pl.pallas_call(
        final_kernel,
        out_shape=[f32(PLANES, rows, cols), f32(2 * MODES * WIN, WIN)],
        in_specs=vmem(5),
        out_specs=vmem(2),
    )(center, from_north, from_south, total.reshape(2 * MODES * WIN, WIN), probe_modes.reshape(2 * MODES * WIN, WIN))
    return object_grad.reshape(object_tiles.shape), probe_new.reshape(probe_modes.shape)


def solution(mesh):
    placed = (
        P(None, None, "row", "col"),
        P(),
        P("row", "col", None, None),
        P("row", "col", None, None, None),
    )
    return jax.shard_map(
        on_device,
        mesh=mesh,
        in_specs=placed,
        out_specs=(P(None, None, "row", "col"), P()),
        check_vma=False,
    )
```

time: 354 us -> 94.4 us (0.27)
  waiting for transfers between devices: 157 us -> 35.2 us
  matrix products: 105 us -> 0 us
  between operations: 27.7 us -> 0.72 us
  local copies, waits for them, and re-layouts: 33.4 us -> 7.72 us
  Pallas kernels: 0 us -> 21.9 us
  starting transfers between devices: 14.7 us -> 28.3 us
  other arithmetic: 12.2 us -> 0 us
    psum x1 -> x0, waiting for transfers between devices: 133 us -> none  [on_device(): grad_total = lax.psum(grad_probe, ('row', 'col'))]
    dot_general x144 -> x0, matrix products: 105 us -> none  [matprod(): return jnp.matmul(left_op, right_op, precision=HIGH)]
    pallas_call x0 -> x4, Pallas kernels: none -> 21.9 us  [the longest x1 13.6 us: on_device(): pl.pallas_call(main_kernel, out_shape=[f32(2, MODES, WIN, WIN), f32(PLANE...]
    all_to_all x0 -> x2, starting transfers between devices: none -> 13 us  [the longest x1 7.05 us: on_device(): parts = lax.all_to_all(parts, BOTH, 0, 0, tiled=True)]
    ppermute x8, waiting for transfers between devices: 24.3 us -> 32.1 us  [moved(): lax.ppermute(block, axis, [(i, (i + distance) % count) for i in range(cou...]
    add_any x2 -> x0, local copies, waits for them, and re-layouts: 6.19 us -> none  [local_loss(): lax.dynamic_slice(ext_tiles, (anchor, anchor, row_start, col_start), (2,...]
    scatter-add x2 -> x0, local copies, waits for them, and re-layouts: 4.66 us -> none  [the longest x1 2.4 us: on_device(): center = center.at[:, :, :, tile_size - HALO:].add(from_right)]
    slice x6 -> x1, local copies, waits for them, and re-layouts: 5.54 us -> 1.11 us  [on_device(): south = moved(tile[:, :HALO], 'row', -1)]
  transfers between devices with their start and end apart: 9 -> 10, of which waited for: 6 -> 9; matrix products, arithmetic and copies ran while one was open for 4% -> 0% of each run, Pallas kernels for 0% -> 0%
where the time goes in v1:
time: 94.4 us; the launch traced here: 93.8 us
  waiting for transfers between devices  35.2 us (37%)
  starting transfers between devices  28.3 us (30%)
  Pallas kernels  21.9 us (23%)
  local copies, waits for them, and re-layouts  7.72 us (8%)
    ppermute x8, waiting for transfers between devices, moved(): lax.ppermute(block, axis, [(i, (i + distance) % count) for i in range(cou...  32.1 us
    ppermute x8, starting transfers between devices, moved(): lax.ppermute(block, axis, [(i, (i + distance) % count) for i in range(cou...  15.3 us
    pallas_call x1, Pallas kernels, on_device(): pl.pallas_call(main_kernel, out_shape=[f32(2, MODES, WIN, WIN), f32(PLANE...  13.6 us
    all_to_all x1, starting transfers between devices, on_device(): parts = lax.all_to_all(parts, BOTH, 0, 0, tiled=True)  7.05 us
    unnamed x33, local copies, waits for them, and re-layouts  6.52 us
    all_to_all x1, starting transfers between devices, on_device(): total = lax.all_to_all(share, BOTH, 0, 0, tiled=True)  5.95 us
    pallas_call x1, Pallas kernels, on_device(): pl.pallas_call(middle_kernel, out_shape=[f32(PLANES, HALO, cols), f32(PLA...  3.13 us
    all_to_all x1, waiting for transfers between devices, on_device(): parts = lax.all_to_all(parts, BOTH, 0, 0, tiled=True)  3.09 us
  transfers between devices with their start and end apart: 10, of which 9 were waited for; matrix products, arithmetic and copies ran while one was open for 0% of the time, Pallas kernels for 0%

profile of v1, /device:TPU:1, one launch (start us, length us, event | category | flops | bytes accessed | tf_op | source)
XLA Modules:
  0.0 93.8 jit_solution(13570565901490245080)
XLA Ops:
  0.6 0.0 copy-start
  0.6 0.0 copy-start.15
  0.7 0.0 copy-start.1
  0.7 0.0 copy-start.8
  0.7 1.1 %fusion = (f32[4,32,256]{2,1,0:T(8,128)S(1)}, f32[4,32,256]{2,1,0:T(8,128)S(1)}) fusion(f32[4,256,256]{2,1,0:T(8,128)} %bitcast.7), kind=kLoop, calls=%fused_computation | loop fusion | bytes 524288 | tf_op jit(solution)/shard_map/slice | solution.py:271
  1.8 6.1 %collective-permute-start.1 = (f32[4,32,256]{2,1,0:T(8,128)S(1)}, f32[4,32,256]{2,1,0:T(8,128)S(1)}, u32[]{:S(2)}, u32[]{:S(2)}) collective-permute-start(f32[4,32,256]{2,1,0:T(8,128)S(1)} %get-tuple-element.26), channel_id=1, source_target_pairs={{0,112},{16,0},{32,16},{48,32},{64,48},{80,64},{96,80},{112,96},{1... | collective-permute-start | bytes 393224 | tf_op jit(solution)/shard_map/ppermute | solution.py:256
  7.9 0.0 collective-permute-start
  7.9 2.2 %collective-permute-done.1.south_ref = f32[4,32,256]{2,1,0:T(8,128)S(1)} collective-permute-done((f32[4,32,256]{2,1,0:T(8,128)S(1)}, f32[4,32,256]{2,1,0:T(8,128)S(1)}, u32[]{:S(2)}, u32[]{:S(2)}) %collective-permute-start.1) | collective-permute-done | bytes 131104 | tf_op jit(solution)/shard_map/ppermute | solution.py:256
  10.1 0.0 copy-start.4
  10.1 5.3 %collective-permute-done.north_ref = f32[4,32,256]{2,1,0:T(8,128)S(1)} collective-permute-done((f32[4,32,256]{2,1,0:T(8,128)S(1)}, f32[4,32,256]{2,1,0:T(8,128)S(1)}, u32[]{:S(2)}, u32[]{:S(2)}) %collective-permute-start) | collective-permute-done | bytes 131104 | tf_op jit(solution)/shard_map/ppermute | solution.py:256
  15.3 0.0 copy-done.4
  15.3 0.0 copy-start.6
  15.3 0.7 copy-done.6
  16.0 2.3 %shard_map.68 = (f32[320,128]{1,0:T(8,128)}, f32[320,128]{1,0:T(8,128)}) custom-call(f32[4,256,256]{2,1,0:T(8,128)} %bitcast.8, f32[4,32,256]{2,1,0:T(8,128)} %copy-done.6, f32[4,32,256]{2,1,0:T(8,128)} %copy-done.4), custom_call_target="tpu_custom_call" | custom-call | tf_op jit(solution)/shard_map/pallas_call | solution.py:272
  18.3 2.3 %collective-permute-start.2 = (f32[320,128]{1,0:T(8,128)}, f32[320,128]{1,0:T(8,128)S(1)}, u32[]{:S(2)}, u32[]{:S(2)}) collective-permute-start(f32[320,128]{1,0:T(8,128)} %get-tuple-element.14), channel_id=1, source_target_pairs={{0,1},{1,2},{2,3},{3,4},{4,5},{5,6},{6,7},{7,8},{8,9},{9,10},{10,1... | collective-permute-start | bytes 491528 | tf_op jit(solution)/shard_map/ppermute | solution.py:256
  20.6 0.0 collective-permute-start.3
  20.6 0.0 copy-done.15
  20.6 0.1 copy.8
  20.7 0.1 reshape.28.offsets_ref
  20.8 2.4 %collective-permute-done.2.from_west_ref = f32[320,128]{1,0:T(8,128)S(1)} collective-permute-done((f32[320,128]{1,0:T(8,128)}, f32[320,128]{1,0:T(8,128)S(1)}, u32[]{:S(2)}, u32[]{:S(2)}) %collective-permute-start.2) | collective-permute-done | bytes 163872 | tf_op jit(solution)/shard_map/ppermute | solution.py:256
  23.2 3.9 %collective-permute-done.3.from_east_ref = f32[320,128]{1,0:T(8,128)S(1)} collective-permute-done((f32[320,128]{1,0:T(8,128)}, f32[320,128]{1,0:T(8,128)S(1)}, u32[]{:S(2)}, u32[]{:S(2)}) %collective-permute-start.3) | collective-permute-done | bytes 163872 | tf_op jit(solution)/shard_map/ppermute | solution.py:256
  27.1 0.0 copy-done
  27.1 0.0 copy-done.1
  27.1 0.0 copy-done.8
  27.1 0.0 copy-start.3
  27.1 1.2 %copy-done.3 = bf16[4,2,256,256]{3,2,1,0:T(8,128)(2,1)S(1)} copy-done((bf16[4,2,256,256]{3,2,1,0:T(8,128)(2,1)S(1)}, bf16[4,2,256,256]{3,2,1,0:T(8,128)(2,1)}, u32[]{:S(2)}) %copy-start.3) | copy-done | bytes 1048600
  28.3 0.0 copy-start.5
  28.3 0.9 copy-done.5
  29.2 0.0 copy-start.7
  29.2 0.9 copy-done.7
  30.1 13.6 %shard_map.69 = (f32[2,4,128,128]{3,2,1,0:T(8,128)}, f32[4,2,320,128]{3,2,1,0:T(8,128)S(1)}, f32[320,128]{1,0:T(8,128)S(1)}, f32[320,128]{1,0:T(8,128)S(1)}) custom-call(s32[6]{0:T(128)S(1)} %reshape.28.offsets_ref, f32[4,256,256]{2,1,0:T(8,128)S(1)} %bitcast.9, f32[4,32,256]{2,1,0:T(8,128)S(1)} %copy-done.7, f32[4,32,256]{2,1,0:T(8,128)S(1)} %copy-done.5, ...), custom_call_target="tpu_custom_call" | custom-call | tf_op jit(solution)/shard_map/pallas_call | solution.py:281
  43.7 0.0 copy-start.2
  43.7 1.1 %copy-done.2 = f32[4,2,320,128]{3,2,1,0:T(8,128)} copy-done((f32[4,2,320,128]{3,2,1,0:T(8,128)}, f32[4,2,320,128]{3,2,1,0:T(8,128)S(1)}, u32[]{:S(2)}) %copy-start.2) | copy-done | bytes 1310744
  44.8 7.0 %all-to-all-start = ((f32[128,8,128]{2,1,0:T(8,128)}), f32[128,8,128]{2,1,0:T(8,128)S(1)}, u32[]{:S(2)}, u32[]{:S(2)}) async-start(f32[128,8,128]{2,1,0:T(8,128)} %bitcast.2), calls=%async_computation | async-start | bytes 1048576 | tf_op jit(solution)/shard_map/all_to_all | solution.py:303
  51.8 1.7 %collective-permute-start.4 = (f32[320,128]{1,0:T(8,128)S(1)}, f32[320,128]{1,0:T(8,128)S(1)}, u32[]{:S(2)}, u32[]{:S(2)}) collective-permute-start(f32[320,128]{1,0:T(8,128)S(1)} %get-tuple-element.17), channel_id=1, source_target_pairs={{0,1},{1,2},{2,3},{3,4},{4,5},{5,6},{6,7},{7,8},{8,9},{9,10},{10,1... | collective-permute-start | bytes 491528 | tf_op jit(solution)/shard_map/ppermute | solution.py:256
  53.5 0.0 collective-permute-start.5
  53.5 6.1 %collective-permute-done.4.from_west_ref = f32[320,128]{1,0:T(8,128)S(1)} collective-permute-done((f32[320,128]{1,0:T(8,128)S(1)}, f32[320,128]{1,0:T(8,128)S(1)}, u32[]{:S(2)}, u32[]{:S(2)}) %collective-permute-start.4) | collective-permute-done | bytes 163872 | tf_op jit(solution)/shard_map/ppermute | solution.py:256
  59.7 0.0 copy-start.11
  59.7 3.3 %collective-permute-done.5.from_east_ref = f32[320,128]{1,0:T(8,128)S(1)} collective-permute-done((f32[320,128]{1,0:T(8,128)S(1)}, f32[320,128]{1,0:T(8,128)S(1)}, u32[]{:S(2)}, u32[]{:S(2)}) %collective-permute-start.5) | collective-permute-done | bytes 163872 | tf_op jit(solution)/shard_map/ppermute | solution.py:256
  62.9 0.0 copy-start.12
  62.9 3.1 %all-to-all-done.parts_ref = f32[128,8,128]{2,1,0:T(8,128)S(1)} async-done(((f32[128,8,128]{2,1,0:T(8,128)}), f32[128,8,128]{2,1,0:T(8,128)S(1)}, u32[]{:S(2)}, u32[]{:S(2)}) %all-to-all-start) | async-done | bytes 524320 | tf_op jit(solution)/shard_map/all_to_all | solution.py:303
  66.0 0.0 copy-start.9
  66.0 0.0 copy-done.11
  66.0 0.0 copy-done.12
  66.0 0.8 copy-done.9
  66.8 3.1 %shard_map.70 = (f32[4,32,256]{2,1,0:T(8,128)}, f32[4,32,256]{2,1,0:T(8,128)}, f32[4,256,256]{2,1,0:T(8,128)}, f32[128,8,128]{2,1,0:T(8,128)}) custom-call(f32[4,2,320,128]{3,2,1,0:T(8,128)} %copy-done.2, f32[320,128]{1,0:T(8,128)} %copy-done.11, f32[320,128]{1,0:T(8,128)} %copy-done.12, f32[128,8,128]{2,1,0:T(8,128)} %copy-done.9), custom_call_target="tpu_custom_call" | custom-call | tf_op jit(solution)/shard_map/pallas_call | solution.py:304
  69.9 5.9 %all-to-all-start.1 = ((f32[128,8,128]{2,1,0:T(8,128)}), f32[128,8,128]{2,1,0:T(8,128)S(1)}, u32[]{:S(2)}, u32[]{:S(2)}) async-start(f32[128,8,128]{2,1,0:T(8,128)} %get-tuple-element.23), calls=%async_computation.1 | async-start | bytes 1048576 | tf_op jit(solution)/shard_map/all_to_all | solution.py:312
  75.9 3.0 %collective-permute-start.6 = (f32[4,32,256]{2,1,0:T(8,128)}, f32[4,32,256]{2,1,0:T(8,128)S(1)}, u32[]{:S(2)}, u32[]{:S(2)}) collective-permute-start(f32[4,32,256]{2,1,0:T(8,128)} %get-tuple-element.21), channel_id=1, source_target_pairs={{0,16},{16,32},{32,48},{48,64},{64,80},{80,96},{96,112},{112,0},{1... | collective-permute-start | bytes 393224 | tf_op jit(solution)/shard_map/ppermute | solution.py:256
  78.9 2.3 %collective-permute-start.7 = (f32[4,32,256]{2,1,0:T(8,128)}, f32[4,32,256]{2,1,0:T(8,128)S(1)}, u32[]{:S(2)}, u32[]{:S(2)}) collective-permute-start(f32[4,32,256]{2,1,0:T(8,128)} %get-tuple-element.22), channel_id=1, source_target_pairs={{0,112},{16,0},{32,16},{48,32},{64,48},{80,64},{96,80},{112,96},{1... | collective-permute-start | bytes 393224 | tf_op jit(solution)/shard_map/ppermute | solution.py:256
  81.1 8.4 %collective-permute-done.6.from_north_ref = f32[4,32,256]{2,1,0:T(8,128)S(1)} collective-permute-done((f32[4,32,256]{2,1,0:T(8,128)}, f32[4,32,256]{2,1,0:T(8,128)S(1)}, u32[]{:S(2)}, u32[]{:S(2)}) %collective-permute-start.6) | collective-permute-done | bytes 131104 | tf_op jit(solution)/shard_map/ppermute | solution.py:256
  89.5 0.0 copy-start.13
  89.5 0.6 collective-permute-done.7.from_south_ref
  90.1 0.0 copy-start.14
  90.1 0.0 all-to-all-done.1
  90.1 0.0 copy-start.10
  90.1 0.0 copy-done.13
  90.2 0.6 copy-done.14
  90.8 0.2 copy-done.10
  91.0 2.8 %shard_map.71 = (f32[4,256,256]{2,1,0:T(8,128)}, f32[1024,128]{1,0:T(8,128)}) custom-call(f32[4,256,256]{2,1,0:T(8,128)} %get-tuple-element.20.center_ref, f32[4,32,256]{2,1,0:T(8,128)} %copy-done.13, f32[4,32,256]{2,1,0:T(8,128)} %copy-done.14, f32[1024,128]{1,0:T(8,128)} %bitcast.12, f32[1024,128]{1,0:T(8,128)} %bitcast.10), custom_call_target="tpu_custom_call" | custom-call | tf_op jit(solution)/shard_map/pallas_call | solution.py:313
Async XLA Ops:
  0.6 26.4 %copy-start = (f32[2,2,256,256]{3,2,1,0:T(8,128)S(1)}, f32[2,2,256,256]{3,2,1,0:T(8,128)}, u32[]{:S(2)}) copy-start(f32[2,2,256,256]{3,2,1,0:T(8,128)} %param.5) | copy-start | bytes 3145732
  0.6 20.0 %copy-start.15 = (s32[1,1,3,2]{2,3,1,0:T(2,128)S(1)}, s32[1,1,3,2]{2,3,1,0:T(2,128)}, u32[]{:S(2)}) copy-start(s32[1,1,3,2]{2,3,1,0:T(2,128)} %param.7) | copy-start | bytes 76
  0.7 26.4 %copy-start.1 = (f32[2,4,128,128]{3,2,1,0:T(8,128)S(1)}, f32[2,4,128,128]{3,2,1,0:T(8,128)}, u32[]{:S(2)}) copy-start(f32[2,4,128,128]{3,2,1,0:T(8,128)} %probe_ref.1) | copy-start | bytes 1572868
  0.7 26.4 %copy-start.8 = (f32[1,1,3,128,128]{4,3,2,1,0:T(8,128)S(1)}, f32[1,1,3,128,128]{4,3,2,1,0:T(8,128)}, u32[]{:S(2)}) copy-start(f32[1,1,3,128,128]{4,3,2,1,0:T(8,128)} %param.8) | copy-start | bytes 589828
  1.8 8.3 %collective-permute-start.1 = (f32[4,32,256]{2,1,0:T(8,128)S(1)}, f32[4,32,256]{2,1,0:T(8,128)S(1)}, u32[]{:S(2)}, u32[]{:S(2)}) collective-permute-start(f32[4,32,256]{2,1,0:T(8,128)S(1)} %get-tuple-element.26), channel_id=1, source_target_pairs={{0,112},{16,0},{32,16},{48,32},{64,48},{80,64},{96,80},{112,96},{1... | collective-permute-start | bytes 393224 | tf_op jit(solution)/shard_map/ppermute | solution.py:256
  7.9 7.4 %collective-permute-start = (f32[4,32,256]{2,1,0:T(8,128)S(1)}, f32[4,32,256]{2,1,0:T(8,128)S(1)}, u32[]{:S(2)}, u32[]{:S(2)}) collective-permute-start(f32[4,32,256]{2,1,0:T(8,128)S(1)} %get-tuple-element.27), channel_id=1, source_target_pairs={{0,16},{16,32},{32,48},{48,64},{64,80},{80,96},{96,112},{112,0},{1... | collective-permute-start | bytes 393224 | tf_op jit(solution)/shard_map/ppermute | solution.py:256
  10.1 5.3 %copy-start.4 = (f32[4,32,256]{2,1,0:T(8,128)}, f32[4,32,256]{2,1,0:T(8,128)S(1)}, u32[]{:S(2)}) copy-start(f32[4,32,256]{2,1,0:T(8,128)S(1)} %collective-permute-done.1.south_ref) | copy-start | bytes 393220
  15.3 0.7 copy-start.6
  18.3 4.9 %collective-permute-start.2 = (f32[320,128]{1,0:T(8,128)}, f32[320,128]{1,0:T(8,128)S(1)}, u32[]{:S(2)}, u32[]{:S(2)}) collective-permute-start(f32[320,128]{1,0:T(8,128)} %get-tuple-element.14), channel_id=1, source_target_pairs={{0,1},{1,2},{2,3},{3,4},{4,5},{5,6},{6,7},{7,8},{8,9},{9,10},{10,1... | collective-permute-start | bytes 491528 | tf_op jit(solution)/shard_map/ppermute | solution.py:256
  20.6 6.5 %collective-permute-start.3 = (f32[320,128]{1,0:T(8,128)}, f32[320,128]{1,0:T(8,128)S(1)}, u32[]{:S(2)}, u32[]{:S(2)}) collective-permute-start(f32[320,128]{1,0:T(8,128)} %get-tuple-element.15), channel_id=1, source_target_pairs={{0,15},{1,0},{2,1},{3,2},{4,3},{5,4},{6,5},{7,6},{8,7},{9,8},{10,9... | collective-permute-start | bytes 491528 | tf_op jit(solution)/shard_map/ppermute | solution.py:256
  27.1 1.2 %copy-start.3 = (bf16[4,2,256,256]{3,2,1,0:T(8,128)(2,1)S(1)}, bf16[4,2,256,256]{3,2,1,0:T(8,128)(2,1)}, u32[]{:S(2)}) copy-start(bf16[4,2,256,256]{3,2,1,0:T(8,128)(2,1)} %constant.2.clone.mat_ref) | copy-start | bytes 3145732
  28.3 0.9 copy-start.5
  29.2 0.9 copy-start.7
  43.7 1.1 %copy-start.2 = (f32[4,2,320,128]{3,2,1,0:T(8,128)}, f32[4,2,320,128]{3,2,1,0:T(8,128)S(1)}, u32[]{:S(2)}) copy-start(f32[4,2,320,128]{3,2,1,0:T(8,128)S(1)} %get-tuple-element.16.core_ref) | copy-start | bytes 3932164
  44.8 21.2 %all-to-all-start = ((f32[128,8,128]{2,1,0:T(8,128)}), f32[128,8,128]{2,1,0:T(8,128)S(1)}, u32[]{:S(2)}, u32[]{:S(2)}) async-start(f32[128,8,128]{2,1,0:T(8,128)} %bitcast.2), calls=%async_computation | async-start | bytes 1048576 | tf_op jit(solution)/shard_map/all_to_all | solution.py:303
  51.8 7.8 %collective-permute-start.4 = (f32[320,128]{1,0:T(8,128)S(1)}, f32[320,128]{1,0:T(8,128)S(1)}, u32[]{:S(2)}, u32[]{:S(2)}) collective-permute-start(f32[320,128]{1,0:T(8,128)S(1)} %get-tuple-element.17), channel_id=1, source_target_pairs={{0,1},{1,2},{2,3},{3,4},{4,5},{5,6},{6,7},{7,8},{8,9},{9,10},{10,1... | collective-permute-start | bytes 491528 | tf_op jit(solution)/shard_map/ppermute | solution.py:256
  53.5 9.4 %collective-permute-start.5 = (f32[320,128]{1,0:T(8,128)S(1)}, f32[320,128]{1,0:T(8,128)S(1)}, u32[]{:S(2)}, u32[]{:S(2)}) collective-permute-start(f32[320,128]{1,0:T(8,128)S(1)} %get-tuple-element.18), channel_id=1, source_target_pairs={{0,15},{1,0},{2,1},{3,2},{4,3},{5,4},{6,5},{7,6},{8,7},{9,8},{10,9... | collective-permute-start | bytes 491528 | tf_op jit(solution)/shard_map/ppermute | solution.py:256
  59.7 6.4 %copy-start.11 = (f32[320,128]{1,0:T(8,128)}, f32[320,128]{1,0:T(8,128)S(1)}, u32[]{:S(2)}) copy-start(f32[320,128]{1,0:T(8,128)S(1)} %collective-permute-done.4.from_west_ref) | copy-start | bytes 491524
  62.9 3.1 %copy-start.12 = (f32[320,128]{1,0:T(8,128)}, f32[320,128]{1,0:T(8,128)S(1)}, u32[]{:S(2)}) copy-start(f32[320,128]{1,0:T(8,128)S(1)} %collective-permute-done.5.from_east_ref) | copy-start | bytes 491524
  66.0 0.8 copy-start.9
  69.9 20.2 %all-to-all-start.1 = ((f32[128,8,128]{2,1,0:T(8,128)}), f32[128,8,128]{2,1,0:T(8,128)S(1)}, u32[]{:S(2)}, u32[]{:S(2)}) async-start(f32[128,8,128]{2,1,0:T(8,128)} %get-tuple-element.23), calls=%async_computation.1 | async-start | bytes 1048576 | tf_op jit(solution)/shard_map/all_to_all | solution.py:312
  75.9 13.6 %collective-permute-start.6 = (f32[4,32,256]{2,1,0:T(8,128)}, f32[4,32,256]{2,1,0:T(8,128)S(1)}, u32[]{:S(2)}, u32[]{:S(2)}) collective-permute-start(f32[4,32,256]{2,1,0:T(8,128)} %get-tuple-element.21), channel_id=1, source_target_pairs={{0,16},{16,32},{32,48},{48,64},{64,80},{80,96},{96,112},{112,0},{1... | collective-permute-start | bytes 393224 | tf_op jit(solution)/shard_map/ppermute | solution.py:256
  78.9 11.3 %collective-permute-start.7 = (f32[4,32,256]{2,1,0:T(8,128)}, f32[4,32,256]{2,1,0:T(8,128)S(1)}, u32[]{:S(2)}, u32[]{:S(2)}) collective-permute-start(f32[4,32,256]{2,1,0:T(8,128)} %get-tuple-element.22), channel_id=1, source_target_pairs={{0,112},{16,0},{32,16},{48,32},{64,48},{80,64},{96,80},{112,96},{1... | collective-permute-start | bytes 393224 | tf_op jit(solution)/shard_map/ppermute | solution.py:256
  89.5 0.6 copy-start.13
  90.1 0.7 copy-start.14
  90.1 0.8 copy-start.10

commit v2 on v1

--- a/solution.py
+++ b/solution.py
@@ -1,5 +1,3 @@
-import functools
-
 import jax
 import jax.numpy as jnp
 import numpy as np
@@ -41,26 +39,28 @@
     return lax.broadcasted_iota(jnp.int32, (rows, LANES), 1)
 
 
-def pack_kernel(tile_ref, north_ref, south_ref, east_ref, west_ref):
-    def strip(src, lo, rows):
-        lane = lane_iota(rows)
-        east = jnp.zeros((rows, LANES), jnp.float32)
-        west = jnp.zeros((rows, LANES), jnp.float32)
-        for p in range(PLANES):
-            here = (lane >= p * HALO) & (lane < (p + 1) * HALO)
-            right = src[p, :, LANES : 2 * LANES]
-            left = src[p, :, 0:LANES]
-            shift = (p * HALO - 3 * HALO) % LANES
-            right = pltpu.roll(right, shift, 1) if shift else right
-            left = pltpu.roll(left, p * HALO, 1) if p else left
-            east = jnp.where(here, right, east)
-            west = jnp.where(here, left, west)
-        east_ref[lo : lo + rows, :] = east
-        west_ref[lo : lo + rows, :] = west
-
-    strip(north_ref, 0, HALO)
-    strip(tile_ref, HALO, tile_ref.shape[1])
-    strip(south_ref, HALO + tile_ref.shape[1], HALO)
+def edges(src, rows):
+    lane = lane_iota(rows)
+    east = jnp.zeros((rows, LANES), jnp.float32)
+    west = jnp.zeros((rows, LANES), jnp.float32)
+    for p in range(PLANES):
+        here = (lane >= p * HALO) & (lane < (p + 1) * HALO)
+        east = jnp.where(here, turned(src[p, :, LANES : 2 * LANES], (p - 3) * HALO), east)
+        west = jnp.where(here, turned(src[p, :, 0:LANES], p * HALO), west)
+    return east, west
+
+
+def turned(block, shift):
+    return pltpu.roll(block, shift % LANES, 1) if shift % LANES else block
+
+
+def pack_kernel(tile_ref, east_ref, west_ref):
+    east_ref[...], west_ref[...] = edges(tile_ref, tile_ref.shape[1])
+
+
+def corner_kernel(north_ref, south_ref, east_ref, west_ref):
+    east_ref[0:HALO, :], west_ref[0:HALO, :] = edges(north_ref, HALO)
+    east_ref[HALO:, :], west_ref[HALO:, :] = edges(south_ref, HALO)
 
 
 def split(value):
@@ -73,25 +73,29 @@
 
 
 def main_kernel(
-    offsets_ref, tile_ref, north_ref, south_ref, from_west_ref, from_east_ref, probe_ref, amp_ref, mat_ref,
-    probe_grad_ref, core_grad_ref, east_rim_ref, west_rim_ref,
+    offsets_ref, tile_ref, north_ref, south_ref, from_west_ref, from_east_ref, west_corners_ref, east_corners_ref,
+    probe_ref, amp_ref, mat_ref,
+    probe_grad_ref, center_ref, north_rim_ref, south_rim_ref, east_rim_ref, west_rim_ref,
     ext, grad, rh, rl, lh, ll, field, d_keep,
 ):
     rows = tile_ref.shape[1]
     ext_rows = rows + 2 * HALO
+    last = HALO + rows
     lane_all = lane_iota(ext_rows)
+
+    def beside(left, right, p):
+        low = lane_iota(left.shape[0]) < 2 * HALO
+        return jnp.where(low, turned(right, -p * HALO), turned(left, (3 - p) * HALO))
+
     for p in range(PLANES):
         for q in range(2):
             cols = slice(q * LANES, (q + 1) * LANES)
             ext[p, q, 0:HALO, :] = north_ref[p, :, cols]
-            ext[p, q, HALO : HALO + rows, :] = tile_ref[p, :, cols]
-            ext[p, q, HALO + rows : ext_rows, :] = south_ref[p, :, cols]
-        right = from_east_ref[...]
-        left = from_west_ref[...]
-        right = pltpu.roll(right, (-p * HALO) % LANES, 1) if p else right
-        shift = (3 * HALO - p * HALO) % LANES
-        left = pltpu.roll(left, shift, 1) if shift else left
-        ext[p, 2, :, :] = jnp.where(lane_all < 2 * HALO, right, left)
+            ext[p, q, HALO:last, :] = tile_ref[p, :, cols]
+            ext[p, q, last:ext_rows, :] = south_ref[p, :, cols]
+        ext[p, 2, 0:HALO, :] = beside(west_corners_ref[0:HALO, :], east_corners_ref[0:HALO, :], p)
+        ext[p, 2, HALO:last, :] = beside(from_west_ref[...], from_east_ref[...], p)
+        ext[p, 2, last:ext_rows, :] = beside(west_corners_ref[HALO:, :], east_corners_ref[HALO:, :], p)
         ext[p, 3, :, :] = ext[p, 0, :, :]
     grad[...] = jnp.zeros_like(grad)
     probe_grad_ref[...] = jnp.zeros_like(probe_grad_ref)
@@ -197,46 +201,49 @@
     east = jnp.zeros((ext_rows, LANES), jnp.float32)
     west = jnp.zeros((ext_rows, LANES), jnp.float32)
     for p in range(PLANES):
-        core_grad_ref[p] = grad[p, 0:2]
+        for q in range(2):
+            cols = slice(q * LANES, (q + 1) * LANES)
+            north_rim_ref[p, :, cols] = grad[p, q, 0:HALO, :]
+            center_ref[p, :, cols] = grad[p, q, HALO:last, :]
+            south_rim_ref[p, :, cols] = grad[p, q, last:ext_rows, :]
         third = grad[p, 2]
         here = (lane_all >= p * HALO) & (lane_all < (p + 1) * HALO)
-        shift = (p * HALO - 3 * HALO) % LANES
-        east = jnp.where(here, pltpu.roll(third, p * HALO, 1) if p else third, east)
-        west = jnp.where(here, pltpu.roll(third, shift, 1) if shift else third, west)
+        east = jnp.where(here, turned(third, p * HALO), east)
+        west = jnp.where(here, turned(third, (p - 3) * HALO), west)
     east_rim_ref[...] = east
     west_rim_ref[...] = west
 
 
-def middle_kernel(
-    core_ref, from_west_ref, from_east_ref, parts_ref, north_ref, south_ref, center_ref, share_ref
+def share_kernel(parts_ref, share_ref):
+    share_ref[...] = jnp.broadcast_to(jnp.sum(parts_ref[...], axis=0)[None], share_ref.shape)
+
+
+def object_kernel(
+    center_ref, from_north_ref, from_south_ref, from_west_ref, from_east_ref, north_corners_ref, south_corners_ref,
+    object_ref,
 ):
-    share = jnp.sum(parts_ref[...], axis=0)
-    share_ref[...] = jnp.broadcast_to(share[None], share_ref.shape)
-    ext_rows = core_ref.shape[2]
-    rows = ext_rows - 2 * HALO
-    lane = lane_iota(ext_rows)
+    rows = center_ref.shape[1]
+
+    def rim(left, right, p):
+        lane = lane_iota(left.shape[0])
+        return (
+            jnp.where(lane < HALO, turned(left, -p * HALO), 0.0),
+            jnp.where(lane >= LANES - HALO, turned(right, (3 - p) * HALO), 0.0),
+        )
+
     for p in range(PLANES):
-        left = from_west_ref[...]
-        right = from_east_ref[...]
-        left = pltpu.roll(left, (-p * HALO) % LANES, 1) if p else left
-        shift = (3 * HALO - p * HALO) % LANES
-        right = pltpu.roll(right, shift, 1) if shift else right
-        cols = (
-            core_ref[p, 0] + jnp.where(lane < HALO, left, 0.0),
-            core_ref[p, 1] + jnp.where(lane >= LANES - HALO, right, 0.0),
-        )
+        sides = rim(from_west_ref[HALO : HALO + rows, :], from_east_ref[HALO : HALO + rows, :], p)
+        north = rim(north_corners_ref[0:HALO, :], north_corners_ref[HALO:, :], p)
+        south = rim(south_corners_ref[0:HALO, :], south_corners_ref[HALO:, :], p)
         for q in range(2):
-            at = slice(q * LANES, (q + 1) * LANES)
-            north_ref[p, :, at] = cols[q][0:HALO]
-            center_ref[p, :, at] = cols[q][HALO : HALO + rows]
-            south_ref[p, :, at] = cols[q][HALO + rows :]
-
-
-def final_kernel(center_ref, from_north_ref, from_south_ref, total_ref, probe_ref, object_ref, probe_new_ref):
-    rows = center_ref.shape[1]
-    object_ref[:, HALO : rows - HALO, :] = center_ref[:, HALO : rows - HALO, :]
-    object_ref[:, 0:HALO, :] = center_ref[:, 0:HALO, :] + from_north_ref[...]
-    object_ref[:, rows - HALO :, :] = center_ref[:, rows - HALO :, :] + from_south_ref[...]
+            cols = slice(q * LANES, (q + 1) * LANES)
+            whole = center_ref[p, :, cols] + sides[q]
+            object_ref[p, 0:HALO, cols] = whole[0:HALO] + from_north_ref[p, :, cols] + north[q]
+            object_ref[p, HALO : rows - HALO, cols] = whole[HALO : rows - HALO]
+            object_ref[p, rows - HALO :, cols] = whole[rows - HALO :] + from_south_ref[p, :, cols] + south[q]
+
+
+def probe_kernel(total_ref, probe_ref, probe_new_ref):
     total = total_ref[...]
     squares = jnp.sum(total * total, axis=0, keepdims=True)
     mean = jnp.sum(squares, axis=1, keepdims=True) / (total.shape[0] * total.shape[1])
@@ -256,7 +263,15 @@
     return lax.ppermute(block, axis, [(i, (i + distance) % count) for i in range(count)])
 
 
-LIMIT = pltpu.CompilerParams(vmem_limit_bytes=40 * 2**20)
+def call(kernel, outs, ins, scratch=(), scalars=0, limit=2):
+    return pl.pallas_call(
+        kernel,
+        out_shape=outs,
+        in_specs=[pl.BlockSpec(memory_space=pltpu.SMEM)] * scalars + vmem(ins),
+        out_specs=vmem(len(outs)) if isinstance(outs, list) else vmem(1)[0],
+        scratch_shapes=scratch,
+        compiler_params=pltpu.CompilerParams(vmem_limit_bytes=limit * 2**20),
+    )
 
 
 def on_device(object_tiles, probe_modes, offsets, amplitude):
@@ -266,56 +281,53 @@
     tile = object_tiles.reshape(PLANES, rows, cols)
     flat_offsets = offsets.reshape(2 * scans)
     amp = amplitude.reshape(scans, WIN, WIN)
+    flat = (2 * MODES * WIN, WIN)
+    devices = lax.axis_size("row") * lax.axis_size("col")
 
     north = moved(tile[:, rows - HALO :], "row", 1)
     south = moved(tile[:, :HALO], "row", -1)
-    east_send, west_send = pl.pallas_call(
-        pack_kernel,
-        out_shape=[f32(ext_rows, LANES)] * 2,
-        in_specs=vmem(3),
-        out_specs=vmem(2),
-    )(tile, north, south)
+    east_send, west_send = call(pack_kernel, [f32(rows, LANES)] * 2, 1)(tile)
     from_west = moved(east_send, "col", 1)
     from_east = moved(west_send, "col", -1)
-
-    probe_grad, core_grad, east_rim, west_rim = pl.pallas_call(
+    east_send, west_send = call(corner_kernel, [f32(2 * HALO, LANES)] * 2, 2)(north, south)
+    west_corners = moved(east_send, "col", 1)
+    east_corners = moved(west_send, "col", -1)
+
+    pair = pltpu.VMEM((MODES * WIN, 2 * WIN), jnp.bfloat16)
+    wide = pltpu.VMEM((2 * WIN, MODES * WIN), jnp.bfloat16)
+    modes = pltpu.VMEM((2, MODES, WIN, WIN), jnp.float32)
+    probe_grad, center, north_rim, south_rim, east_rim, west_rim = call(
         main_kernel,
-        out_shape=[f32(2, MODES, WIN, WIN), f32(PLANES, 2, ext_rows, LANES), f32(ext_rows, LANES), f32(ext_rows, LANES)],
-        in_specs=[pl.BlockSpec(memory_space=pltpu.SMEM)] + vmem(8),
-        out_specs=vmem(4),
-        scratch_shapes=[
+        [f32(2, MODES, WIN, WIN), f32(PLANES, rows, cols)]
+        + [f32(PLANES, HALO, cols)] * 2
+        + [f32(ext_rows, LANES)] * 2,
+        10,
+        [
             pltpu.VMEM((PLANES, 4, ext_rows, LANES), jnp.float32),
             pltpu.VMEM((PLANES, 3, ext_rows, LANES), jnp.float32),
-            pltpu.VMEM((MODES * WIN, 2 * WIN), jnp.bfloat16),
-            pltpu.VMEM((MODES * WIN, 2 * WIN), jnp.bfloat16),
-            pltpu.VMEM((2 * WIN, MODES * WIN), jnp.bfloat16),
-            pltpu.VMEM((2 * WIN, MODES * WIN), jnp.bfloat16),
-            pltpu.VMEM((2, MODES, WIN, WIN), jnp.float32),
-            pltpu.VMEM((2, MODES, WIN, WIN), jnp.float32),
+            pair, pair, wide, wide, modes, modes,
         ],
-        compiler_params=LIMIT,
-    )(flat_offsets, tile, north, south, from_west, from_east, probe_modes, amp, jnp.asarray(matrices()))
-
+        scalars=1,
+        limit=16,
+    )(
+        flat_offsets, tile, north, south, from_west, from_east, west_corners, east_corners,
+        probe_modes, amp, jnp.asarray(matrices()),
+    )
+
+    parts = lax.all_to_all(probe_grad.reshape(devices, -1, LANES), BOTH, 0, 0, tiled=True)
     rim_from_west = moved(east_rim, "col", 1)
     rim_from_east = moved(west_rim, "col", -1)
-    devices = lax.axis_size("row") * lax.axis_size("col")
-    parts = probe_grad.reshape(devices, -1, LANES)
-    parts = lax.all_to_all(parts, BOTH, 0, 0, tiled=True)
-    north_rim, south_rim, center, share = pl.pallas_call(
-        middle_kernel,
-        out_shape=[f32(PLANES, HALO, cols), f32(PLANES, HALO, cols), f32(PLANES, rows, cols), f32(*parts.shape)],
-        in_specs=vmem(4),
-        out_specs=vmem(4),
-    )(core_grad, rim_from_west, rim_from_east, parts)
     from_south = moved(north_rim, "row", -1)
     from_north = moved(south_rim, "row", 1)
+    share = call(share_kernel, f32(*parts.shape), 1)(parts)
     total = lax.all_to_all(share, BOTH, 0, 0, tiled=True)
-    object_grad, probe_new = pl.pallas_call(
-        final_kernel,
-        out_shape=[f32(PLANES, rows, cols), f32(2 * MODES * WIN, WIN)],
-        in_specs=vmem(5),
-        out_specs=vmem(2),
-    )(center, from_north, from_south, total.reshape(2 * MODES * WIN, WIN), probe_modes.reshape(2 * MODES * WIN, WIN))
+    sides = (rim_from_west, rim_from_east)
+    south_corners = moved(jnp.concatenate([side[:HALO] for side in sides]), "row", -1)
+    north_corners = moved(jnp.concatenate([side[ext_rows - HALO :] for side in sides]), "row", 1)
+    object_grad = call(object_kernel, f32(PLANES, rows, cols), 7)(
+        center, from_north, from_south, rim_from_west, rim_from_east, north_corners, south_corners
+    )
+    probe_new = call(probe_kernel, f32(*flat), 2)(total.reshape(flat), probe_modes.reshape(flat))
     return object_grad.reshape(object_tiles.shape), probe_new.reshape(probe_modes.shape)
 
 

time: 94.4 us -> 81.5 us (0.86)
  waiting for transfers between devices: 35.2 us -> 22.7 us
  starting transfers between devices: 28.3 us -> 34.7 us
  Pallas kernels: 21.9 us -> 17.2 us
  local copies, waits for them, and re-layouts: 7.72 us -> 5.67 us
    ppermute x8 -> x12, waiting for transfers between devices: 32.1 us -> 14.1 us  [moved(): lax.ppermute(block, axis, [(i, (i + distance) % count) for i in range(cou...]
    ppermute x8 -> x12, starting transfers between devices: 15.3 us -> 21.9 us  [moved(): lax.ppermute(block, axis, [(i, (i + distance) % count) for i in range(cou...]
    pallas_call x4 -> x6, Pallas kernels: 21.9 us -> 17.2 us  [the longest x1 13.5 us: on_device(): call(main_kernel, [f32(2, MODES, WIN, WIN), f32(PLANES, rows, cols)] + [f...]
    all_to_all x1, waiting for transfers between devices: 3.09 us -> 7.31 us  [on_device(): lax.all_to_all(probe_grad.reshape(devices, -1, LANES), BOTH, 0, 0, tiled=...]
    unnamed x33 -> x25, local copies, waits for them, and re-layouts: 6.52 us -> 4.53 us
    all_to_all x1, starting transfers between devices: 5.95 us -> 4.29 us  [on_device(): total = lax.all_to_all(share, BOTH, 0, 0, tiled=True)]
    all_to_all x1, starting transfers between devices: 7.05 us -> 8.51 us  [on_device(): lax.all_to_all(probe_grad.reshape(devices, -1, LANES), BOTH, 0, 0, tiled=...]
    all_to_all x1, waiting for transfers between devices: 0.01 us -> 1.39 us  [on_device(): total = lax.all_to_all(share, BOTH, 0, 0, tiled=True)]
  transfers between devices with their start and end apart: 10 -> 14, of which waited for: 9 -> 6; matrix products, arithmetic and copies ran while one was open for 0% -> 0% of each run, Pallas kernels for 0% -> 3%
where the time goes in v2:
time: 81.5 us; the launch traced here: 81.2 us
  starting transfers between devices  34.7 us (43%)
  waiting for transfers between devices  22.7 us (28%)
  Pallas kernels  17.2 us (21%)
  local copies, waits for them, and re-layouts  5.67 us (7%)
    ppermute x12, starting transfers between devices, moved(): lax.ppermute(block, axis, [(i, (i + distance) % count) for i in range(cou...  21.9 us
    ppermute x12, waiting for transfers between devices, moved(): lax.ppermute(block, axis, [(i, (i + distance) % count) for i in range(cou...  14.1 us
    pallas_call x1, Pallas kernels, on_device(): call(main_kernel, [f32(2, MODES, WIN, WIN), f32(PLANES, rows, cols)] + [f...  13.5 us
    all_to_all x1, starting transfers between devices, on_device(): lax.all_to_all(probe_grad.reshape(devices, -1, LANES), BOTH, 0, 0, tiled=...  8.51 us
    all_to_all x1, waiting for transfers between devices, on_device(): lax.all_to_all(probe_grad.reshape(devices, -1, LANES), BOTH, 0, 0, tiled=...  7.31 us
    unnamed x25, local copies, waits for them, and re-layouts  4.53 us
    all_to_all x1, starting transfers between devices, on_device(): total = lax.all_to_all(share, BOTH, 0, 0, tiled=True)  4.29 us
  transfers between devices with their start and end apart: 14, of which 6 were waited for; matrix products, arithmetic and copies ran while one was open for 0% of the time, Pallas kernels for 3%

profile of v2, /device:TPU:1, one launch (start us, length us, event | category | flops | bytes accessed | tf_op | source)
XLA Modules:
  0.0 81.2 jit_solution(4258581855007572679)
XLA Ops:
  0.6 0.0 copy-start.2
  0.6 1.0 %fusion = (f32[4,32,256]{2,1,0:T(8,128)S(1)}, f32[4,32,256]{2,1,0:T(8,128)S(1)}) fusion(f32[4,256,256]{2,1,0:T(8,128)} %bitcast.7), kind=kLoop, calls=%fused_computation.2 | loop fusion | bytes 524288 | tf_op jit(solution)/shard_map/slice | solution.py:288
  1.7 6.1 %collective-permute-start.1 = (f32[4,32,256]{2,1,0:T(8,128)S(1)}, f32[4,32,256]{2,1,0:T(8,128)S(1)}, u32[]{:S(2)}, u32[]{:S(2)}) collective-permute-start(f32[4,32,256]{2,1,0:T(8,128)S(1)} %get-tuple-element.22), channel_id=1, source_target_pairs={{0,112},{16,0},{32,16},{48,32},{64,48},{80,64},{96,80},{112,96},{1... | collective-permute-start | bytes 393224 | tf_op jit(solution)/shard_map/ppermute | solution.py:263
  7.8 0.0 collective-permute-start
  7.8 0.0 copy-start
  7.8 1.2 %copy-done = f32[2,2,256,256]{3,2,1,0:T(8,128)S(1)} copy-done((f32[2,2,256,256]{3,2,1,0:T(8,128)S(1)}, f32[2,2,256,256]{3,2,1,0:T(8,128)}, u32[]{:S(2)}) %copy-start) | copy-done | bytes 1048600
  9.0 0.0 copy-start.1
  9.0 0.3 shard_map.68
  9.3 0.0 copy-start.4
  9.3 1.2 %collective-permute-start.2 = (f32[256,128]{1,0:T(8,128)S(1)}, f32[256,128]{1,0:T(8,128)S(1)}, u32[]{:S(2)}, u32[]{:S(2)}) collective-permute-start(f32[256,128]{1,0:T(8,128)S(1)} %get-tuple-element.12), channel_id=1, source_target_pairs={{0,1},{1,2},{2,3},{3,4},{4,5},{5,6},{6,7},{7,8},{8,9},{9,10},{10,1... | collective-permute-start | bytes 393224 | tf_op jit(solution)/shard_map/ppermute | solution.py:263
  10.5 0.0 collective-permute-start.3
  10.5 0.0 collective-permute-done.1.south_ref
  10.5 4.7 %collective-permute-done.north_ref = f32[4,32,256]{2,1,0:T(8,128)S(1)} collective-permute-done((f32[4,32,256]{2,1,0:T(8,128)S(1)}, f32[4,32,256]{2,1,0:T(8,128)S(1)}, u32[]{:S(2)}, u32[]{:S(2)}) %collective-permute-start) | collective-permute-done | bytes 131104 | tf_op jit(solution)/shard_map/ppermute | solution.py:263
  15.2 0.1 shard_map.69
  15.3 0.0 copy-start.11
  15.4 2.4 %collective-permute-start.4 = (f32[64,128]{1,0:T(8,128)S(1)}, f32[64,128]{1,0:T(8,128)S(1)}, u32[]{:S(2)}, u32[]{:S(2)}) collective-permute-start(f32[64,128]{1,0:T(8,128)S(1)} %get-tuple-element.14), channel_id=1, source_target_pairs={{0,1},{1,2},{2,3},{3,4},{4,5},{5,6},{6,7},{7,8},{8,9},{9,10},{10,1... | collective-permute-start | bytes 98312 | tf_op jit(solution)/shard_map/ppermute | solution.py:263
  17.7 0.0 collective-permute-start.5
  17.7 0.0 copy-done.11
  17.7 0.1 copy.8
  17.8 0.1 reshape.28.offsets_ref
  17.9 0.0 collective-permute-done.2.from_west_ref
  17.9 0.0 collective-permute-done.3.from_east_ref
  17.9 0.8 %collective-permute-done.4.west_corners_ref = f32[64,128]{1,0:T(8,128)S(1)} collective-permute-done((f32[64,128]{1,0:T(8,128)S(1)}, f32[64,128]{1,0:T(8,128)S(1)}, u32[]{:S(2)}, u32[]{:S(2)}) %collective-permute-start.4) | collective-permute-done | bytes 32800 | tf_op jit(solution)/shard_map/ppermute | solution.py:263
  18.8 2.3 %collective-permute-done.5.east_corners_ref = f32[64,128]{1,0:T(8,128)S(1)} collective-permute-done((f32[64,128]{1,0:T(8,128)S(1)}, f32[64,128]{1,0:T(8,128)S(1)}, u32[]{:S(2)}, u32[]{:S(2)}) %collective-permute-start.5) | collective-permute-done | bytes 32800 | tf_op jit(solution)/shard_map/ppermute | solution.py:263
  21.1 0.0 copy-done.2
  21.1 0.0 copy-done.1
  21.1 0.0 copy-done.4
  21.1 0.0 copy-start.3
  21.1 1.2 %copy-done.3 = bf16[4,2,256,256]{3,2,1,0:T(8,128)(2,1)S(1)} copy-done((bf16[4,2,256,256]{3,2,1,0:T(8,128)(2,1)S(1)}, bf16[4,2,256,256]{3,2,1,0:T(8,128)(2,1)}, u32[]{:S(2)}) %copy-start.3) | copy-done | bytes 1048600
  22.3 13.5 %shard_map.70 = (f32[2,4,128,128]{3,2,1,0:T(8,128)}, f32[4,256,256]{2,1,0:T(8,128)S(1)}, f32[4,32,256]{2,1,0:T(8,128)S(1)}, f32[4,32,256]{2,1,0:T(8,128)S(1)}, f...) custom-call(s32[6]{0:T(128)S(1)} %reshape.28.offsets_ref, f32[4,256,256]{2,1,0:T(8,128)S(1)} %bitcast.9, ...), custom_call_target="tpu_custom_call" | custom-call | tf_op jit(solution)/shard_map/pallas_call | solution.py:299
  35.8 0.0 copy-start.5
  35.8 0.7 copy-done.5
  36.4 0.0 copy-start.7
  36.4 0.7 copy-done.7
  37.1 0.0 copy-start.9
  37.1 0.6 copy-done.9
  37.7 0.0 copy-start.8
  37.8 0.0 copy-start.10
  37.8 0.0 copy-start.6
  37.8 8.5 %all-to-all-start = ((f32[128,8,128]{2,1,0:T(8,128)}), f32[128,8,128]{2,1,0:T(8,128)S(1)}, u32[]{:S(2)}, u32[]{:S(2)}) async-start(f32[128,8,128]{2,1,0:T(8,128)} %bitcast.3), calls=%async_computation | async-start | bytes 1048576 | tf_op jit(solution)/shard_map/all_to_all | solution.py:317
  46.3 0.0 copy-done.8
  46.3 1.7 %collective-permute-start.8 = (f32[320,128]{1,0:T(8,128)S(1)}, f32[320,128]{1,0:T(8,128)S(1)}, u32[]{:S(2)}, u32[]{:S(2)}) collective-permute-start(f32[320,128]{1,0:T(8,128)S(1)} %copy-done.8), channel_id=1, source_target_pairs={{0,1},{1,2},{2,3},{3,4},{4,5},{5,6},{6,7},{7,8},{8,9},{9,10},{10,1... | collective-permute-start | bytes 491528 | tf_op jit(solution)/shard_map/ppermute | solution.py:263
  48.0 0.0 copy-done.10
  48.0 2.4 %collective-permute-start.6 = (f32[4,32,256]{2,1,0:T(8,128)S(1)}, f32[4,32,256]{2,1,0:T(8,128)S(1)}, u32[]{:S(2)}, u32[]{:S(2)}) collective-permute-start(f32[4,32,256]{2,1,0:T(8,128)S(1)} %copy-done.10), channel_id=1, source_target_pairs={{0,16},{16,32},{32,48},{48,64},{64,80},{80,96},{96,112},{112,0},{1... | collective-permute-start | bytes 393224 | tf_op jit(solution)/shard_map/ppermute | solution.py:263
  50.4 2.7 %collective-permute-start.7 = (f32[4,32,256]{2,1,0:T(8,128)S(1)}, f32[4,32,256]{2,1,0:T(8,128)S(1)}, u32[]{:S(2)}, u32[]{:S(2)}) collective-permute-start(f32[4,32,256]{2,1,0:T(8,128)S(1)} %get-tuple-element.18), channel_id=1, source_target_pairs={{0,112},{16,0},{32,16},{48,32},{64,48},{80,64},{96,80},{112,96},{1... | collective-permute-start | bytes 393224 | tf_op jit(solution)/shard_map/ppermute | solution.py:263
  53.1 0.0 copy-done.6
  53.1 0.1 collective-permute-start.9
  53.2 7.3 %all-to-all-done.parts_ref = f32[128,8,128]{2,1,0:T(8,128)S(1)} async-done(((f32[128,8,128]{2,1,0:T(8,128)}), f32[128,8,128]{2,1,0:T(8,128)S(1)}, u32[]{:S(2)}, u32[]{:S(2)}) %all-to-all-start) | async-done | bytes 524320 | tf_op jit(solution)/shard_map/all_to_all | solution.py:317
  60.5 1.0 %shard_map.72 = f32[128,8,128]{2,1,0:T(8,128)} custom-call(f32[128,8,128]{2,1,0:T(8,128)S(1)} %all-to-all-done.parts_ref), custom_call_target="tpu_custom_call" | custom-call | tf_op jit(solution)/shard_map/pallas_call | solution.py:322
  61.4 4.3 %all-to-all-start.1 = ((f32[128,8,128]{2,1,0:T(8,128)}), f32[128,8,128]{2,1,0:T(8,128)S(1)}, u32[]{:S(2)}, u32[]{:S(2)}) async-start(f32[128,8,128]{2,1,0:T(8,128)} %shard_map.72), calls=%async_computation.1 | async-start | bytes 1048576 | tf_op jit(solution)/shard_map/all_to_all | solution.py:323
  65.7 0.0 collective-permute-done.8.from_west_ref
  65.8 0.0 collective-permute-done.9.from_east_ref
  65.8 3.0 %collective-permute-start.10 = (f32[64,128]{1,0:T(8,128)S(1)}, f32[64,128]{1,0:T(8,128)S(1)}, u32[]{:S(2)}, u32[]{:S(2)}) collective-permute-start(f32[64,128]{1,0:T(8,128)S(1)} %pad_maximum_fusion), channel_id=1, source_target_pairs={{0,16},{16,32},{32,48},{48,64},{64,80},{80,96},{96,112},{112,0},{1... | collective-permute-start | bytes 98312 | tf_op jit(solution)/shard_map/ppermute | solution.py:263
  68.8 2.4 %collective-permute-start.11 = (f32[64,128]{1,0:T(8,128)S(1)}, f32[64,128]{1,0:T(8,128)S(1)}, u32[]{:S(2)}, u32[]{:S(2)}) collective-permute-start(f32[64,128]{1,0:T(8,128)S(1)} %pad_maximum_fusion.1), channel_id=1, source_target_pairs={{0,112},{16,0},{32,16},{48,32},{64,48},{80,64},{96,80},{112,96},{1... | collective-permute-start | bytes 98312 | tf_op jit(solution)/shard_map/ppermute | solution.py:263
  71.2 0.0 collective-permute-done.6.from_north_ref
  71.2 0.0 collective-permute-done.7.from_south_ref
  71.2 6.2 %collective-permute-done.10.north_corners_ref = f32[64,128]{1,0:T(8,128)S(1)} collective-permute-done((f32[64,128]{1,0:T(8,128)S(1)}, f32[64,128]{1,0:T(8,128)S(1)}, u32[]{:S(2)}, u32[]{:S(2)}) %collective-permute-start.10) | collective-permute-done | bytes 32800 | tf_op jit(solution)/shard_map/ppermute | solution.py:263
  77.4 0.0 collective-permute-done.11.south_corners_ref
  77.4 1.3 %shard_map.71 = f32[4,256,256]{2,1,0:T(8,128)} custom-call(f32[4,256,256]{2,1,0:T(8,128)S(1)} %get-tuple-element.16.center_ref, f32[4,32,256]{2,1,0:T(8,128)S(1)} %collective-permute-done.6.from_north_ref, f32[4,32,256]{2,1,0:T(8,128)S(1)} %collective-permute-done.7.from_south_ref, f32[320,128]{1,0:T(8,128)S(1)} %collective-permute-done.8.from_west_ref, ...), custom_call_target="tpu_custom_call" | custom-call | tf_op jit(solution)/shard_map/pallas_call | solution.py:327
  78.7 1.4 %all-to-all-done.1 = f32[128,8,128]{2,1,0:T(8,128)S(1)} async-done(((f32[128,8,128]{2,1,0:T(8,128)}), f32[128,8,128]{2,1,0:T(8,128)S(1)}, u32[]{:S(2)}, u32[]{:S(2)}) %all-to-all-start.1) | async-done | bytes 524320 | tf_op jit(solution)/shard_map/all_to_all | solution.py:323
  80.1 1.1 %shard_map.73 = f32[1024,128]{1,0:T(8,128)} custom-call(f32[1024,128]{1,0:T(8,128)S(1)} %bitcast.10, f32[1024,128]{1,0:T(8,128)S(1)} %bitcast.11), custom_call_target="tpu_custom_call" | custom-call | tf_op jit(solution)/shard_map/pallas_call | solution.py:330
  (4 shorter events, 0.0 us)
Async XLA Ops:
  0.6 20.4 %copy-start.2 = (f32[2,4,128,128]{3,2,1,0:T(8,128)S(1)}, f32[2,4,128,128]{3,2,1,0:T(8,128)}, u32[]{:S(2)}) copy-start(f32[2,4,128,128]{3,2,1,0:T(8,128)} %probe_ref.1) | copy-start | bytes 1572868
  1.7 8.8 %collective-permute-start.1 = (f32[4,32,256]{2,1,0:T(8,128)S(1)}, f32[4,32,256]{2,1,0:T(8,128)S(1)}, u32[]{:S(2)}, u32[]{:S(2)}) collective-permute-start(f32[4,32,256]{2,1,0:T(8,128)S(1)} %get-tuple-element.22), channel_id=1, source_target_pairs={{0,112},{16,0},{32,16},{48,32},{64,48},{80,64},{96,80},{112,96},{1... | collective-permute-start | bytes 393224 | tf_op jit(solution)/shard_map/ppermute | solution.py:263
  7.8 7.4 %collective-permute-start = (f32[4,32,256]{2,1,0:T(8,128)S(1)}, f32[4,32,256]{2,1,0:T(8,128)S(1)}, u32[]{:S(2)}, u32[]{:S(2)}) collective-permute-start(f32[4,32,256]{2,1,0:T(8,128)S(1)} %get-tuple-element.23), channel_id=1, source_target_pairs={{0,16},{16,32},{32,48},{48,64},{64,80},{80,96},{96,112},{112,0},{1... | collective-permute-start | bytes 393224 | tf_op jit(solution)/shard_map/ppermute | solution.py:263
  7.8 1.2 %copy-start = (f32[2,2,256,256]{3,2,1,0:T(8,128)S(1)}, f32[2,2,256,256]{3,2,1,0:T(8,128)}, u32[]{:S(2)}) copy-start(f32[2,2,256,256]{3,2,1,0:T(8,128)} %param.5) | copy-start | bytes 3145732
  9.0 12.1 %copy-start.1 = (f32[2,2,256,256]{3,2,1,0:T(8,128)S(1)}, f32[2,2,256,256]{3,2,1,0:T(8,128)}, u32[]{:S(2)}) copy-start(f32[2,2,256,256]{3,2,1,0:T(8,128)} %param.5) | copy-start | bytes 3145732
  9.3 11.8 %copy-start.4 = (f32[1,1,3,128,128]{4,3,2,1,0:T(8,128)S(1)}, f32[1,1,3,128,128]{4,3,2,1,0:T(8,128)}, u32[]{:S(2)}) copy-start(f32[1,1,3,128,128]{4,3,2,1,0:T(8,128)} %param.8) | copy-start | bytes 589828
  9.3 8.6 %collective-permute-start.2 = (f32[256,128]{1,0:T(8,128)S(1)}, f32[256,128]{1,0:T(8,128)S(1)}, u32[]{:S(2)}, u32[]{:S(2)}) collective-permute-start(f32[256,128]{1,0:T(8,128)S(1)} %get-tuple-element.12), channel_id=1, source_target_pairs={{0,1},{1,2},{2,3},{3,4},{4,5},{5,6},{6,7},{7,8},{8,9},{9,10},{10,1... | collective-permute-start | bytes 393224 | tf_op jit(solution)/shard_map/ppermute | solution.py:263
  10.5 7.4 %collective-permute-start.3 = (f32[256,128]{1,0:T(8,128)S(1)}, f32[256,128]{1,0:T(8,128)S(1)}, u32[]{:S(2)}, u32[]{:S(2)}) collective-permute-start(f32[256,128]{1,0:T(8,128)S(1)} %get-tuple-element.13), channel_id=1, source_target_pairs={{0,15},{1,0},{2,1},{3,2},{4,3},{5,4},{6,5},{7,6},{8,7},{9,8},{10,9... | collective-permute-start | bytes 393224 | tf_op jit(solution)/shard_map/ppermute | solution.py:263
  15.3 2.4 %copy-start.11 = (s32[1,1,3,2]{2,3,1,0:T(2,128)S(1)}, s32[1,1,3,2]{2,3,1,0:T(2,128)}, u32[]{:S(2)}) copy-start(s32[1,1,3,2]{2,3,1,0:T(2,128)} %param.7) | copy-start | bytes 76
  15.4 3.4 %collective-permute-start.4 = (f32[64,128]{1,0:T(8,128)S(1)}, f32[64,128]{1,0:T(8,128)S(1)}, u32[]{:S(2)}, u32[]{:S(2)}) collective-permute-start(f32[64,128]{1,0:T(8,128)S(1)} %get-tuple-element.14), channel_id=1, source_target_pairs={{0,1},{1,2},{2,3},{3,4},{4,5},{5,6},{6,7},{7,8},{8,9},{9,10},{10,1... | collective-permute-start | bytes 98312 | tf_op jit(solution)/shard_map/ppermute | solution.py:263
  17.7 3.3 %collective-permute-start.5 = (f32[64,128]{1,0:T(8,128)S(1)}, f32[64,128]{1,0:T(8,128)S(1)}, u32[]{:S(2)}, u32[]{:S(2)}) collective-permute-start(f32[64,128]{1,0:T(8,128)S(1)} %get-tuple-element.15), channel_id=1, source_target_pairs={{0,15},{1,0},{2,1},{3,2},{4,3},{5,4},{6,5},{7,6},{8,7},{9,8},{10,9... | collective-permute-start | bytes 98312 | tf_op jit(solution)/shard_map/ppermute | solution.py:263
  21.1 1.2 %copy-start.3 = (bf16[4,2,256,256]{3,2,1,0:T(8,128)(2,1)S(1)}, bf16[4,2,256,256]{3,2,1,0:T(8,128)(2,1)}, u32[]{:S(2)}) copy-start(bf16[4,2,256,256]{3,2,1,0:T(8,128)(2,1)} %constant.2.clone.mat_ref) | copy-start | bytes 3145732
  35.8 0.7 copy-start.5
  36.4 0.7 copy-start.7
  37.1 0.6 copy-start.9
  37.7 8.5 %copy-start.8 = (f32[320,128]{1,0:T(8,128)S(1)}, f32[320,128]{1,0:T(8,128)}, u32[]{:S(2)}) copy-start(f32[320,128]{1,0:T(8,128)} %copy-done.7) | copy-start | bytes 491524
  37.8 10.2 %copy-start.10 = (f32[4,32,256]{2,1,0:T(8,128)S(1)}, f32[4,32,256]{2,1,0:T(8,128)}, u32[]{:S(2)}) copy-start(f32[4,32,256]{2,1,0:T(8,128)} %copy-done.9) | copy-start | bytes 393220
  37.8 15.3 %copy-start.6 = (f32[320,128]{1,0:T(8,128)S(1)}, f32[320,128]{1,0:T(8,128)}, u32[]{:S(2)}) copy-start(f32[320,128]{1,0:T(8,128)} %copy-done.5) | copy-start | bytes 491524
  37.8 22.7 %all-to-all-start = ((f32[128,8,128]{2,1,0:T(8,128)}), f32[128,8,128]{2,1,0:T(8,128)S(1)}, u32[]{:S(2)}, u32[]{:S(2)}) async-start(f32[128,8,128]{2,1,0:T(8,128)} %bitcast.3), calls=%async_computation | async-start | bytes 1048576 | tf_op jit(solution)/shard_map/all_to_all | solution.py:317
  46.3 19.4 %collective-permute-start.8 = (f32[320,128]{1,0:T(8,128)S(1)}, f32[320,128]{1,0:T(8,128)S(1)}, u32[]{:S(2)}, u32[]{:S(2)}) collective-permute-start(f32[320,128]{1,0:T(8,128)S(1)} %copy-done.8), channel_id=1, source_target_pairs={{0,1},{1,2},{2,3},{3,4},{4,5},{5,6},{6,7},{7,8},{8,9},{9,10},{10,1... | collective-permute-start | bytes 491528 | tf_op jit(solution)/shard_map/ppermute | solution.py:263
  48.0 23.2 %collective-permute-start.6 = (f32[4,32,256]{2,1,0:T(8,128)S(1)}, f32[4,32,256]{2,1,0:T(8,128)S(1)}, u32[]{:S(2)}, u32[]{:S(2)}) collective-permute-start(f32[4,32,256]{2,1,0:T(8,128)S(1)} %copy-done.10), channel_id=1, source_target_pairs={{0,16},{16,32},{32,48},{48,64},{64,80},{80,96},{96,112},{112,0},{1... | collective-permute-start | bytes 393224 | tf_op jit(solution)/shard_map/ppermute | solution.py:263
  50.4 20.8 %collective-permute-start.7 = (f32[4,32,256]{2,1,0:T(8,128)S(1)}, f32[4,32,256]{2,1,0:T(8,128)S(1)}, u32[]{:S(2)}, u32[]{:S(2)}) collective-permute-start(f32[4,32,256]{2,1,0:T(8,128)S(1)} %get-tuple-element.18), channel_id=1, source_target_pairs={{0,112},{16,0},{32,16},{48,32},{64,48},{80,64},{96,80},{112,96},{1... | collective-permute-start | bytes 393224 | tf_op jit(solution)/shard_map/ppermute | solution.py:263
  53.1 12.7 %collective-permute-start.9 = (f32[320,128]{1,0:T(8,128)S(1)}, f32[320,128]{1,0:T(8,128)S(1)}, u32[]{:S(2)}, u32[]{:S(2)}) collective-permute-start(f32[320,128]{1,0:T(8,128)S(1)} %copy-done.6), channel_id=1, source_target_pairs={{0,15},{1,0},{2,1},{3,2},{4,3},{5,4},{6,5},{7,6},{8,7},{9,8},{10,9... | collective-permute-start | bytes 491528 | tf_op jit(solution)/shard_map/ppermute | solution.py:263
  61.4 18.6 %all-to-all-start.1 = ((f32[128,8,128]{2,1,0:T(8,128)}), f32[128,8,128]{2,1,0:T(8,128)S(1)}, u32[]{:S(2)}, u32[]{:S(2)}) async-start(f32[128,8,128]{2,1,0:T(8,128)} %shard_map.72), calls=%async_computation.1 | async-start | bytes 1048576 | tf_op jit(solution)/shard_map/all_to_all | solution.py:323
  65.8 11.6 %collective-permute-start.10 = (f32[64,128]{1,0:T(8,128)S(1)}, f32[64,128]{1,0:T(8,128)S(1)}, u32[]{:S(2)}, u32[]{:S(2)}) collective-permute-start(f32[64,128]{1,0:T(8,128)S(1)} %pad_maximum_fusion), channel_id=1, source_target_pairs={{0,16},{16,32},{32,48},{48,64},{64,80},{80,96},{96,112},{112,0},{1... | collective-permute-start | bytes 98312 | tf_op jit(solution)/shard_map/ppermute | solution.py:263
  68.8 8.6 %collective-permute-start.11 = (f32[64,128]{1,0:T(8,128)S(1)}, f32[64,128]{1,0:T(8,128)S(1)}, u32[]{:S(2)}, u32[]{:S(2)}) collective-permute-start(f32[64,128]{1,0:T(8,128)S(1)} %pad_maximum_fusion.1), channel_id=1, source_target_pairs={{0,112},{16,0},{32,16},{48,32},{64,48},{80,64},{96,80},{112,96},{1... | collective-permute-start | bytes 98312 | tf_op jit(solution)/shard_map/ppermute | solution.py:263

commit v3 on v2

v3 whole, which is shorter than its diff:
```python
import jax
import jax.numpy as jnp
import numpy as np
from jax import lax
from jax.experimental import pallas as pl
from jax.experimental.pallas import tpu as pltpu
from jax.sharding import PartitionSpec as P

HALO = 32
WIN = 128
MODES = 4
PLANES = 4
LANES = 128
PROP = 0.002
SHIFT_AMP = 0.5
STEP_SIZE = 0.5
EPSILON = 1e-06
BOTH = ("row", "col")


def matrices():
    k = np.arange(WIN)
    c = np.exp(-2j * np.pi * (np.outer(k, k) % WIN) / WIN) / np.sqrt(WIN)
    f = ((k + WIN // 2) % WIN - WIN // 2).astype(np.float64)
    g = c.conj() @ np.diag(np.exp(-1j * PROP * f * f)) @ c
    stack = []
    for m in (c, c.conj(), g, g.conj()):
        w = np.block([[m.real, m.imag], [-m.imag, m.real]]).astype(np.float32)
        high = w.astype(jnp.bfloat16)
        low = (w - high.astype(np.float32)).astype(jnp.bfloat16)
        stack.append(np.stack([high, low]))
    return np.stack(stack)


C, C_CONJ, G, G_CONJ = range(4)


def lane_iota(rows):
    return lax.broadcasted_iota(jnp.int32, (rows, LANES), 1)


def edges(src, rows):
    lane = lane_iota(rows)
    east = jnp.zeros((rows, LANES), jnp.float32)
    west = jnp.zeros((rows, LANES), jnp.float32)
    for p in range(PLANES):
        here = (lane >= p * HALO) & (lane < (p + 1) * HALO)
        east = jnp.where(here, turned(src[p, :, LANES : 2 * LANES], (p - 3) * HALO), east)
        west = jnp.where(here, turned(src[p, :, 0:LANES], p * HALO), west)
    return east, west


def turned(block, shift):
    return pltpu.roll(block, shift % LANES, 1) if shift % LANES else block


def pack_kernel(tile_ref, east_ref, west_ref):
    east_ref[...], west_ref[...] = edges(tile_ref, tile_ref.shape[1])


def corner_kernel(north_ref, south_ref, east_ref, west_ref):
    east_ref[0:HALO, :], west_ref[0:HALO, :] = edges(north_ref, HALO)
    east_ref[HALO:, :], west_ref[HALO:, :] = edges(south_ref, HALO)


def split(value):
    high = value.astype(jnp.bfloat16)
    return high, (value - high.astype(jnp.float32)).astype(jnp.bfloat16)


def dot(left, right):
    return jnp.dot(left, right, preferred_element_type=jnp.float32)


def assemble_kernel(tile_ref, north_ref, south_ref, ext):
    rows = tile_ref.shape[1]
    for p in range(PLANES):
        for q in range(2):
            cols = slice(q * LANES, (q + 1) * LANES)
            ext[p, q, 0:HALO, :] = north_ref[p, :, cols]
            ext[p, q, HALO : HALO + rows, :] = tile_ref[p, :, cols]
            ext[p, q, HALO + rows :, :] = south_ref[p, :, cols]


def place(offsets_ref, s, q_count=3):
    start = lax.rem(offsets_ref[2 * s + 1] + (q_count * LANES - HALO), q_count * LANES)
    first = lax.div(start, LANES)
    return offsets_ref[2 * s], first, lax.rem(first + 1, q_count), lax.rem(start, LANES)


def main_kernel(
    offsets_ref, ext_in, from_west_ref, from_east_ref, west_corners_ref, east_corners_ref, amp_ref, probe_ref, mat_ref,
    probe_grad_ref, window_grad_ref, ext,
    rh, rl, lh, ll, field, d_keep, win,
):
    del ext_in
    ext_rows = ext.shape[2]
    last = ext_rows - HALO

    def beside(left, right, p):
        low = lane_iota(left.shape[0]) < 2 * HALO
        return jnp.where(low, turned(right, -p * HALO), turned(left, (3 - p) * HALO))

    for p in range(PLANES):
        ext[p, 2, 0:HALO, :] = beside(west_corners_ref[0:HALO, :], east_corners_ref[0:HALO, :], p)
        ext[p, 2, HALO:last, :] = beside(from_west_ref[...], from_east_ref[...], p)
        ext[p, 2, last:ext_rows, :] = beside(west_corners_ref[HALO:, :], east_corners_ref[HALO:, :], p)
    probe_grad_ref[...] = jnp.zeros_like(probe_grad_ref)

    lane = lane_iota(WIN)
    chains = range(MODES // 2)

    def put(high, low, at, value):
        high[at], low[at] = split(value)

    def put_r(c, k, real, imag):
        rows = slice(k * WIN, (k + 1) * WIN)
        put(rh, rl, (c, rows, slice(0, WIN)), real)
        put(rh, rl, (c, rows, slice(WIN, 2 * WIN)), imag)

    def put_l(c, k, real, imag):
        cols = slice(k * WIN, (k + 1) * WIN)
        put(lh, ll, (c, slice(0, WIN), cols), real)
        put(lh, ll, (c, slice(WIN, 2 * WIN), cols), imag)

    def from_right(which):
        for c in chains:
            high, low = mat_ref[which, 0], mat_ref[which, 1]
            out = dot(jnp.concatenate([rh[c], rl[c], rh[c]], axis=1), jnp.concatenate([high, high, low], axis=0))
            for k in range(2):
                rows = slice(k * WIN, (k + 1) * WIN)
                yield c, k, out[rows, 0:WIN], out[rows, WIN:]

    def from_left(which):
        for c in chains:
            high, low = mat_ref[which ^ 1, 0], mat_ref[which ^ 1, 1]
            out = dot(jnp.concatenate([high, high, low], axis=1), jnp.concatenate([lh[c], ll[c], lh[c]], axis=0))
            for k in range(2):
                cols = slice(k * WIN, (k + 1) * WIN)
                yield c, k, out[0:WIN, cols], out[WIN:, cols]

    def scan_step(s, carry):
        row, q, q_next, shift = place(offsets_ref, s)
        back = lax.rem(LANES - shift, LANES)

        def window(p):
            a = pltpu.roll(ext[p, q, pl.ds(row, WIN), :], back, 1)
            b = pltpu.roll(ext[p, q_next, pl.ds(row, WIN), :], back, 1)
            return jnp.where(lane < LANES - shift, a, b)

        for p in range(PLANES):
            win[p] = window(p)
        for c in chains:
            for k in range(2):
                pr, pi = probe_ref[0, 2 * c + k], probe_ref[1, 2 * c + k]
                put_r(c, k, pr * win[0] - pi * win[2], pr * win[2] + pi * win[0])
        for c, k, real, imag in from_right(G):
            put_l(c, k, real, imag)
        for c, k, real, imag in from_left(G):
            m = 2 * c + k
            d_keep[0, m] = real
            d_keep[1, m] = imag
            put_l(c, k, real * win[1] - imag * win[3], real * win[3] + imag * win[1])
        for c, k, real, imag in from_left(C):
            put_r(c, k, real, imag)
        intensity = jnp.full((WIN, WIN), SHIFT_AMP, jnp.float32)
        for c, k, real, imag in from_right(C):
            m = 2 * c + k
            field[0, m] = real
            field[1, m] = imag
            intensity = intensity + (real * real + imag * imag)
        factor = 2.0 - 2.0 * amp_ref[s] / jnp.sqrt(intensity)
        for c in chains:
            for k in range(2):
                m = 2 * c + k
                put_r(c, k, field[0, m] * factor, field[1, m] * factor)
        for c, k, real, imag in from_right(C_CONJ):
            put_l(c, k, real, imag)
        sum_r = jnp.zeros((WIN, WIN), jnp.float32)
        sum_i = jnp.zeros((WIN, WIN), jnp.float32)
        for c, k, real, imag in from_left(C_CONJ):
            dr, di = d_keep[0, 2 * c + k], d_keep[1, 2 * c + k]
            sum_r = sum_r + (dr * real + di * imag)
            sum_i = sum_i + (dr * imag - di * real)
            put_l(c, k, win[1] * real + win[3] * imag, win[1] * imag - win[3] * real)
        window_grad_ref[s, 1] = sum_r
        window_grad_ref[s, 3] = sum_i
        for c, k, real, imag in from_left(G_CONJ):
            put_r(c, k, real, imag)
        sum_r = jnp.zeros((WIN, WIN), jnp.float32)
        sum_i = jnp.zeros((WIN, WIN), jnp.float32)
        for c, k, real, imag in from_right(G_CONJ):
            m = 2 * c + k
            pr, pi = probe_ref[0, m], probe_ref[1, m]
            sum_r = sum_r + (pr * real + pi * imag)
            sum_i = sum_i + (pr * imag - pi * real)
            probe_grad_ref[0, m] += win[0] * real + win[2] * imag
            probe_grad_ref[1, m] += win[0] * imag - win[2] * real
        window_grad_ref[s, 0] = sum_r
        window_grad_ref[s, 2] = sum_i
        return carry

    lax.fori_loop(0, amp_ref.shape[0], scan_step, 0)


def scatter_kernel(offsets_ref, window_grad_ref, center_ref, north_rim_ref, south_rim_ref, east_rim_ref, west_rim_ref, grad):
    grad[...] = jnp.zeros_like(grad)
    lane = lane_iota(WIN)
    for s in range(window_grad_ref.shape[0]):
        row, q, q_next, shift = place(offsets_ref, s)
        for p in range(PLANES):
            value = pltpu.roll(window_grad_ref[s, p], shift, 1)
            grad[p, q, pl.ds(row, WIN), :] += jnp.where(lane >= shift, value, 0.0)
            grad[p, q_next, pl.ds(row, WIN), :] += jnp.where(lane < shift, value, 0.0)
    ext_rows = grad.shape[2]
    last = ext_rows - HALO
    lane = lane_iota(ext_rows)
    east = jnp.zeros((ext_rows, LANES), jnp.float32)
    west = jnp.zeros((ext_rows, LANES), jnp.float32)
    for p in range(PLANES):
        for q in range(2):
            cols = slice(q * LANES, (q + 1) * LANES)
            north_rim_ref[p, :, cols] = grad[p, q, 0:HALO, :]
            center_ref[p, :, cols] = grad[p, q, HALO:last, :]
            south_rim_ref[p, :, cols] = grad[p, q, last:ext_rows, :]
        third = grad[p, 2]
        here = (lane >= p * HALO) & (lane < (p + 1) * HALO)
        east = jnp.where(here, turned(third, p * HALO), east)
        west = jnp.where(here, turned(third, (p - 3) * HALO), west)
    east_rim_ref[...] = east
    west_rim_ref[...] = west


def rim_corner_kernel(from_west_ref, from_east_ref, to_north_ref, to_south_ref):
    for k, ref in enumerate((from_west_ref, from_east_ref)):
        to_north_ref[k * HALO : (k + 1) * HALO, :] = ref[0:HALO, :]
        to_south_ref[k * HALO : (k + 1) * HALO, :] = ref[ref.shape[0] - HALO :, :]


def share_kernel(parts_ref, from_west_ref, from_east_ref, share_ref):
    del from_west_ref, from_east_ref
    share_ref[...] = jnp.broadcast_to(jnp.sum(parts_ref[...], axis=0)[None], share_ref.shape)


def object_kernel(
    center_ref, from_north_ref, from_south_ref, from_west_ref, from_east_ref, north_corners_ref, south_corners_ref,
    object_ref,
):
    rows = center_ref.shape[1]

    def rim(left, right, p):
        lane = lane_iota(left.shape[0])
        return (
            jnp.where(lane < HALO, turned(left, -p * HALO), 0.0),
            jnp.where(lane >= LANES - HALO, turned(right, (3 - p) * HALO), 0.0),
        )

    for p in range(PLANES):
        sides = rim(from_west_ref[HALO : HALO + rows, :], from_east_ref[HALO : HALO + rows, :], p)
        north = rim(north_corners_ref[0:HALO, :], north_corners_ref[HALO:, :], p)
        south = rim(south_corners_ref[0:HALO, :], south_corners_ref[HALO:, :], p)
        for q in range(2):
            cols = slice(q * LANES, (q + 1) * LANES)
            whole = center_ref[p, :, cols] + sides[q]
            object_ref[p, 0:HALO, cols] = whole[0:HALO] + from_north_ref[p, :, cols] + north[q]
            object_ref[p, HALO : rows - HALO, cols] = whole[HALO : rows - HALO]
            object_ref[p, rows - HALO :, cols] = whole[rows - HALO :] + from_south_ref[p, :, cols] + south[q]


def probe_kernel(total_ref, probe_ref, probe_new_ref):
    total = total_ref[...]
    squares = jnp.sum(total * total, axis=0, keepdims=True)
    mean = jnp.sum(squares, axis=1, keepdims=True) / (total.shape[0] * total.shape[1])
    probe_new_ref[...] = probe_ref[...] - total * (STEP_SIZE / jnp.sqrt(mean + EPSILON))


def vmem(count):
    return [pl.BlockSpec(memory_space=pltpu.VMEM)] * count


def f32(*shape):
    return jax.ShapeDtypeStruct(shape, jnp.float32)


def moved(block, axis, distance):
    count = lax.axis_size(axis)
    return lax.ppermute(block, axis, [(i, (i + distance) % count) for i in range(count)])


def cost(us):
    return pl.CostEstimate(flops=int(us * 1e9), bytes_accessed=int(us * 3e6), transcendentals=0)


def call(kernel, outs, ins, scratch=(), scalars=0, limit=2, us=1):
    return pl.pallas_call(
        kernel,
        out_shape=outs,
        in_specs=[pl.BlockSpec(memory_space=pltpu.SMEM)] * scalars + vmem(ins),
        out_specs=vmem(len(outs)) if isinstance(outs, list) else vmem(1)[0],
        scratch_shapes=scratch,
        compiler_params=pltpu.CompilerParams(vmem_limit_bytes=limit * 2**20),
        cost_estimate=cost(us),
    )


def main_call(scans, ext_rows):
    pair = pltpu.VMEM((MODES // 2, 2 * WIN, 2 * WIN), jnp.bfloat16)
    modes = pltpu.VMEM((2, MODES, WIN, WIN), jnp.float32)
    run = pl.pallas_call(
        main_kernel,
        out_shape=[f32(2, MODES, WIN, WIN), f32(scans, PLANES, WIN, WIN), f32(PLANES, 3, ext_rows, LANES)],
        in_specs=[pl.BlockSpec(memory_space=pltpu.SMEM)] + vmem(8),
        out_specs=vmem(3),
        scratch_shapes=[
            pair, pair, pair, pair, modes, modes,
            pltpu.VMEM((PLANES, WIN, WIN), jnp.float32),
        ],
        input_output_aliases={1: 2},
        compiler_params=pltpu.CompilerParams(vmem_limit_bytes=12 * 2**20),
        cost_estimate=cost(12),
    )
    return lambda *args: run(*args)[:2]


def on_device(object_tiles, probe_modes, offsets, amplitude):
    rows, cols = object_tiles.shape[2:]
    ext_rows = rows + 2 * HALO
    scans = offsets.shape[2]
    tile = object_tiles.reshape(PLANES, rows, cols)
    tile, flat_offsets = lax.optimization_barrier((tile, offsets.reshape(2 * scans)))
    amp = amplitude.reshape(scans, WIN, WIN)
    flat = (2 * MODES * WIN, WIN)
    mats = jnp.asarray(matrices())
    devices = lax.axis_size("row") * lax.axis_size("col")

    north = moved(tile[:, rows - HALO :], "row", 1)
    south = moved(tile[:, :HALO], "row", -1)
    east_send, west_send = call(pack_kernel, [f32(rows, LANES)] * 2, 1)(tile)
    from_west = moved(east_send, "col", 1)
    from_east = moved(west_send, "col", -1)
    east_send, west_send = call(corner_kernel, [f32(2 * HALO, LANES)] * 2, 2)(north, south)
    west_corners = moved(east_send, "col", 1)
    east_corners = moved(west_send, "col", -1)

    ext = call(assemble_kernel, f32(PLANES, 3, ext_rows, LANES), 3, us=4)(tile, north, south)
    probe_grad, window_grad = main_call(scans, ext_rows)(
        flat_offsets, ext, from_west, from_east, west_corners, east_corners, amp, probe_modes, mats
    )
    center, north_rim, south_rim, east_rim, west_rim = call(
        scatter_kernel,
        [f32(PLANES, rows, cols)] + [f32(PLANES, HALO, cols)] * 2 + [f32(ext_rows, LANES)] * 2,
        1,
        [pltpu.VMEM((PLANES, 3, ext_rows, LANES), jnp.float32)],
        scalars=1,
        limit=6,
    )(flat_offsets, window_grad)

    parts = lax.all_to_all(probe_grad.reshape(devices, -1, LANES), BOTH, 0, 0, tiled=True)
    rim_from_west = moved(east_rim, "col", 1)
    rim_from_east = moved(west_rim, "col", -1)
    from_south = moved(north_rim, "row", -1)
    from_north = moved(south_rim, "row", 1)
    share = call(share_kernel, f32(*parts.shape), 3)(parts, rim_from_west, rim_from_east)
    total = lax.all_to_all(share, BOTH, 0, 0, tiled=True)
    to_north, to_south = call(rim_corner_kernel, [f32(2 * HALO, LANES)] * 2, 2)(rim_from_west, rim_from_east)
    south_corners = moved(to_north, "row", -1)
    north_corners = moved(to_south, "row", 1)
    object_grad = call(object_kernel, f32(PLANES, rows, cols), 7)(
        center, from_north, from_south, rim_from_west, rim_from_east, north_corners, south_corners
    )
    probe_new = call(probe_kernel, f32(*flat), 2)(total.reshape(flat), probe_modes.reshape(flat))
    return object_grad.reshape(object_tiles.shape), probe_new.reshape(probe_modes.shape)


def solution(mesh):
    placed = (
        P(None, None, "row", "col"),
        P(),
        P("row", "col", None, None),
        P("row", "col", None, None, None),
    )
    return jax.shard_map(
        on_device,
        mesh=mesh,
        in_specs=placed,
        out_specs=(P(None, None, "row", "col"), P()),
        check_vma=False,
    )
```

time: 81.5 us -> 83.2 us (1.021)
  waiting for transfers between devices: 22.7 us -> 25.7 us
  local copies, waits for them, and re-layouts: 5.67 us -> 3.08 us
  starting transfers between devices: 34.7 us -> 36.1 us
    ppermute x12, waiting for transfers between devices: 14.1 us -> 22.6 us  [moved(): lax.ppermute(block, axis, [(i, (i + distance) % count) for i in range(cou...]
    all_to_all x1, waiting for transfers between devices: 7.31 us -> 3.1 us  [on_device(): lax.all_to_all(probe_grad.reshape(devices, -1, LANES), BOTH, 0, 0, tiled=...]
    unnamed x25 -> x11, local copies, waits for them, and re-layouts: 4.53 us -> 2.01 us
    all_to_all x1, starting transfers between devices: 4.29 us -> 5.9 us  [on_device(): total = lax.all_to_all(share, BOTH, 0, 0, tiled=True)]
    all_to_all x1, waiting for transfers between devices: 1.39 us -> 0.01 us  [on_device(): total = lax.all_to_all(share, BOTH, 0, 0, tiled=True)]
    pallas_call x2 -> x5, Pallas kernels: 14.4 us -> 14.4 us  [the longest x1 12.1 us: main_call(): return lambda *args: run(*args)[:2]]
  transfers between devices with their start and end apart: 14 -> 14, of which waited for: 6 -> 9; matrix products, arithmetic and copies ran while one was open for 0% -> 0% of each run, Pallas kernels for 3% -> 4%
where the time goes in v3:
time: 83.2 us; the launch traced here: 82.8 us
  starting transfers between devices  36.1 us (43%)
  waiting for transfers between devices  25.7 us (31%)
  Pallas kernels  17.1 us (21%)
  local copies, waits for them, and re-layouts  3.08 us (4%)
    ppermute x12, waiting for transfers between devices, moved(): lax.ppermute(block, axis, [(i, (i + distance) % count) for i in range(cou...  22.6 us
    ppermute x12, starting transfers between devices, moved(): lax.ppermute(block, axis, [(i, (i + distance) % count) for i in range(cou...  21.7 us
    pallas_call x1, Pallas kernels, main_call(): return lambda *args: run(*args)[:2]  12.1 us
    all_to_all x1, starting transfers between devices, on_device(): lax.all_to_all(probe_grad.reshape(devices, -1, LANES), BOTH, 0, 0, tiled=...  8.52 us
    all_to_all x1, starting transfers between devices, on_device(): total = lax.all_to_all(share, BOTH, 0, 0, tiled=True)  5.9 us
    all_to_all x1, waiting for transfers between devices, on_device(): lax.all_to_all(probe_grad.reshape(devices, -1, LANES), BOTH, 0, 0, tiled=...  3.1 us
    unnamed x11, local copies, waits for them, and re-layouts  2.01 us
  transfers between devices with their start and end apart: 14, of which 9 were waited for; matrix products, arithmetic and copies ran while one was open for 0% of the time, Pallas kernels for 4%

profile of v3, /device:TPU:1, one launch (start us, length us, event | category | flops | bytes accessed | tf_op | source)
XLA Modules:
  0.0 82.8 jit_solution(11392184883554655721)
XLA Ops:
  0.6 0.8 copy.9
  1.4 0.1 reshape.29.offsets_ref
  1.5 1.0 %fusion = (f32[4,32,256]{2,1,0:T(8,128)S(1)}, f32[4,32,256]{2,1,0:T(8,128)S(1)}) fusion(f32[4,256,256]{2,1,0:T(8,128)} %bitcast.8), kind=kLoop, calls=%fused_computation | loop fusion | bytes 524288 | tf_op jit(solution)/shard_map/slice | solution.py:337
  2.5 6.1 %collective-permute-start.1 = (f32[4,32,256]{2,1,0:T(8,128)S(1)}, f32[4,32,256]{2,1,0:T(8,128)S(1)}, u32[]{:S(2)}, u32[]{:S(2)}) collective-permute-start(f32[4,32,256]{2,1,0:T(8,128)S(1)} %get-tuple-element.32), channel_id=1, source_target_pairs={{0,112},{16,0},{32,16},{48,32},{64,48},{80,64},{96,80},{112,96},{1... | collective-permute-start | bytes 393224 | tf_op jit(solution)/shard_map/ppermute | solution.py:287
  8.6 0.0 collective-permute-start
  8.6 0.0 copy-start
  8.6 1.2 %copy-done = f32[2,2,256,256]{3,2,1,0:T(8,128)S(1)} copy-done((f32[2,2,256,256]{3,2,1,0:T(8,128)S(1)}, f32[2,2,256,256]{3,2,1,0:T(8,128)}, u32[]{:S(2)}) %copy-start) | copy-done | bytes 1048600
  9.8 0.3 shard_map.69
  10.1 0.0 copy-start.1
  10.1 1.2 %collective-permute-start.2 = (f32[256,128]{1,0:T(8,128)S(1)}, f32[256,128]{1,0:T(8,128)S(1)}, u32[]{:S(2)}, u32[]{:S(2)}) collective-permute-start(f32[256,128]{1,0:T(8,128)S(1)} %get-tuple-element.19), channel_id=1, source_target_pairs={{0,1},{1,2},{2,3},{3,4},{4,5},{5,6},{6,7},{7,8},{8,9},{9,10},{10,1... | collective-permute-start | bytes 393224 | tf_op jit(solution)/shard_map/ppermute | solution.py:287
  11.3 0.0 collective-permute-start.3
  11.3 0.0 collective-permute-done.1.south_ref
  11.3 4.7 %collective-permute-done.north_ref = f32[4,32,256]{2,1,0:T(8,128)S(1)} collective-permute-done((f32[4,32,256]{2,1,0:T(8,128)S(1)}, f32[4,32,256]{2,1,0:T(8,128)S(1)}, u32[]{:S(2)}, u32[]{:S(2)}) %collective-permute-start) | collective-permute-done | bytes 131104 | tf_op jit(solution)/shard_map/ppermute | solution.py:287
  16.0 0.1 shard_map.70
  16.1 2.4 %collective-permute-start.4 = (f32[64,128]{1,0:T(8,128)S(1)}, f32[64,128]{1,0:T(8,128)S(1)}, u32[]{:S(2)}, u32[]{:S(2)}) collective-permute-start(f32[64,128]{1,0:T(8,128)S(1)} %get-tuple-element.21), channel_id=1, source_target_pairs={{0,1},{1,2},{2,3},{3,4},{4,5},{5,6},{6,7},{7,8},{8,9},{9,10},{10,1... | collective-permute-start | bytes 98312 | tf_op jit(solution)/shard_map/ppermute | solution.py:287
  18.5 0.0 copy-start.2
  18.5 0.0 copy-start.3
  18.5 0.0 copy-start.4
  18.5 0.0 collective-permute-start.5
  18.5 0.0 copy-done.1
  18.5 0.1 shard_map.68.ext_in
  18.6 0.0 collective-permute-done.2.from_west_ref
  18.6 0.0 collective-permute-done.3.from_east_ref
  18.6 0.9 %collective-permute-done.4.west_corners_ref = f32[64,128]{1,0:T(8,128)S(1)} collective-permute-done((f32[64,128]{1,0:T(8,128)S(1)}, f32[64,128]{1,0:T(8,128)S(1)}, u32[]{:S(2)}, u32[]{:S(2)}) %collective-permute-start.4) | collective-permute-done | bytes 32800 | tf_op jit(solution)/shard_map/ppermute | solution.py:287
  19.5 2.3 %collective-permute-done.5.east_corners_ref = f32[64,128]{1,0:T(8,128)S(1)} collective-permute-done((f32[64,128]{1,0:T(8,128)S(1)}, f32[64,128]{1,0:T(8,128)S(1)}, u32[]{:S(2)}, u32[]{:S(2)}) %collective-permute-start.5) | collective-permute-done | bytes 32800 | tf_op jit(solution)/shard_map/ppermute | solution.py:287
  21.8 0.0 copy-done.2
  21.8 0.0 copy-done.3
  21.8 0.0 copy-done.4
  21.8 12.1 %shard_map.71 = (f32[2,4,128,128]{3,2,1,0:T(8,128)}, f32[3,4,128,128]{3,2,1,0:T(8,128)S(1)}, f32[4,3,320,128]{3,2,1,0:T(8,128)S(1)}) custom-call(s32[6]{0:T(128)S(1)} %reshape.29.offsets_ref, f32[4,3,320,128]{3,2,1,0:T(8,128)S(1)} %shard_map.68.ext_in, f32[256,128]{1,0:T(8,128)S(1)} %collective-permute-done.2.from_west_ref, ...), custom_call_target="tpu_custom_call", output_to_operand_aliasing={{2}: (1, {})} | custom-call | flops 12000000000 | bytes 36000000 | tf_op jit(solution)/shard_map/pallas_call | solution.py:322
  33.9 8.5 %all-to-all-start = ((f32[128,8,128]{2,1,0:T(8,128)}), f32[128,8,128]{2,1,0:T(8,128)S(1)}, u32[]{:S(2)}, u32[]{:S(2)}) async-start(f32[128,8,128]{2,1,0:T(8,128)} %bitcast.3), calls=%async_computation | async-start | bytes 1048576 | tf_op jit(solution)/shard_map/all_to_all | solution.py:358
  42.5 1.2 %shard_map.72 = (f32[4,256,256]{2,1,0:T(8,128)S(1)}, f32[4,32,256]{2,1,0:T(8,128)S(1)}, f32[4,32,256]{2,1,0:T(8,128)S(1)}, f32[320,128]{1,0:T(8,128)S(1)}, f32[320,128]{1,0:T(8,128)S(1)}) custom-call(s32[6]{0:T(128)S(1)} %reshape.29.offsets_ref, f32[3,4,128,128]{3,2,1,0:T(8,128)S(1)} %get-tuple-element.23.window_grad_ref), custom_call_target="tpu_custom_call" | custom-call | flops 1000000000 | bytes 3000000 | tf_op jit(solution)/shard_map/pallas_call | solution.py:349
  43.7 1.7 %collective-permute-start.8 = (f32[320,128]{1,0:T(8,128)S(1)}, f32[320,128]{1,0:T(8,128)S(1)}, u32[]{:S(2)}, u32[]{:S(2)}) collective-permute-start(f32[320,128]{1,0:T(8,128)S(1)} %get-tuple-element.27), channel_id=1, source_target_pairs={{0,1},{1,2},{2,3},{3,4},{4,5},{5,6},{6,7},{7,8},{8,9},{9,10},{10,1... | collective-permute-start | bytes 491528 | tf_op jit(solution)/shard_map/ppermute | solution.py:287
  45.4 0.0 collective-permute-start.9
  45.4 4.5 %collective-permute-done.8.from_west_ref = f32[320,128]{1,0:T(8,128)S(1)} collective-permute-done((f32[320,128]{1,0:T(8,128)S(1)}, f32[320,128]{1,0:T(8,128)S(1)}, u32[]{:S(2)}, u32[]{:S(2)}) %collective-permute-start.8) | collective-permute-done | bytes 163872 | tf_op jit(solution)/shard_map/ppermute | solution.py:287
  49.9 3.6 %collective-permute-done.9.from_east_ref = f32[320,128]{1,0:T(8,128)S(1)} collective-permute-done((f32[320,128]{1,0:T(8,128)S(1)}, f32[320,128]{1,0:T(8,128)S(1)}, u32[]{:S(2)}, u32[]{:S(2)}) %collective-permute-start.9) | collective-permute-done | bytes 163872 | tf_op jit(solution)/shard_map/ppermute | solution.py:287
  53.5 3.1 %all-to-all-done.parts_ref = f32[128,8,128]{2,1,0:T(8,128)S(1)} async-done(((f32[128,8,128]{2,1,0:T(8,128)}), f32[128,8,128]{2,1,0:T(8,128)S(1)}, u32[]{:S(2)}, u32[]{:S(2)}) %all-to-all-start) | async-done | bytes 524320 | tf_op jit(solution)/shard_map/all_to_all | solution.py:358
  56.6 1.0 %shard_map.75 = f32[128,8,128]{2,1,0:T(8,128)} custom-call(f32[128,8,128]{2,1,0:T(8,128)S(1)} %all-to-all-done.parts_ref, f32[320,128]{1,0:T(8,128)S(1)} %collective-permute-done.8.from_west_ref, f32[320,128]{1,0:T(8,128)S(1)} %collective-permute-done.9.from_east_ref), custom_call_target="tpu_custom_call" | custom-call | flops 1000000000 | bytes 3000000 | tf_op jit(solution)/shard_map/pallas_call | solution.py:363
  57.6 5.9 %all-to-all-start.1 = ((f32[128,8,128]{2,1,0:T(8,128)}), f32[128,8,128]{2,1,0:T(8,128)S(1)}, u32[]{:S(2)}, u32[]{:S(2)}) async-start(f32[128,8,128]{2,1,0:T(8,128)} %shard_map.75), calls=%async_computation.1 | async-start | bytes 1048576 | tf_op jit(solution)/shard_map/all_to_all | solution.py:364
  63.5 3.0 %collective-permute-start.6 = (f32[4,32,256]{2,1,0:T(8,128)S(1)}, f32[4,32,256]{2,1,0:T(8,128)S(1)}, u32[]{:S(2)}, u32[]{:S(2)}) collective-permute-start(f32[4,32,256]{2,1,0:T(8,128)S(1)} %get-tuple-element.25), channel_id=1, source_target_pairs={{0,16},{16,32},{32,48},{48,64},{64,80},{80,96},{96,112},{112,0},{1... | collective-permute-start | bytes 393224 | tf_op jit(solution)/shard_map/ppermute | solution.py:287
  66.5 2.3 %collective-permute-start.7 = (f32[4,32,256]{2,1,0:T(8,128)S(1)}, f32[4,32,256]{2,1,0:T(8,128)S(1)}, u32[]{:S(2)}, u32[]{:S(2)}) collective-permute-start(f32[4,32,256]{2,1,0:T(8,128)S(1)} %get-tuple-element.26), channel_id=1, source_target_pairs={{0,112},{16,0},{32,16},{48,32},{64,48},{80,64},{96,80},{112,96},{1... | collective-permute-start | bytes 393224 | tf_op jit(solution)/shard_map/ppermute | solution.py:287
  68.8 0.7 collective-permute-start.10
  69.4 4.4 %collective-permute-start.11 = (f32[64,128]{1,0:T(8,128)S(1)}, f32[64,128]{1,0:T(8,128)S(1)}, u32[]{:S(2)}, u32[]{:S(2)}) collective-permute-start(f32[64,128]{1,0:T(8,128)S(1)} %get-tuple-element.30), channel_id=1, source_target_pairs={{0,112},{16,0},{32,16},{48,32},{64,48},{80,64},{96,80},{112,96},{1... | collective-permute-start | bytes 98312 | tf_op jit(solution)/shard_map/ppermute | solution.py:287
  73.8 3.3 %collective-permute-done.6.from_north_ref = f32[4,32,256]{2,1,0:T(8,128)S(1)} collective-permute-done((f32[4,32,256]{2,1,0:T(8,128)S(1)}, f32[4,32,256]{2,1,0:T(8,128)S(1)}, u32[]{:S(2)}, u32[]{:S(2)}) %collective-permute-start.6) | collective-permute-done | bytes 131104 | tf_op jit(solution)/shard_map/ppermute | solution.py:287
  77.1 0.6 collective-permute-done.7.from_south_ref
  77.7 2.6 %collective-permute-done.10.north_corners_ref = f32[64,128]{1,0:T(8,128)S(1)} collective-permute-done((f32[64,128]{1,0:T(8,128)S(1)}, f32[64,128]{1,0:T(8,128)S(1)}, u32[]{:S(2)}, u32[]{:S(2)}) %collective-permute-start.10) | collective-permute-done | bytes 32800 | tf_op jit(solution)/shard_map/ppermute | solution.py:287
  80.3 0.0 collective-permute-done.11.south_corners_ref
  80.3 1.3 %shard_map.74 = f32[4,256,256]{2,1,0:T(8,128)} custom-call(f32[4,256,256]{2,1,0:T(8,128)S(1)} %get-tuple-element.24.center_ref, f32[4,32,256]{2,1,0:T(8,128)S(1)} %collective-permute-done.6.from_north_ref, f32[4,32,256]{2,1,0:T(8,128)S(1)} %collective-permute-done.7.from_south_ref, f32[320,128]{1,0:T(8,128)S(1)} %collective-permute-done.8.from_west_ref, ...), custom_call_target="tpu_custom_call" | custom-call | flops 1000000000 | bytes 3000000 | tf_op jit(solution)/shard_map/pallas_call | solution.py:368
  81.7 0.0 all-to-all-done.1
  81.7 1.1 %shard_map.76 = f32[1024,128]{1,0:T(8,128)} custom-call(f32[1024,128]{1,0:T(8,128)S(1)} %bitcast.7, f32[1024,128]{1,0:T(8,128)S(1)} %bitcast.11), custom_call_target="tpu_custom_call" | custom-call | flops 1000000000 | bytes 3000000 | tf_op jit(solution)/shard_map/pallas_call | solution.py:371
  (1 shorter events, 0.0 us)
Async XLA Ops:
  2.5 8.8 %collective-permute-start.1 = (f32[4,32,256]{2,1,0:T(8,128)S(1)}, f32[4,32,256]{2,1,0:T(8,128)S(1)}, u32[]{:S(2)}, u32[]{:S(2)}) collective-permute-start(f32[4,32,256]{2,1,0:T(8,128)S(1)} %get-tuple-element.32), channel_id=1, source_target_pairs={{0,112},{16,0},{32,16},{48,32},{64,48},{80,64},{96,80},{112,96},{1... | collective-permute-start | bytes 393224 | tf_op jit(solution)/shard_map/ppermute | solution.py:287
  8.6 7.4 %collective-permute-start = (f32[4,32,256]{2,1,0:T(8,128)S(1)}, f32[4,32,256]{2,1,0:T(8,128)S(1)}, u32[]{:S(2)}, u32[]{:S(2)}) collective-permute-start(f32[4,32,256]{2,1,0:T(8,128)S(1)} %get-tuple-element.33), channel_id=1, source_target_pairs={{0,16},{16,32},{32,48},{48,64},{64,80},{80,96},{96,112},{112,0},{1... | collective-permute-start | bytes 393224 | tf_op jit(solution)/shard_map/ppermute | solution.py:287
  8.6 1.2 %copy-start = (f32[2,2,256,256]{3,2,1,0:T(8,128)S(1)}, f32[2,2,256,256]{3,2,1,0:T(8,128)}, u32[]{:S(2)}) copy-start(f32[2,2,256,256]{3,2,1,0:T(8,128)} %param.5) | copy-start | bytes 3145732
  10.1 8.4 %copy-start.1 = (f32[2,2,256,256]{3,2,1,0:T(8,128)S(1)}, f32[2,2,256,256]{3,2,1,0:T(8,128)}, u32[]{:S(2)}) copy-start(f32[2,2,256,256]{3,2,1,0:T(8,128)} %param.5) | copy-start | bytes 3145732
  10.1 8.5 %collective-permute-start.2 = (f32[256,128]{1,0:T(8,128)S(1)}, f32[256,128]{1,0:T(8,128)S(1)}, u32[]{:S(2)}, u32[]{:S(2)}) collective-permute-start(f32[256,128]{1,0:T(8,128)S(1)} %get-tuple-element.19), channel_id=1, source_target_pairs={{0,1},{1,2},{2,3},{3,4},{4,5},{5,6},{6,7},{7,8},{8,9},{9,10},{10,1... | collective-permute-start | bytes 393224 | tf_op jit(solution)/shard_map/ppermute | solution.py:287
  11.3 7.3 %collective-permute-start.3 = (f32[256,128]{1,0:T(8,128)S(1)}, f32[256,128]{1,0:T(8,128)S(1)}, u32[]{:S(2)}, u32[]{:S(2)}) collective-permute-start(f32[256,128]{1,0:T(8,128)S(1)} %get-tuple-element.20), channel_id=1, source_target_pairs={{0,15},{1,0},{2,1},{3,2},{4,3},{5,4},{6,5},{7,6},{8,7},{9,8},{10,9... | collective-permute-start | bytes 393224 | tf_op jit(solution)/shard_map/ppermute | solution.py:287
  16.1 3.4 %collective-permute-start.4 = (f32[64,128]{1,0:T(8,128)S(1)}, f32[64,128]{1,0:T(8,128)S(1)}, u32[]{:S(2)}, u32[]{:S(2)}) collective-permute-start(f32[64,128]{1,0:T(8,128)S(1)} %get-tuple-element.21), channel_id=1, source_target_pairs={{0,1},{1,2},{2,3},{3,4},{4,5},{5,6},{6,7},{7,8},{8,9},{9,10},{10,1... | collective-permute-start | bytes 98312 | tf_op jit(solution)/shard_map/ppermute | solution.py:287
  18.5 3.3 %copy-start.2 = (f32[2,4,128,128]{3,2,1,0:T(8,128)S(1)}, f32[2,4,128,128]{3,2,1,0:T(8,128)}, u32[]{:S(2)}) copy-start(f32[2,4,128,128]{3,2,1,0:T(8,128)} %probe_ref.1) | copy-start | bytes 1572868
  18.5 3.3 %copy-start.3 = (f32[1,1,3,128,128]{4,3,2,1,0:T(8,128)S(1)}, f32[1,1,3,128,128]{4,3,2,1,0:T(8,128)}, u32[]{:S(2)}) copy-start(f32[1,1,3,128,128]{4,3,2,1,0:T(8,128)} %param.8) | copy-start | bytes 589828
  18.5 3.4 %copy-start.4 = (bf16[4,2,256,256]{3,2,1,0:T(8,128)(2,1)S(1)}, bf16[4,2,256,256]{3,2,1,0:T(8,128)(2,1)}, u32[]{:S(2)}) copy-start(bf16[4,2,256,256]{3,2,1,0:T(8,128)(2,1)} %constant.2.clone.mat_ref) | copy-start | bytes 3145732
  18.5 3.3 %collective-permute-start.5 = (f32[64,128]{1,0:T(8,128)S(1)}, f32[64,128]{1,0:T(8,128)S(1)}, u32[]{:S(2)}, u32[]{:S(2)}) collective-permute-start(f32[64,128]{1,0:T(8,128)S(1)} %get-tuple-element.22), channel_id=1, source_target_pairs={{0,15},{1,0},{2,1},{3,2},{4,3},{5,4},{6,5},{7,6},{8,7},{9,8},{10,9... | collective-permute-start | bytes 98312 | tf_op jit(solution)/shard_map/ppermute | solution.py:287
  33.9 22.7 %all-to-all-start = ((f32[128,8,128]{2,1,0:T(8,128)}), f32[128,8,128]{2,1,0:T(8,128)S(1)}, u32[]{:S(2)}, u32[]{:S(2)}) async-start(f32[128,8,128]{2,1,0:T(8,128)} %bitcast.3), calls=%async_computation | async-start | bytes 1048576 | tf_op jit(solution)/shard_map/all_to_all | solution.py:358
  43.7 6.2 %collective-permute-start.8 = (f32[320,128]{1,0:T(8,128)S(1)}, f32[320,128]{1,0:T(8,128)S(1)}, u32[]{:S(2)}, u32[]{:S(2)}) collective-permute-start(f32[320,128]{1,0:T(8,128)S(1)} %get-tuple-element.27), channel_id=1, source_target_pairs={{0,1},{1,2},{2,3},{3,4},{4,5},{5,6},{6,7},{7,8},{8,9},{9,10},{10,1... | collective-permute-start | bytes 491528 | tf_op jit(solution)/shard_map/ppermute | solution.py:287
  45.4 8.2 %collective-permute-start.9 = (f32[320,128]{1,0:T(8,128)S(1)}, f32[320,128]{1,0:T(8,128)S(1)}, u32[]{:S(2)}, u32[]{:S(2)}) collective-permute-start(f32[320,128]{1,0:T(8,128)S(1)} %get-tuple-element.28), channel_id=1, source_target_pairs={{0,15},{1,0},{2,1},{3,2},{4,3},{5,4},{6,5},{7,6},{8,7},{9,8},{10,9... | collective-permute-start | bytes 491528 | tf_op jit(solution)/shard_map/ppermute | solution.py:287
  57.6 24.1 %all-to-all-start.1 = ((f32[128,8,128]{2,1,0:T(8,128)}), f32[128,8,128]{2,1,0:T(8,128)S(1)}, u32[]{:S(2)}, u32[]{:S(2)}) async-start(f32[128,8,128]{2,1,0:T(8,128)} %shard_map.75), calls=%async_computation.1 | async-start | bytes 1048576 | tf_op jit(solution)/shard_map/all_to_all | solution.py:364
  63.5 13.6 %collective-permute-start.6 = (f32[4,32,256]{2,1,0:T(8,128)S(1)}, f32[4,32,256]{2,1,0:T(8,128)S(1)}, u32[]{:S(2)}, u32[]{:S(2)}) collective-permute-start(f32[4,32,256]{2,1,0:T(8,128)S(1)} %get-tuple-element.25), channel_id=1, source_target_pairs={{0,16},{16,32},{32,48},{48,64},{64,80},{80,96},{96,112},{112,0},{1... | collective-permute-start | bytes 393224 | tf_op jit(solution)/shard_map/ppermute | solution.py:287
  66.5 11.3 %collective-permute-start.7 = (f32[4,32,256]{2,1,0:T(8,128)S(1)}, f32[4,32,256]{2,1,0:T(8,128)S(1)}, u32[]{:S(2)}, u32[]{:S(2)}) collective-permute-start(f32[4,32,256]{2,1,0:T(8,128)S(1)} %get-tuple-element.26), channel_id=1, source_target_pairs={{0,112},{16,0},{32,16},{48,32},{64,48},{80,64},{96,80},{112,96},{1... | collective-permute-start | bytes 393224 | tf_op jit(solution)/shard_map/ppermute | solution.py:287
  68.8 11.6 %collective-permute-start.10 = (f32[64,128]{1,0:T(8,128)S(1)}, f32[64,128]{1,0:T(8,128)S(1)}, u32[]{:S(2)}, u32[]{:S(2)}) collective-permute-start(f32[64,128]{1,0:T(8,128)S(1)} %get-tuple-element.29), channel_id=1, source_target_pairs={{0,16},{16,32},{32,48},{48,64},{64,80},{80,96},{96,112},{112,0},{1... | collective-permute-start | bytes 98312 | tf_op jit(solution)/shard_map/ppermute | solution.py:287
  69.4 10.9 %collective-permute-start.11 = (f32[64,128]{1,0:T(8,128)S(1)}, f32[64,128]{1,0:T(8,128)S(1)}, u32[]{:S(2)}, u32[]{:S(2)}) collective-permute-start(f32[64,128]{1,0:T(8,128)S(1)} %get-tuple-element.30), channel_id=1, source_target_pairs={{0,112},{16,0},{32,16},{48,32},{64,48},{80,64},{96,80},{112,96},{1... | collective-permute-start | bytes 98312 | tf_op jit(solution)/shard_map/ppermute | solution.py:287

commit v4 on v3

v4 whole, which is shorter than its diff:
```python
import jax
import jax.numpy as jnp
import numpy as np
from jax import lax
from jax.experimental import pallas as pl
from jax.experimental.pallas import tpu as pltpu
from jax.sharding import PartitionSpec as P

HALO = 32
WIN = 128
MODES = 4
PLANES = 4
LANES = 128
PROP = 0.002
SHIFT_AMP = 0.5
STEP_SIZE = 0.5
EPSILON = 1e-06
BOTH = ("row", "col")


def matrices():
    k = np.arange(WIN)
    c = np.exp(-2j * np.pi * (np.outer(k, k) % WIN) / WIN) / np.sqrt(WIN)
    f = ((k + WIN // 2) % WIN - WIN // 2).astype(np.float64)
    g = c.conj() @ np.diag(np.exp(-1j * PROP * f * f)) @ c
    stack = []
    for m in (c, c.conj(), g, g.conj()):
        w = np.block([[m.real, m.imag], [-m.imag, m.real]]).astype(np.float32)
        high = w.astype(jnp.bfloat16)
        low = (w - high.astype(np.float32)).astype(jnp.bfloat16)
        stack.append(np.stack([high, low]))
    return np.stack(stack)


C, C_CONJ, G, G_CONJ = range(4)
BLOCKS = 2
ROWS = 2 * WIN // BLOCKS


def lane_iota(rows):
    return lax.broadcasted_iota(jnp.int32, (rows, LANES), 1)


def edges(src, rows):
    lane = lane_iota(rows)
    east = jnp.zeros((rows, LANES), jnp.float32)
    west = jnp.zeros((rows, LANES), jnp.float32)
    for p in range(PLANES):
        here = (lane >= p * HALO) & (lane < (p + 1) * HALO)
        east = jnp.where(here, turned(src[p, :, LANES : 2 * LANES], (p - 3) * HALO), east)
        west = jnp.where(here, turned(src[p, :, 0:LANES], p * HALO), west)
    return east, west


def turned(block, shift):
    return pltpu.roll(block, shift % LANES, 1) if shift % LANES else block


def pack_kernel(tile_ref, east_ref, west_ref):
    east_ref[...], west_ref[...] = edges(tile_ref, tile_ref.shape[1])


def corner_kernel(north_ref, south_ref, east_ref, west_ref):
    east_ref[0:HALO, :], west_ref[0:HALO, :] = edges(north_ref, HALO)
    east_ref[HALO:, :], west_ref[HALO:, :] = edges(south_ref, HALO)


def split(value):
    high = value.astype(jnp.bfloat16)
    return high, (value - high.astype(jnp.float32)).astype(jnp.bfloat16)


def dot(left, right):
    return jnp.dot(left, right, preferred_element_type=jnp.float32)


def assemble_kernel(tile_ref, north_ref, south_ref, ext):
    rows = tile_ref.shape[1]
    for p in range(PLANES):
        for q in range(2):
            cols = slice(q * LANES, (q + 1) * LANES)
            ext[p, q, 0:HALO, :] = north_ref[p, :, cols]
            ext[p, q, HALO : HALO + rows, :] = tile_ref[p, :, cols]
            ext[p, q, HALO + rows :, :] = south_ref[p, :, cols]


def place(offsets_ref, s, q_count=3):
    start = lax.rem(offsets_ref[1, s] + (q_count * LANES - HALO), q_count * LANES)
    first = lax.div(start, LANES)
    return offsets_ref[0, s], first, lax.rem(first + 1, q_count), lax.rem(start, LANES)


def main_kernel(
    offsets_ref, ext_in, from_west_ref, from_east_ref, west_corners_ref, east_corners_ref, amp_ref, probe_ref, mat_ref,
    probe_grad_ref, center_ref, north_rim_ref, south_rim_ref, east_rim_ref, west_rim_ref, ext,
    rh, rl, lh, ll, field, d_keep, win, factor, grad,
):
    del ext_in
    ext_rows = ext.shape[2]
    last = ext_rows - HALO

    def beside(left, right, p):
        low = lane_iota(left.shape[0]) < 2 * HALO
        return jnp.where(low, turned(right, -p * HALO), turned(left, (3 - p) * HALO))

    for p in range(PLANES):
        ext[p, 2, 0:HALO, :] = beside(west_corners_ref[0:HALO, :], east_corners_ref[0:HALO, :], p)
        ext[p, 2, HALO:last, :] = beside(from_west_ref[...], from_east_ref[...], p)
        ext[p, 2, last:ext_rows, :] = beside(west_corners_ref[HALO:, :], east_corners_ref[HALO:, :], p)

    lane = lane_iota(WIN)
    chains = range(MODES // 2)
    scans = range(amp_ref.shape[0])

    def put(high, low, at, value):
        high[at], low[at] = split(value)

    def run(*accs):
        def blocks(s, c):
            first = (s * len(chains) + c) * BLOCKS
            return accs[first : first + BLOCKS]

        def multiply(s, c, rhs, lhss, stage):
            pltpu.matmul_push_rhs(rhs, stage, c)
            for lhs in lhss:
                for b, acc in enumerate(blocks(s, c)):
                    pltpu.matmul_acc_lhs(acc, lhs[b * ROWS : (b + 1) * ROWS, :], stage)
                    stage = None

        def start_right(s, which):
            for c in chains:
                multiply(s, c, mat_ref[which, 0], (rh[s, c], rl[s, c]), 0)
                multiply(s, c, mat_ref[which, 1], (rh[s, c],), 1)

        def start_left(s, which):
            high, low = mat_ref[which ^ 1, 0], mat_ref[which ^ 1, 1]
            for c in chains:
                multiply(s, c, lh[s, c], (high, low), 0)
                multiply(s, c, ll[s, c], (high,), 1)

        def planes_right(s):
            for c in chains:
                out = jnp.concatenate([pltpu.matmul_pop(acc) for acc in blocks(s, c)], axis=0)
                for k in range(2):
                    yield c, k, out[k * WIN : (k + 1) * WIN, 0:WIN], out[k * WIN : (k + 1) * WIN, WIN:]

        def planes_left(s):
            for c in chains:
                out = jnp.concatenate([pltpu.matmul_pop(acc) for acc in blocks(s, c)], axis=0)
                for k in range(2):
                    yield c, k, out[0:WIN, k * WIN : (k + 1) * WIN], out[WIN:, k * WIN : (k + 1) * WIN]

        def put_r(s, c, k, real, imag):
            rows = slice(k * WIN, (k + 1) * WIN)
            put(rh, rl, (s, c, rows, slice(0, WIN)), real)
            put(rh, rl, (s, c, rows, slice(WIN, 2 * WIN)), imag)

        def put_l(s, c, k, real, imag):
            cols = slice(k * WIN, (k + 1) * WIN)
            put(lh, ll, (s, c, slice(0, WIN), cols), real)
            put(lh, ll, (s, c, slice(WIN, 2 * WIN), cols), imag)

        def steps(s):
            row, q, q_next, shift = place(offsets_ref, s)
            back = lax.rem(LANES - shift, LANES)

            def scatter(p, value):
                value = pltpu.roll(value, shift, 1)
                grad[p, q, pl.ds(row, WIN), :] += jnp.where(lane >= shift, value, 0.0)
                grad[p, q_next, pl.ds(row, WIN), :] += jnp.where(lane < shift, value, 0.0)

            for p in range(PLANES):
                a = pltpu.roll(ext[p, q, pl.ds(row, WIN), :], back, 1)
                b = pltpu.roll(ext[p, q_next, pl.ds(row, WIN), :], back, 1)
                win[s, p] = jnp.where(lane < LANES - shift, a, b)
            for c in chains:
                for k in range(2):
                    pr, pi = probe_ref[0, 2 * c + k], probe_ref[1, 2 * c + k]
                    put_r(s, c, k, pr * win[s, 0] - pi * win[s, 2], pr * win[s, 2] + pi * win[s, 0])
            start_right(s, G)
            if s == 0:
                grad[...] = jnp.zeros_like(grad)
            yield
            for c, k, real, imag in planes_right(s):
                put_l(s, c, k, real, imag)
            start_left(s, G)
            yield
            for c, k, real, imag in planes_left(s):
                m = 2 * c + k
                d_keep[s, 0, m] = real
                d_keep[s, 1, m] = imag
                second_r, second_i = win[s, 1], win[s, 3]
                put_l(s, c, k, real * second_r - imag * second_i, real * second_i + imag * second_r)
            start_left(s, C)
            yield
            for c, k, real, imag in planes_left(s):
                put_r(s, c, k, real, imag)
            start_right(s, C)
            yield
            intensity = jnp.full((WIN, WIN), SHIFT_AMP, jnp.float32)
            for c, k, real, imag in planes_right(s):
                m = 2 * c + k
                field[s, 0, m] = real
                field[s, 1, m] = imag
                intensity = intensity + (real * real + imag * imag)
            factor[s] = 2.0 - 2.0 * amp_ref[s] / jnp.sqrt(intensity)
            for c in chains:
                for k in range(2):
                    m = 2 * c + k
                    put_r(s, c, k, field[s, 0, m] * factor[s], field[s, 1, m] * factor[s])
            start_right(s, C_CONJ)
            yield
            for c, k, real, imag in planes_right(s):
                put_l(s, c, k, real, imag)
            start_left(s, C_CONJ)
            yield
            sum_r = jnp.zeros((WIN, WIN), jnp.float32)
            sum_i = jnp.zeros((WIN, WIN), jnp.float32)
            for c, k, real, imag in planes_left(s):
                dr, di = d_keep[s, 0, 2 * c + k], d_keep[s, 1, 2 * c + k]
                second_r, second_i = win[s, 1], win[s, 3]
                sum_r = sum_r + (dr * real + di * imag)
                sum_i = sum_i + (dr * imag - di * real)
                put_l(s, c, k, second_r * real + second_i * imag, second_r * imag - second_i * real)
            start_left(s, G_CONJ)
            scatter(1, sum_r)
            scatter(3, sum_i)
            yield
            for c, k, real, imag in planes_left(s):
                put_r(s, c, k, real, imag)
            start_right(s, G_CONJ)
            yield
            sum_r = jnp.zeros((WIN, WIN), jnp.float32)
            sum_i = jnp.zeros((WIN, WIN), jnp.float32)
            for c, k, real, imag in planes_right(s):
                m = 2 * c + k
                pr, pi = probe_ref[0, m], probe_ref[1, m]
                first_r, first_i = win[s, 0], win[s, 2]
                sum_r = sum_r + (pr * real + pi * imag)
                sum_i = sum_i + (pr * imag - pi * real)
                grad_r = first_r * real + first_i * imag
                grad_i = first_r * imag - first_i * real
                probe_grad_ref[0, m] = grad_r if s == 0 else probe_grad_ref[0, m] + grad_r
                probe_grad_ref[1, m] = grad_i if s == 0 else probe_grad_ref[1, m] + grad_i
            scatter(0, sum_r)
            scatter(2, sum_i)

        under_way = [steps(s) for s in scans]
        while under_way:
            under_way = [step for step in under_way if next(step, True) is None]

    pl.run_scoped(
        run, *[pltpu.ACC(c)((ROWS, 2 * WIN), jnp.float32) for _ in scans for c in chains for _ in range(BLOCKS)]
    )

    lane_all = lane_iota(ext_rows)
    east = jnp.zeros((ext_rows, LANES), jnp.float32)
    west = jnp.zeros((ext_rows, LANES), jnp.float32)
    for p in range(PLANES):
        for q in range(2):
            cols = slice(q * LANES, (q + 1) * LANES)
            north_rim_ref[p, :, cols] = grad[p, q, 0:HALO, :]
            center_ref[p, :, cols] = grad[p, q, HALO:last, :]
            south_rim_ref[p, :, cols] = grad[p, q, last:ext_rows, :]
        third = grad[p, 2]
        here = (lane_all >= p * HALO) & (lane_all < (p + 1) * HALO)
        east = jnp.where(here, turned(third, p * HALO), east)
        west = jnp.where(here, turned(third, (p - 3) * HALO), west)
    east_rim_ref[...] = east
    west_rim_ref[...] = west


def rim_corner_kernel(from_west_ref, from_east_ref, to_north_ref, to_south_ref):
    for k, ref in enumerate((from_west_ref, from_east_ref)):
        to_north_ref[k * HALO : (k + 1) * HALO, :] = ref[0:HALO, :]
        to_south_ref[k * HALO : (k + 1) * HALO, :] = ref[ref.shape[0] - HALO :, :]


def share_kernel(parts_ref, from_north_ref, from_south_ref, share_ref):
    del from_north_ref, from_south_ref
    share_ref[...] = jnp.broadcast_to(jnp.sum(parts_ref[...], axis=0)[None], share_ref.shape)


def object_kernel(
    center_ref, from_north_ref, from_south_ref, from_west_ref, from_east_ref, north_corners_ref, south_corners_ref,
    object_ref,
):
    rows = center_ref.shape[1]

    def rim(left, right, p):
        lane = lane_iota(left.shape[0])
        return (
            jnp.where(lane < HALO, turned(left, -p * HALO), 0.0),
            jnp.where(lane >= LANES - HALO, turned(right, (3 - p) * HALO), 0.0),
        )

    for p in range(PLANES):
        sides = rim(from_west_ref[HALO : HALO + rows, :], from_east_ref[HALO : HALO + rows, :], p)
        north = rim(north_corners_ref[0:HALO, :], north_corners_ref[HALO:, :], p)
        south = rim(south_corners_ref[0:HALO, :], south_corners_ref[HALO:, :], p)
        for q in range(2):
            cols = slice(q * LANES, (q + 1) * LANES)
            whole = center_ref[p, :, cols] + sides[q]
            object_ref[p, 0:HALO, cols] = whole[0:HALO] + from_north_ref[p, :, cols] + north[q]
            object_ref[p, HALO : rows - HALO, cols] = whole[HALO : rows - HALO]
            object_ref[p, rows - HALO :, cols] = whole[rows - HALO :] + from_south_ref[p, :, cols] + south[q]


def probe_kernel(total_ref, probe_ref, probe_new_ref):
    total = total_ref[...]
    squares = jnp.sum(total * total, axis=0, keepdims=True)
    mean = jnp.sum(squares, axis=1, keepdims=True) / (total.shape[0] * total.shape[1])
    probe_new_ref[...] = probe_ref[...] - total * (STEP_SIZE / jnp.sqrt(mean + EPSILON))


def vmem(count):
    return [pl.BlockSpec(memory_space=pltpu.VMEM)] * count


def f32(*shape):
    return jax.ShapeDtypeStruct(shape, jnp.float32)


def moved(block, axis, distance):
    count = lax.axis_size(axis)
    return lax.ppermute(block, axis, [(i, (i + distance) % count) for i in range(count)])


def cost(us):
    return pl.CostEstimate(flops=int(us * 1e9), bytes_accessed=int(us * 3e6), transcendentals=0)


def call(kernel, outs, ins, scratch=(), scalars=0, limit=2, us=0):
    return pl.pallas_call(
        kernel,
        out_shape=outs,
        in_specs=[pl.BlockSpec(memory_space=pltpu.SMEM)] * scalars + vmem(ins),
        out_specs=vmem(len(outs)) if isinstance(outs, list) else vmem(1)[0],
        scratch_shapes=scratch,
        compiler_params=pltpu.CompilerParams(vmem_limit_bytes=limit * 2**20),
        cost_estimate=cost(us) if us else None,
    )


def main_call(scans, rows, cols):
    ext_rows = rows + 2 * HALO
    pair = pltpu.VMEM((scans, MODES // 2, 2 * WIN, 2 * WIN), jnp.bfloat16)
    modes = pltpu.VMEM((scans, 2, MODES, WIN, WIN), jnp.float32)
    outs = [f32(2, MODES, WIN, WIN), f32(PLANES, rows, cols)]
    outs += [f32(PLANES, HALO, cols)] * 2 + [f32(ext_rows, LANES)] * 2 + [f32(PLANES, 3, ext_rows, LANES)]
    run = pl.pallas_call(
        main_kernel,
        out_shape=outs,
        in_specs=[pl.BlockSpec(memory_space=pltpu.SMEM)] + vmem(8),
        out_specs=vmem(len(outs)),
        scratch_shapes=[
            pair, pair, pair, pair, modes, modes,
            pltpu.VMEM((scans, PLANES, WIN, WIN), jnp.float32),
            pltpu.VMEM((scans, WIN, WIN), jnp.float32),
            pltpu.VMEM((PLANES, 3, ext_rows, LANES), jnp.float32),
        ],
        input_output_aliases={1: 6},
        compiler_params=pltpu.CompilerParams(vmem_limit_bytes=24 * 2**20),
        cost_estimate=cost(12),
    )
    return lambda *args: run(*args)[:6]


def on_device(object_tiles, probe_modes, offsets, amplitude):
    rows, cols = object_tiles.shape[2:]
    ext_rows = rows + 2 * HALO
    scans = offsets.shape[2]
    tile = object_tiles.reshape(PLANES, rows, cols)
    offset_pairs = jnp.swapaxes(offsets, 2, 3).reshape(2, scans)
    amp = amplitude.reshape(scans, WIN, WIN)
    flat = (2 * MODES * WIN, WIN)
    mats = jnp.asarray(matrices())
    devices = lax.axis_size("row") * lax.axis_size("col")

    north = moved(tile[:, rows - HALO :], "row", 1)
    south = moved(tile[:, :HALO], "row", -1)
    east_send, west_send = call(pack_kernel, [f32(rows, LANES)] * 2, 1)(tile)
    from_west = moved(east_send, "col", 1)
    from_east = moved(west_send, "col", -1)
    east_send, west_send = call(corner_kernel, [f32(2 * HALO, LANES)] * 2, 2)(north, south)
    west_corners = moved(east_send, "col", 1)
    east_corners = moved(west_send, "col", -1)

    ext = call(assemble_kernel, f32(PLANES, 3, ext_rows, LANES), 3, us=4)(tile, north, south)
    probe_grad, center, north_rim, south_rim, east_rim, west_rim = main_call(scans, rows, cols)(
        offset_pairs, ext, from_west, from_east, west_corners, east_corners, amp, probe_modes, mats
    )

    parts = lax.all_to_all(probe_grad.reshape(devices, -1, LANES), BOTH, 0, 0, tiled=True)
    rim_from_west = moved(east_rim, "col", 1)
    rim_from_east = moved(west_rim, "col", -1)
    from_south = moved(north_rim, "row", -1)
    from_north = moved(south_rim, "row", 1)
    share = call(share_kernel, f32(*parts.shape), 3)(parts, from_north, from_south)
    total = lax.all_to_all(share, BOTH, 0, 0, tiled=True)
    to_north, to_south = call(rim_corner_kernel, [f32(2 * HALO, LANES)] * 2, 2)(rim_from_west, rim_from_east)
    south_corners = moved(to_north, "row", -1)
    north_corners = moved(to_south, "row", 1)
    object_grad = call(object_kernel, f32(PLANES, rows, cols), 7)(
        center, from_north, from_south, rim_from_west, rim_from_east, north_corners, south_corners
    )
    probe_new = call(probe_kernel, f32(*flat), 2)(total.reshape(flat), probe_modes.reshape(flat))
    return object_grad.reshape(object_tiles.shape), probe_new.reshape(probe_modes.shape)


def solution(mesh):
    placed = (
        P(None, None, "row", "col"),
        P(),
        P("row", "col", None, None),
        P("row", "col", None, None, None),
    )
    return jax.shard_map(
        on_device,
        mesh=mesh,
        in_specs=placed,
        out_specs=(P(None, None, "row", "col"), P()),
        check_vma=False,
    )
```

time: 83.2 us -> 85.3 us (1.025)
  the two profiles are of different devices: /device:TPU:1 before, /device:TPU:0 now
where the time goes in v4:
time: 85.3 us; the launch traced here: 85 us
  starting transfers between devices  44.5 us (52%)
  waiting for transfers between devices  23 us (27%)
  Pallas kernels  12.2 us (14%)
  local copies, waits for them, and re-layouts  4.54 us (5%)
    ppermute x12, starting transfers between devices, moved(): lax.ppermute(block, axis, [(i, (i + distance) % count) for i in range(cou...  28.8 us
    ppermute x12, waiting for transfers between devices, moved(): lax.ppermute(block, axis, [(i, (i + distance) % count) for i in range(cou...  23 us
    all_to_all x1, starting transfers between devices, on_device(): total = lax.all_to_all(share, BOTH, 0, 0, tiled=True)  9.12 us
    pallas_call x1, Pallas kernels, main_call(): return lambda *args: run(*args)[:6]  8.32 us
    all_to_all x1, starting transfers between devices, on_device(): lax.all_to_all(probe_grad.reshape(devices, -1, LANES), BOTH, 0, 0, tiled=...  6.61 us
    unnamed x12, local copies, waits for them, and re-layouts  3.55 us
  transfers between devices with their start and end apart: 14, of which 7 were waited for; matrix products, arithmetic and copies ran while one was open for 0% of the time, Pallas kernels for 2%

profile of v4, /device:TPU:0, one launch (start us, length us, event | category | flops | bytes accessed | tf_op | source)
XLA Modules:
  0.0 85.0 jit_solution(13972606244331850059)
XLA Ops:
  0.6 1.0 %fusion = (f32[4,32,256]{2,1,0:T(8,128)S(1)}, f32[4,32,256]{2,1,0:T(8,128)S(1)}) fusion(f32[4,256,256]{2,1,0:T(8,128)} %bitcast.11), kind=kLoop, calls=%fused_computation | loop fusion | bytes 524288 | tf_op jit(solution)/shard_map/slice | solution.py:381
  1.6 5.6 %collective-permute-start.1 = (f32[4,32,256]{2,1,0:T(8,128)S(1)}, f32[4,32,256]{2,1,0:T(8,128)S(1)}, u32[]{:S(2)}, u32[]{:S(2)}) collective-permute-start(f32[4,32,256]{2,1,0:T(8,128)S(1)} %get-tuple-element.26), channel_id=1, source_target_pairs={{0,112},{16,0},{32,16},{48,32},{64,48},{80,64},{96,80},{112,96},{1... | collective-permute-start | bytes 393224 | tf_op jit(solution)/shard_map/ppermute | solution.py:326
  7.3 0.0 collective-permute-start
  7.3 0.0 copy-start
  7.3 1.2 %copy-done = f32[2,2,256,256]{3,2,1,0:T(8,128)S(1)} copy-done((f32[2,2,256,256]{3,2,1,0:T(8,128)S(1)}, f32[2,2,256,256]{3,2,1,0:T(8,128)}, u32[]{:S(2)}) %copy-start) | copy-done | bytes 1048600
  8.5 0.3 shard_map.69
  8.8 0.1 collective-permute-start.2
  8.8 3.8 %collective-permute-start.3 = (f32[256,128]{1,0:T(8,128)S(1)}, f32[256,128]{1,0:T(8,128)S(1)}, u32[]{:S(2)}, u32[]{:S(2)}) collective-permute-start(f32[256,128]{1,0:T(8,128)S(1)} %get-tuple-element.15), channel_id=1, source_target_pairs={{0,15},{1,0},{2,1},{3,2},{4,3},{5,4},{6,5},{7,6},{8,7},{9,8},{10,9... | collective-permute-start | bytes 393224 | tf_op jit(solution)/shard_map/ppermute | solution.py:326
  12.7 0.0 collective-permute-done.1.south_ref
  12.7 3.2 %collective-permute-done.north_ref = f32[4,32,256]{2,1,0:T(8,128)S(1)} collective-permute-done((f32[4,32,256]{2,1,0:T(8,128)S(1)}, f32[4,32,256]{2,1,0:T(8,128)S(1)}, u32[]{:S(2)}, u32[]{:S(2)}) %collective-permute-start) | collective-permute-done | bytes 131104 | tf_op jit(solution)/shard_map/ppermute | solution.py:326
  15.8 0.1 shard_map.70
  16.0 0.1 collective-permute-start.4
  16.0 3.8 %collective-permute-start.5 = (f32[64,128]{1,0:T(8,128)S(1)}, f32[64,128]{1,0:T(8,128)S(1)}, u32[]{:S(2)}, u32[]{:S(2)}) collective-permute-start(f32[64,128]{1,0:T(8,128)S(1)} %get-tuple-element.17), channel_id=1, source_target_pairs={{0,15},{1,0},{2,1},{3,2},{4,3},{5,4},{6,5},{7,6},{8,7},{9,8},{10,9... | collective-permute-start | bytes 98312 | tf_op jit(solution)/shard_map/ppermute | solution.py:326
  19.9 0.0 copy-start.1
  19.9 1.2 %copy-done.1 = f32[2,2,256,256]{3,2,1,0:T(8,128)S(1)} copy-done((f32[2,2,256,256]{3,2,1,0:T(8,128)S(1)}, f32[2,2,256,256]{3,2,1,0:T(8,128)}, u32[]{:S(2)}) %copy-start.1) | copy-done | bytes 1048600
  21.1 0.0 copy-start.2
  21.1 0.0 copy-start.3
  21.1 0.0 copy-start.4
  21.1 0.0 copy-start.5
  21.1 0.1 shard_map.68.ext_in
  21.2 0.0 collective-permute-done.2.from_west_ref
  21.2 0.0 collective-permute-done.3.from_east_ref
  21.2 0.2 collective-permute-done.4.west_corners_ref
  21.5 0.0 collective-permute-done.5.east_corners_ref
  21.5 0.7 copy-done.2
  22.1 0.0 copy-done.3
  22.2 0.0 copy-done.4
  22.2 0.4 copy-done.5
  22.6 8.3 %shard_map.71 = (f32[2,4,128,128]{3,2,1,0:T(8,128)}, f32[4,256,256]{2,1,0:T(8,128)S(1)}, f32[4,32,256]{2,1,0:T(8,128)S(1)}, f32[4,32,256]{2,1,0:T(8,128)S(1)}, f...) custom-call(s32[2,3]{1,0:T(2,128)S(1)} %bitcast.16, ...), custom_call_target="tpu_custom_call", output_to_operand_aliasing={{6}: (1, {})} | custom-call | flops 12000000000 | bytes 36000000 | tf_op jit(solution)/shard_map/pallas_call | solution.py:366
  30.9 6.6 %all-to-all-start = ((f32[128,8,128]{2,1,0:T(8,128)}), f32[128,8,128]{2,1,0:T(8,128)S(1)}, u32[]{:S(2)}, u32[]{:S(2)}) async-start(f32[128,8,128]{2,1,0:T(8,128)} %bitcast.5), calls=%async_computation | async-start | bytes 1048576 | tf_op jit(solution)/shard_map/all_to_all | solution.py:394
  37.5 2.5 %collective-permute-start.6 = (f32[4,32,256]{2,1,0:T(8,128)S(1)}, f32[4,32,256]{2,1,0:T(8,128)S(1)}, u32[]{:S(2)}, u32[]{:S(2)}) collective-permute-start(f32[4,32,256]{2,1,0:T(8,128)S(1)} %get-tuple-element.19), channel_id=1, source_target_pairs={{0,16},{16,32},{32,48},{48,64},{64,80},{80,96},{96,112},{112,0},{1... | collective-permute-start | bytes 393224 | tf_op jit(solution)/shard_map/ppermute | solution.py:326
  40.0 3.2 %collective-permute-start.7 = (f32[4,32,256]{2,1,0:T(8,128)S(1)}, f32[4,32,256]{2,1,0:T(8,128)S(1)}, u32[]{:S(2)}, u32[]{:S(2)}) collective-permute-start(f32[4,32,256]{2,1,0:T(8,128)S(1)} %get-tuple-element.20), channel_id=1, source_target_pairs={{0,112},{16,0},{32,16},{48,32},{64,48},{80,64},{96,80},{112,96},{1... | collective-permute-start | bytes 393224 | tf_op jit(solution)/shard_map/ppermute | solution.py:326
  43.2 8.2 %collective-permute-done.6.from_north_ref = f32[4,32,256]{2,1,0:T(8,128)S(1)} collective-permute-done((f32[4,32,256]{2,1,0:T(8,128)S(1)}, f32[4,32,256]{2,1,0:T(8,128)S(1)}, u32[]{:S(2)}, u32[]{:S(2)}) %collective-permute-start.6) | collective-permute-done | bytes 131104 | tf_op jit(solution)/shard_map/ppermute | solution.py:326
  51.4 0.1 collective-permute-done.7.from_south_ref
  51.5 0.0 all-to-all-done.parts_ref
  51.5 1.0 %shard_map.74 = f32[128,8,128]{2,1,0:T(8,128)} custom-call(f32[128,8,128]{2,1,0:T(8,128)S(1)} %all-to-all-done.parts_ref, f32[4,32,256]{2,1,0:T(8,128)S(1)} %collective-permute-done.6.from_north_ref, f32[4,32,256]{2,1,0:T(8,128)S(1)} %collective-permute-done.7.from_south_ref), custom_call_target="tpu_custom_call" | custom-call | tf_op jit(solution)/shard_map/pallas_call | solution.py:399
  52.5 9.1 %all-to-all-start.1 = ((f32[128,8,128]{2,1,0:T(8,128)}), f32[128,8,128]{2,1,0:T(8,128)S(1)}, u32[]{:S(2)}, u32[]{:S(2)}) async-start(f32[128,8,128]{2,1,0:T(8,128)} %shard_map.74), calls=%async_computation.1 | async-start | bytes 1048576 | tf_op jit(solution)/shard_map/all_to_all | solution.py:400
  61.6 0.1 collective-permute-start.8
  61.7 3.8 %collective-permute-start.9 = (f32[320,128]{1,0:T(8,128)S(1)}, f32[320,128]{1,0:T(8,128)S(1)}, u32[]{:S(2)}, u32[]{:S(2)}) collective-permute-start(f32[320,128]{1,0:T(8,128)S(1)} %get-tuple-element.22), channel_id=1, source_target_pairs={{0,15},{1,0},{2,1},{3,2},{4,3},{5,4},{6,5},{7,6},{8,7},{9,8},{10,9... | collective-permute-start | bytes 491528 | tf_op jit(solution)/shard_map/ppermute | solution.py:326
  65.6 9.0 %collective-permute-done.8.from_west_ref = f32[320,128]{1,0:T(8,128)S(1)} collective-permute-done((f32[320,128]{1,0:T(8,128)S(1)}, f32[320,128]{1,0:T(8,128)S(1)}, u32[]{:S(2)}, u32[]{:S(2)}) %collective-permute-start.8) | collective-permute-done | bytes 163872 | tf_op jit(solution)/shard_map/ppermute | solution.py:326
  74.6 0.0 collective-permute-done.9.from_east_ref
  74.6 2.6 %collective-permute-start.10 = (f32[64,128]{1,0:T(8,128)S(1)}, f32[64,128]{1,0:T(8,128)S(1)}, u32[]{:S(2)}, u32[]{:S(2)}) collective-permute-start(f32[64,128]{1,0:T(8,128)S(1)} %get-tuple-element.23), channel_id=1, source_target_pairs={{0,16},{16,32},{32,48},{48,64},{64,80},{80,96},{96,112},{112,0},{1... | collective-permute-start | bytes 98312 | tf_op jit(solution)/shard_map/ppermute | solution.py:326
  77.2 3.1 %collective-permute-start.11 = (f32[64,128]{1,0:T(8,128)S(1)}, f32[64,128]{1,0:T(8,128)S(1)}, u32[]{:S(2)}, u32[]{:S(2)}) collective-permute-start(f32[64,128]{1,0:T(8,128)S(1)} %get-tuple-element.24), channel_id=1, source_target_pairs={{0,112},{16,0},{32,16},{48,32},{64,48},{80,64},{96,80},{112,96},{1... | collective-permute-start | bytes 98312 | tf_op jit(solution)/shard_map/ppermute | solution.py:326
  80.3 1.9 %collective-permute-done.10.north_corners_ref = f32[64,128]{1,0:T(8,128)S(1)} collective-permute-done((f32[64,128]{1,0:T(8,128)S(1)}, f32[64,128]{1,0:T(8,128)S(1)}, u32[]{:S(2)}, u32[]{:S(2)}) %collective-permute-start.10) | collective-permute-done | bytes 32800 | tf_op jit(solution)/shard_map/ppermute | solution.py:326
  82.2 0.4 collective-permute-done.11.south_corners_ref
  82.6 1.3 %shard_map.73 = f32[4,256,256]{2,1,0:T(8,128)} custom-call(f32[4,256,256]{2,1,0:T(8,128)S(1)} %get-tuple-element.18.center_ref, f32[4,32,256]{2,1,0:T(8,128)S(1)} %collective-permute-done.6.from_north_ref, f32[4,32,256]{2,1,0:T(8,128)S(1)} %collective-permute-done.7.from_south_ref, f32[320,128]{1,0:T(8,128)S(1)} %collective-permute-done.8.from_west_ref, ...), custom_call_target="tpu_custom_call" | custom-call | tf_op jit(solution)/shard_map/pallas_call | solution.py:404
  83.9 0.0 all-to-all-done.1
  83.9 1.1 %shard_map.75 = f32[1024,128]{1,0:T(8,128)} custom-call(f32[1024,128]{1,0:T(8,128)S(1)} %bitcast.10, f32[1024,128]{1,0:T(8,128)S(1)} %bitcast.14), custom_call_target="tpu_custom_call" | custom-call | tf_op jit(solution)/shard_map/pallas_call | solution.py:407
  (1 shorter events, 0.0 us)
Async XLA Ops:
  1.6 11.1 %collective-permute-start.1 = (f32[4,32,256]{2,1,0:T(8,128)S(1)}, f32[4,32,256]{2,1,0:T(8,128)S(1)}, u32[]{:S(2)}, u32[]{:S(2)}) collective-permute-start(f32[4,32,256]{2,1,0:T(8,128)S(1)} %get-tuple-element.26), channel_id=1, source_target_pairs={{0,112},{16,0},{32,16},{48,32},{64,48},{80,64},{96,80},{112,96},{1... | collective-permute-start | bytes 393224 | tf_op jit(solution)/shard_map/ppermute | solution.py:326
  7.3 8.6 %collective-permute-start = (f32[4,32,256]{2,1,0:T(8,128)S(1)}, f32[4,32,256]{2,1,0:T(8,128)S(1)}, u32[]{:S(2)}, u32[]{:S(2)}) collective-permute-start(f32[4,32,256]{2,1,0:T(8,128)S(1)} %get-tuple-element.27), channel_id=1, source_target_pairs={{0,16},{16,32},{32,48},{48,64},{64,80},{80,96},{96,112},{112,0},{1... | collective-permute-start | bytes 393224 | tf_op jit(solution)/shard_map/ppermute | solution.py:326
  7.3 1.2 %copy-start = (f32[2,2,256,256]{3,2,1,0:T(8,128)S(1)}, f32[2,2,256,256]{3,2,1,0:T(8,128)}, u32[]{:S(2)}) copy-start(f32[2,2,256,256]{3,2,1,0:T(8,128)} %param.5) | copy-start | bytes 3145732
  8.8 12.5 %collective-permute-start.2 = (f32[256,128]{1,0:T(8,128)S(1)}, f32[256,128]{1,0:T(8,128)S(1)}, u32[]{:S(2)}, u32[]{:S(2)}) collective-permute-start(f32[256,128]{1,0:T(8,128)S(1)} %get-tuple-element.14), channel_id=1, source_target_pairs={{0,1},{1,2},{2,3},{3,4},{4,5},{5,6},{6,7},{7,8},{8,9},{9,10},{10,1... | collective-permute-start | bytes 393224 | tf_op jit(solution)/shard_map/ppermute | solution.py:326
  8.8 12.4 %collective-permute-start.3 = (f32[256,128]{1,0:T(8,128)S(1)}, f32[256,128]{1,0:T(8,128)S(1)}, u32[]{:S(2)}, u32[]{:S(2)}) collective-permute-start(f32[256,128]{1,0:T(8,128)S(1)} %get-tuple-element.15), channel_id=1, source_target_pairs={{0,15},{1,0},{2,1},{3,2},{4,3},{5,4},{6,5},{7,6},{8,7},{9,8},{10,9... | collective-permute-start | bytes 393224 | tf_op jit(solution)/shard_map/ppermute | solution.py:326
  16.0 5.5 %collective-permute-start.4 = (f32[64,128]{1,0:T(8,128)S(1)}, f32[64,128]{1,0:T(8,128)S(1)}, u32[]{:S(2)}, u32[]{:S(2)}) collective-permute-start(f32[64,128]{1,0:T(8,128)S(1)} %get-tuple-element.16), channel_id=1, source_target_pairs={{0,1},{1,2},{2,3},{3,4},{4,5},{5,6},{6,7},{7,8},{8,9},{9,10},{10,1... | collective-permute-start | bytes 98312 | tf_op jit(solution)/shard_map/ppermute | solution.py:326
  16.0 5.4 %collective-permute-start.5 = (f32[64,128]{1,0:T(8,128)S(1)}, f32[64,128]{1,0:T(8,128)S(1)}, u32[]{:S(2)}, u32[]{:S(2)}) collective-permute-start(f32[64,128]{1,0:T(8,128)S(1)} %get-tuple-element.17), channel_id=1, source_target_pairs={{0,15},{1,0},{2,1},{3,2},{4,3},{5,4},{6,5},{7,6},{8,7},{9,8},{10,9... | collective-permute-start | bytes 98312 | tf_op jit(solution)/shard_map/ppermute | solution.py:326
  19.9 1.2 %copy-start.1 = (f32[2,2,256,256]{3,2,1,0:T(8,128)S(1)}, f32[2,2,256,256]{3,2,1,0:T(8,128)}, u32[]{:S(2)}) copy-start(f32[2,2,256,256]{3,2,1,0:T(8,128)} %param.5) | copy-start | bytes 3145732
  21.1 1.0 %copy-start.2 = (f32[2,4,128,128]{3,2,1,0:T(8,128)S(1)}, f32[2,4,128,128]{3,2,1,0:T(8,128)}, u32[]{:S(2)}) copy-start(f32[2,4,128,128]{3,2,1,0:T(8,128)} %probe_ref.1) | copy-start | bytes 1572868
  21.1 1.1 %copy-start.3 = (f32[1,1,3,128,128]{4,3,2,1,0:T(8,128)S(1)}, f32[1,1,3,128,128]{4,3,2,1,0:T(8,128)}, u32[]{:S(2)}) copy-start(f32[1,1,3,128,128]{4,3,2,1,0:T(8,128)} %param.8) | copy-start | bytes 589828
  21.1 1.1 %copy-start.4 = (s32[1,1,3,2]{2,3,1,0:T(2,128)S(1)}, s32[1,1,3,2]{2,3,1,0:T(2,128)}, u32[]{:S(2)}) copy-start(s32[1,1,3,2]{2,3,1,0:T(2,128)} %param.7) | copy-start | bytes 76
  21.1 1.5 %copy-start.5 = (bf16[4,2,256,256]{3,2,1,0:T(8,128)(2,1)S(1)}, bf16[4,2,256,256]{3,2,1,0:T(8,128)(2,1)}, u32[]{:S(2)}) copy-start(bf16[4,2,256,256]{3,2,1,0:T(8,128)(2,1)} %constant.2.clone.mat_ref) | copy-start | bytes 3145732
  30.9 20.7 %all-to-all-start = ((f32[128,8,128]{2,1,0:T(8,128)}), f32[128,8,128]{2,1,0:T(8,128)S(1)}, u32[]{:S(2)}, u32[]{:S(2)}) async-start(f32[128,8,128]{2,1,0:T(8,128)} %bitcast.5), calls=%async_computation | async-start | bytes 1048576 | tf_op jit(solution)/shard_map/all_to_all | solution.py:394
  37.5 13.9 %collective-permute-start.6 = (f32[4,32,256]{2,1,0:T(8,128)S(1)}, f32[4,32,256]{2,1,0:T(8,128)S(1)}, u32[]{:S(2)}, u32[]{:S(2)}) collective-permute-start(f32[4,32,256]{2,1,0:T(8,128)S(1)} %get-tuple-element.19), channel_id=1, source_target_pairs={{0,16},{16,32},{32,48},{48,64},{64,80},{80,96},{96,112},{112,0},{1... | collective-permute-start | bytes 393224 | tf_op jit(solution)/shard_map/ppermute | solution.py:326
  40.0 11.5 %collective-permute-start.7 = (f32[4,32,256]{2,1,0:T(8,128)S(1)}, f32[4,32,256]{2,1,0:T(8,128)S(1)}, u32[]{:S(2)}, u32[]{:S(2)}) collective-permute-start(f32[4,32,256]{2,1,0:T(8,128)S(1)} %get-tuple-element.20), channel_id=1, source_target_pairs={{0,112},{16,0},{32,16},{48,32},{64,48},{80,64},{96,80},{112,96},{1... | collective-permute-start | bytes 393224 | tf_op jit(solution)/shard_map/ppermute | solution.py:326
  52.5 31.4 %all-to-all-start.1 = ((f32[128,8,128]{2,1,0:T(8,128)}), f32[128,8,128]{2,1,0:T(8,128)S(1)}, u32[]{:S(2)}, u32[]{:S(2)}) async-start(f32[128,8,128]{2,1,0:T(8,128)} %shard_map.74), calls=%async_computation.1 | async-start | bytes 1048576 | tf_op jit(solution)/shard_map/all_to_all | solution.py:400
  61.6 12.9 %collective-permute-start.8 = (f32[320,128]{1,0:T(8,128)S(1)}, f32[320,128]{1,0:T(8,128)S(1)}, u32[]{:S(2)}, u32[]{:S(2)}) collective-permute-start(f32[320,128]{1,0:T(8,128)S(1)} %get-tuple-element.21), channel_id=1, source_target_pairs={{0,1},{1,2},{2,3},{3,4},{4,5},{5,6},{6,7},{7,8},{8,9},{9,10},{10,1... | collective-permute-start | bytes 491528 | tf_op jit(solution)/shard_map/ppermute | solution.py:326
  61.7 12.8 %collective-permute-start.9 = (f32[320,128]{1,0:T(8,128)S(1)}, f32[320,128]{1,0:T(8,128)S(1)}, u32[]{:S(2)}, u32[]{:S(2)}) collective-permute-start(f32[320,128]{1,0:T(8,128)S(1)} %get-tuple-element.22), channel_id=1, source_target_pairs={{0,15},{1,0},{2,1},{3,2},{4,3},{5,4},{6,5},{7,6},{8,7},{9,8},{10,9... | collective-permute-start | bytes 491528 | tf_op jit(solution)/shard_map/ppermute | solution.py:326
  74.6 7.6 %collective-permute-start.10 = (f32[64,128]{1,0:T(8,128)S(1)}, f32[64,128]{1,0:T(8,128)S(1)}, u32[]{:S(2)}, u32[]{:S(2)}) collective-permute-start(f32[64,128]{1,0:T(8,128)S(1)} %get-tuple-element.23), channel_id=1, source_target_pairs={{0,16},{16,32},{32,48},{48,64},{64,80},{80,96},{96,112},{112,0},{1... | collective-permute-start | bytes 98312 | tf_op jit(solution)/shard_map/ppermute | solution.py:326
  77.2 5.4 %collective-permute-start.11 = (f32[64,128]{1,0:T(8,128)S(1)}, f32[64,128]{1,0:T(8,128)S(1)}, u32[]{:S(2)}, u32[]{:S(2)}) collective-permute-start(f32[64,128]{1,0:T(8,128)S(1)} %get-tuple-element.24), channel_id=1, source_target_pairs={{0,112},{16,0},{32,16},{48,32},{64,48},{80,64},{96,80},{112,96},{1... | collective-permute-start | bytes 98312 | tf_op jit(solution)/shard_map/ppermute | solution.py:326

commit v5 on v4

--- a/solution.py
+++ b/solution.py
@@ -276,8 +276,8 @@
         to_south_ref[k * HALO : (k + 1) * HALO, :] = ref[ref.shape[0] - HALO :, :]
 
 
-def share_kernel(parts_ref, from_north_ref, from_south_ref, share_ref):
-    del from_north_ref, from_south_ref
+def share_kernel(parts_ref, *refs):
+    share_ref = refs[-1]
     share_ref[...] = jnp.broadcast_to(jnp.sum(parts_ref[...], axis=0)[None], share_ref.shape)
 
 
@@ -379,10 +379,10 @@
 
     north = moved(tile[:, rows - HALO :], "row", 1)
     south = moved(tile[:, :HALO], "row", -1)
-    east_send, west_send = call(pack_kernel, [f32(rows, LANES)] * 2, 1)(tile)
+    east_send, west_send = call(pack_kernel, [f32(rows, LANES)] * 2, 1, us=1)(tile)
     from_west = moved(east_send, "col", 1)
     from_east = moved(west_send, "col", -1)
-    east_send, west_send = call(corner_kernel, [f32(2 * HALO, LANES)] * 2, 2)(north, south)
+    east_send, west_send = call(corner_kernel, [f32(2 * HALO, LANES)] * 2, 2, us=1)(north, south)
     west_corners = moved(east_send, "col", 1)
     east_corners = moved(west_send, "col", -1)
 
@@ -396,7 +396,9 @@
     rim_from_east = moved(west_rim, "col", -1)
     from_south = moved(north_rim, "row", -1)
     from_north = moved(south_rim, "row", 1)
-    share = call(share_kernel, f32(*parts.shape), 3)(parts, from_north, from_south)
+    share = call(share_kernel, f32(*parts.shape), 5)(
+        parts, rim_from_west, rim_from_east, from_north, from_south
+    )
     total = lax.all_to_all(share, BOTH, 0, 0, tiled=True)
     to_north, to_south = call(rim_corner_kernel, [f32(2 * HALO, LANES)] * 2, 2)(rim_from_west, rim_from_east)
     south_corners = moved(to_north, "row", -1)

time: 85.3 us -> 81.2 us (0.952)
  the two profiles are of different devices: /device:TPU:0 before, /device:TPU:1 now
where the time goes in v5:
time: 81.2 us; the launch traced here: 80.9 us
  starting transfers between devices  39.2 us (48%)
  waiting for transfers between devices  26.5 us (33%)
  Pallas kernels  12.2 us (15%)
  local copies, waits for them, and re-layouts  2.24 us (3%)
    ppermute x12, waiting for transfers between devices, moved(): lax.ppermute(block, axis, [(i, (i + distance) % count) for i in range(cou...  25.1 us
    ppermute x12, starting transfers between devices, moved(): lax.ppermute(block, axis, [(i, (i + distance) % count) for i in range(cou...  21.8 us
    all_to_all x1, starting transfers between devices, on_device(): total = lax.all_to_all(share, BOTH, 0, 0, tiled=True)  8.92 us
    all_to_all x1, starting transfers between devices, on_device(): lax.all_to_all(probe_grad.reshape(devices, -1, LANES), BOTH, 0, 0, tiled=...  8.52 us
    pallas_call x1, Pallas kernels, main_call(): return lambda *args: run(*args)[:6]  8.32 us
  transfers between devices with their start and end apart: 14, of which 7 were waited for; matrix products, arithmetic and copies ran while one was open for 0% of the time, Pallas kernels for 2%

profile of v5, /device:TPU:1, one launch (start us, length us, event | category | flops | bytes accessed | tf_op | source)
XLA Modules:
  0.0 80.9 jit_solution(6459417421272056993)
XLA Ops:
  0.6 1.0 %fusion = (f32[4,32,256]{2,1,0:T(8,128)S(1)}, f32[4,32,256]{2,1,0:T(8,128)S(1)}) fusion(f32[4,256,256]{2,1,0:T(8,128)} %bitcast.12), kind=kLoop, calls=%fused_computation | loop fusion | bytes 524288 | tf_op jit(solution)/shard_map/slice | solution.py:381
  1.6 6.1 %collective-permute-start.1 = (f32[4,32,256]{2,1,0:T(8,128)S(1)}, f32[4,32,256]{2,1,0:T(8,128)S(1)}, u32[]{:S(2)}, u32[]{:S(2)}) collective-permute-start(f32[4,32,256]{2,1,0:T(8,128)S(1)} %get-tuple-element.26), channel_id=1, source_target_pairs={{0,112},{16,0},{32,16},{48,32},{64,48},{80,64},{96,80},{112,96},{1... | collective-permute-start | bytes 393224 | tf_op jit(solution)/shard_map/ppermute | solution.py:326
  7.7 0.0 collective-permute-start
  7.7 0.0 copy-start.1
  7.7 1.2 %copy-done.1 = f32[2,2,256,256]{3,2,1,0:T(8,128)S(1)} copy-done((f32[2,2,256,256]{3,2,1,0:T(8,128)S(1)}, f32[2,2,256,256]{3,2,1,0:T(8,128)}, u32[]{:S(2)}) %copy-start.1) | copy-done | bytes 1048600
  8.9 0.3 shard_map.69
  9.2 0.0 copy-start.2
  9.2 1.2 %collective-permute-start.2 = (f32[256,128]{1,0:T(8,128)S(1)}, f32[256,128]{1,0:T(8,128)S(1)}, u32[]{:S(2)}, u32[]{:S(2)}) collective-permute-start(f32[256,128]{1,0:T(8,128)S(1)} %get-tuple-element.14), channel_id=1, source_target_pairs={{0,1},{1,2},{2,3},{3,4},{4,5},{5,6},{6,7},{7,8},{8,9},{9,10},{10,1... | collective-permute-start | bytes 393224 | tf_op jit(solution)/shard_map/ppermute | solution.py:326
  10.5 0.0 collective-permute-start.3
  10.5 0.0 collective-permute-done.1.south_ref
  10.5 4.7 %collective-permute-done.north_ref = f32[4,32,256]{2,1,0:T(8,128)S(1)} collective-permute-done((f32[4,32,256]{2,1,0:T(8,128)S(1)}, f32[4,32,256]{2,1,0:T(8,128)S(1)}, u32[]{:S(2)}, u32[]{:S(2)}) %collective-permute-start) | collective-permute-done | bytes 131104 | tf_op jit(solution)/shard_map/ppermute | solution.py:326
  15.2 0.1 shard_map.70
  15.3 2.4 %collective-permute-start.4 = (f32[64,128]{1,0:T(8,128)S(1)}, f32[64,128]{1,0:T(8,128)S(1)}, u32[]{:S(2)}, u32[]{:S(2)}) collective-permute-start(f32[64,128]{1,0:T(8,128)S(1)} %get-tuple-element.16), channel_id=1, source_target_pairs={{0,1},{1,2},{2,3},{3,4},{4,5},{5,6},{6,7},{7,8},{8,9},{9,10},{10,1... | collective-permute-start | bytes 98312 | tf_op jit(solution)/shard_map/ppermute | solution.py:326
  17.6 0.0 copy-start
  17.6 0.0 copy-start.3
  17.7 0.0 copy-start.4
  17.7 0.0 copy-start.5
  17.7 0.1 collective-permute-start.5
  17.7 0.0 copy-done.2
  17.8 0.1 shard_map.68.ext_in
  17.8 0.0 collective-permute-done.2.from_west_ref
  17.9 0.0 collective-permute-done.3.from_east_ref
  17.9 0.8 collective-permute-done.4.west_corners_ref
  18.7 2.4 %collective-permute-done.5.east_corners_ref = f32[64,128]{1,0:T(8,128)S(1)} collective-permute-done((f32[64,128]{1,0:T(8,128)S(1)}, f32[64,128]{1,0:T(8,128)S(1)}, u32[]{:S(2)}, u32[]{:S(2)}) %collective-permute-start.5) | collective-permute-done | bytes 32800 | tf_op jit(solution)/shard_map/ppermute | solution.py:326
  21.1 0.0 copy-done
  21.1 0.0 copy-done.3
  21.1 0.0 copy-done.4
  21.1 0.0 copy-done.5
  21.1 8.3 %shard_map.71 = (f32[2,4,128,128]{3,2,1,0:T(8,128)}, f32[4,256,256]{2,1,0:T(8,128)S(1)}, f32[4,32,256]{2,1,0:T(8,128)S(1)}, f32[4,32,256]{2,1,0:T(8,128)S(1)}, f...) custom-call(s32[2,3]{1,0:T(2,128)S(1)} %bitcast.16, ...), custom_call_target="tpu_custom_call", output_to_operand_aliasing={{6}: (1, {})} | custom-call | flops 12000000000 | bytes 36000000 | tf_op jit(solution)/shard_map/pallas_call | solution.py:366
  29.4 8.5 %all-to-all-start = ((f32[128,8,128]{2,1,0:T(8,128)}), f32[128,8,128]{2,1,0:T(8,128)S(1)}, u32[]{:S(2)}, u32[]{:S(2)}) async-start(f32[128,8,128]{2,1,0:T(8,128)} %bitcast.5), calls=%async_computation | async-start | bytes 1048576 | tf_op jit(solution)/shard_map/all_to_all | solution.py:394
  37.9 1.7 %collective-permute-start.8 = (f32[320,128]{1,0:T(8,128)S(1)}, f32[320,128]{1,0:T(8,128)S(1)}, u32[]{:S(2)}, u32[]{:S(2)}) collective-permute-start(f32[320,128]{1,0:T(8,128)S(1)} %get-tuple-element.21), channel_id=1, source_target_pairs={{0,1},{1,2},{2,3},{3,4},{4,5},{5,6},{6,7},{7,8},{8,9},{9,10},{10,1... | collective-permute-start | bytes 491528 | tf_op jit(solution)/shard_map/ppermute | solution.py:326
  39.6 0.0 collective-permute-start.9
  39.6 2.4 %collective-permute-start.6 = (f32[4,32,256]{2,1,0:T(8,128)S(1)}, f32[4,32,256]{2,1,0:T(8,128)S(1)}, u32[]{:S(2)}, u32[]{:S(2)}) collective-permute-start(f32[4,32,256]{2,1,0:T(8,128)S(1)} %get-tuple-element.19), channel_id=1, source_target_pairs={{0,16},{16,32},{32,48},{48,64},{64,80},{80,96},{96,112},{112,0},{1... | collective-permute-start | bytes 393224 | tf_op jit(solution)/shard_map/ppermute | solution.py:326
  42.0 2.7 %collective-permute-start.7 = (f32[4,32,256]{2,1,0:T(8,128)S(1)}, f32[4,32,256]{2,1,0:T(8,128)S(1)}, u32[]{:S(2)}, u32[]{:S(2)}) collective-permute-start(f32[4,32,256]{2,1,0:T(8,128)S(1)} %get-tuple-element.20), channel_id=1, source_target_pairs={{0,112},{16,0},{32,16},{48,32},{64,48},{80,64},{96,80},{112,96},{1... | collective-permute-start | bytes 393224 | tf_op jit(solution)/shard_map/ppermute | solution.py:326
  44.7 10.3 %collective-permute-done.6.from_north_ref.refs_2_ = f32[4,32,256]{2,1,0:T(8,128)S(1)} collective-permute-done((f32[4,32,256]{2,1,0:T(8,128)S(1)}, f32[4,32,256]{2,1,0:T(8,128)S(1)}, u32[]{:S(2)}, u32[]{:S(2)}) %collective-permute-start.6) | collective-permute-done | bytes 131104 | tf_op jit(solution)/shard_map/ppermute | solution.py:326
  55.1 0.6 collective-permute-done.7.from_south_ref.refs_3_
  55.7 0.0 collective-permute-done.8.from_west_ref.refs_0_
  55.7 0.0 collective-permute-done.9.from_east_ref.refs_1_
  55.7 0.0 all-to-all-done.parts_ref
  55.7 1.0 %shard_map.74 = f32[128,8,128]{2,1,0:T(8,128)} custom-call(f32[128,8,128]{2,1,0:T(8,128)S(1)} %all-to-all-done.parts_ref, f32[320,128]{1,0:T(8,128)S(1)} %collective-permute-done.8.from_west_ref.refs_0_, f32[320,128]{1,0:T(8,128)S(1)} %collective-permute-done.9.from_east_ref.refs_1_, f32[4,32,256]{2,1,0:T(8,128)S(1)} %collective-permute-done.6.from_north_ref.refs_2_, ...), custom_call_target="tpu_custom_call" | custom-call | tf_op jit(solution)/shard_map/pallas_call | solution.py:399
  56.7 8.9 %all-to-all-start.1 = ((f32[128,8,128]{2,1,0:T(8,128)}), f32[128,8,128]{2,1,0:T(8,128)S(1)}, u32[]{:S(2)}, u32[]{:S(2)}) async-start(f32[128,8,128]{2,1,0:T(8,128)} %shard_map.74), calls=%async_computation.1 | async-start | bytes 1048576 | tf_op jit(solution)/shard_map/all_to_all | solution.py:402
  65.6 3.0 %collective-permute-start.10 = (f32[64,128]{1,0:T(8,128)S(1)}, f32[64,128]{1,0:T(8,128)S(1)}, u32[]{:S(2)}, u32[]{:S(2)}) collective-permute-start(f32[64,128]{1,0:T(8,128)S(1)} %get-tuple-element.23), channel_id=1, source_target_pairs={{0,16},{16,32},{32,48},{48,64},{64,80},{80,96},{96,112},{112,0},{1... | collective-permute-start | bytes 98312 | tf_op jit(solution)/shard_map/ppermute | solution.py:326
  68.6 2.3 %collective-permute-start.11 = (f32[64,128]{1,0:T(8,128)S(1)}, f32[64,128]{1,0:T(8,128)S(1)}, u32[]{:S(2)}, u32[]{:S(2)}) collective-permute-start(f32[64,128]{1,0:T(8,128)S(1)} %get-tuple-element.24), channel_id=1, source_target_pairs={{0,112},{16,0},{32,16},{48,32},{64,48},{80,64},{96,80},{112,96},{1... | collective-permute-start | bytes 98312 | tf_op jit(solution)/shard_map/ppermute | solution.py:326
  70.8 6.3 %collective-permute-done.10.north_corners_ref = f32[64,128]{1,0:T(8,128)S(1)} collective-permute-done((f32[64,128]{1,0:T(8,128)S(1)}, f32[64,128]{1,0:T(8,128)S(1)}, u32[]{:S(2)}, u32[]{:S(2)}) %collective-permute-start.10) | collective-permute-done | bytes 32800 | tf_op jit(solution)/shard_map/ppermute | solution.py:326
  77.1 0.0 collective-permute-done.11.south_corners_ref
  77.1 1.3 %shard_map.73 = f32[4,256,256]{2,1,0:T(8,128)} custom-call(f32[4,256,256]{2,1,0:T(8,128)S(1)} %get-tuple-element.18.center_ref, f32[4,32,256]{2,1,0:T(8,128)S(1)} %collective-permute-done.6.from_north_ref.refs_2_, f32[4,32,256]{2,1,0:T(8,128)S(1)} %collective-permute-done.7.from_south_ref.refs_3_, ...), custom_call_target="tpu_custom_call" | custom-call | tf_op jit(solution)/shard_map/pallas_call | solution.py:406
  78.4 1.4 %all-to-all-done.1 = f32[128,8,128]{2,1,0:T(8,128)S(1)} async-done(((f32[128,8,128]{2,1,0:T(8,128)}), f32[128,8,128]{2,1,0:T(8,128)S(1)}, u32[]{:S(2)}, u32[]{:S(2)}) %all-to-all-start.1) | async-done | bytes 524320 | tf_op jit(solution)/shard_map/all_to_all | solution.py:402
  79.8 1.1 %shard_map.75 = f32[1024,128]{1,0:T(8,128)} custom-call(f32[1024,128]{1,0:T(8,128)S(1)} %bitcast.10, f32[1024,128]{1,0:T(8,128)S(1)} %bitcast.11), custom_call_target="tpu_custom_call" | custom-call | tf_op jit(solution)/shard_map/pallas_call | solution.py:409
  (1 shorter events, 0.0 us)
Async XLA Ops:
  1.6 8.8 %collective-permute-start.1 = (f32[4,32,256]{2,1,0:T(8,128)S(1)}, f32[4,32,256]{2,1,0:T(8,128)S(1)}, u32[]{:S(2)}, u32[]{:S(2)}) collective-permute-start(f32[4,32,256]{2,1,0:T(8,128)S(1)} %get-tuple-element.26), channel_id=1, source_target_pairs={{0,112},{16,0},{32,16},{48,32},{64,48},{80,64},{96,80},{112,96},{1... | collective-permute-start | bytes 393224 | tf_op jit(solution)/shard_map/ppermute | solution.py:326
  7.7 7.4 %collective-permute-start = (f32[4,32,256]{2,1,0:T(8,128)S(1)}, f32[4,32,256]{2,1,0:T(8,128)S(1)}, u32[]{:S(2)}, u32[]{:S(2)}) collective-permute-start(f32[4,32,256]{2,1,0:T(8,128)S(1)} %get-tuple-element.27), channel_id=1, source_target_pairs={{0,16},{16,32},{32,48},{48,64},{64,80},{80,96},{96,112},{112,0},{1... | collective-permute-start | bytes 393224 | tf_op jit(solution)/shard_map/ppermute | solution.py:326
  7.7 1.2 %copy-start.1 = (f32[2,2,256,256]{3,2,1,0:T(8,128)S(1)}, f32[2,2,256,256]{3,2,1,0:T(8,128)}, u32[]{:S(2)}) copy-start(f32[2,2,256,256]{3,2,1,0:T(8,128)} %param.5) | copy-start | bytes 3145732
  9.2 8.5 %copy-start.2 = (f32[2,2,256,256]{3,2,1,0:T(8,128)S(1)}, f32[2,2,256,256]{3,2,1,0:T(8,128)}, u32[]{:S(2)}) copy-start(f32[2,2,256,256]{3,2,1,0:T(8,128)} %param.5) | copy-start | bytes 3145732
  9.2 8.6 %collective-permute-start.2 = (f32[256,128]{1,0:T(8,128)S(1)}, f32[256,128]{1,0:T(8,128)S(1)}, u32[]{:S(2)}, u32[]{:S(2)}) collective-permute-start(f32[256,128]{1,0:T(8,128)S(1)} %get-tuple-element.14), channel_id=1, source_target_pairs={{0,1},{1,2},{2,3},{3,4},{4,5},{5,6},{6,7},{7,8},{8,9},{9,10},{10,1... | collective-permute-start | bytes 393224 | tf_op jit(solution)/shard_map/ppermute | solution.py:326
  10.5 7.4 %collective-permute-start.3 = (f32[256,128]{1,0:T(8,128)S(1)}, f32[256,128]{1,0:T(8,128)S(1)}, u32[]{:S(2)}, u32[]{:S(2)}) collective-permute-start(f32[256,128]{1,0:T(8,128)S(1)} %get-tuple-element.15), channel_id=1, source_target_pairs={{0,15},{1,0},{2,1},{3,2},{4,3},{5,4},{6,5},{7,6},{8,7},{9,8},{10,9... | collective-permute-start | bytes 393224 | tf_op jit(solution)/shard_map/ppermute | solution.py:326
  15.3 3.4 %collective-permute-start.4 = (f32[64,128]{1,0:T(8,128)S(1)}, f32[64,128]{1,0:T(8,128)S(1)}, u32[]{:S(2)}, u32[]{:S(2)}) collective-permute-start(f32[64,128]{1,0:T(8,128)S(1)} %get-tuple-element.16), channel_id=1, source_target_pairs={{0,1},{1,2},{2,3},{3,4},{4,5},{5,6},{6,7},{7,8},{8,9},{9,10},{10,1... | collective-permute-start | bytes 98312 | tf_op jit(solution)/shard_map/ppermute | solution.py:326
  17.6 3.4 %copy-start = (f32[2,4,128,128]{3,2,1,0:T(8,128)S(1)}, f32[2,4,128,128]{3,2,1,0:T(8,128)}, u32[]{:S(2)}) copy-start(f32[2,4,128,128]{3,2,1,0:T(8,128)} %probe_ref.1) | copy-start | bytes 1572868
  17.6 3.4 %copy-start.3 = (f32[1,1,3,128,128]{4,3,2,1,0:T(8,128)S(1)}, f32[1,1,3,128,128]{4,3,2,1,0:T(8,128)}, u32[]{:S(2)}) copy-start(f32[1,1,3,128,128]{4,3,2,1,0:T(8,128)} %param.8) | copy-start | bytes 589828
  17.7 3.4 %copy-start.4 = (s32[1,1,3,2]{2,3,1,0:T(2,128)S(1)}, s32[1,1,3,2]{2,3,1,0:T(2,128)}, u32[]{:S(2)}) copy-start(s32[1,1,3,2]{2,3,1,0:T(2,128)} %param.7) | copy-start | bytes 76
  17.7 3.4 %copy-start.5 = (bf16[4,2,256,256]{3,2,1,0:T(8,128)(2,1)S(1)}, bf16[4,2,256,256]{3,2,1,0:T(8,128)(2,1)}, u32[]{:S(2)}) copy-start(bf16[4,2,256,256]{3,2,1,0:T(8,128)(2,1)} %constant.2.clone.mat_ref) | copy-start | bytes 3145732
  17.7 3.4 %collective-permute-start.5 = (f32[64,128]{1,0:T(8,128)S(1)}, f32[64,128]{1,0:T(8,128)S(1)}, u32[]{:S(2)}, u32[]{:S(2)}) collective-permute-start(f32[64,128]{1,0:T(8,128)S(1)} %get-tuple-element.17), channel_id=1, source_target_pairs={{0,15},{1,0},{2,1},{3,2},{4,3},{5,4},{6,5},{7,6},{8,7},{9,8},{10,9... | collective-permute-start | bytes 98312 | tf_op jit(solution)/shard_map/ppermute | solution.py:326
  29.4 26.3 %all-to-all-start = ((f32[128,8,128]{2,1,0:T(8,128)}), f32[128,8,128]{2,1,0:T(8,128)S(1)}, u32[]{:S(2)}, u32[]{:S(2)}) async-start(f32[128,8,128]{2,1,0:T(8,128)} %bitcast.5), calls=%async_computation | async-start | bytes 1048576 | tf_op jit(solution)/shard_map/all_to_all | solution.py:394
  37.9 17.7 %collective-permute-start.8 = (f32[320,128]{1,0:T(8,128)S(1)}, f32[320,128]{1,0:T(8,128)S(1)}, u32[]{:S(2)}, u32[]{:S(2)}) collective-permute-start(f32[320,128]{1,0:T(8,128)S(1)} %get-tuple-element.21), channel_id=1, source_target_pairs={{0,1},{1,2},{2,3},{3,4},{4,5},{5,6},{6,7},{7,8},{8,9},{9,10},{10,1... | collective-permute-start | bytes 491528 | tf_op jit(solution)/shard_map/ppermute | solution.py:326
  39.6 16.0 %collective-permute-start.9 = (f32[320,128]{1,0:T(8,128)S(1)}, f32[320,128]{1,0:T(8,128)S(1)}, u32[]{:S(2)}, u32[]{:S(2)}) collective-permute-start(f32[320,128]{1,0:T(8,128)S(1)} %get-tuple-element.22), channel_id=1, source_target_pairs={{0,15},{1,0},{2,1},{3,2},{4,3},{5,4},{6,5},{7,6},{8,7},{9,8},{10,9... | collective-permute-start | bytes 491528 | tf_op jit(solution)/shard_map/ppermute | solution.py:326
  39.6 15.4 %collective-permute-start.6 = (f32[4,32,256]{2,1,0:T(8,128)S(1)}, f32[4,32,256]{2,1,0:T(8,128)S(1)}, u32[]{:S(2)}, u32[]{:S(2)}) collective-permute-start(f32[4,32,256]{2,1,0:T(8,128)S(1)} %get-tuple-element.19), channel_id=1, source_target_pairs={{0,16},{16,32},{32,48},{48,64},{64,80},{80,96},{96,112},{112,0},{1... | collective-permute-start | bytes 393224 | tf_op jit(solution)/shard_map/ppermute | solution.py:326
  42.0 13.6 %collective-permute-start.7 = (f32[4,32,256]{2,1,0:T(8,128)S(1)}, f32[4,32,256]{2,1,0:T(8,128)S(1)}, u32[]{:S(2)}, u32[]{:S(2)}) collective-permute-start(f32[4,32,256]{2,1,0:T(8,128)S(1)} %get-tuple-element.20), channel_id=1, source_target_pairs={{0,112},{16,0},{32,16},{48,32},{64,48},{80,64},{96,80},{112,96},{1... | collective-permute-start | bytes 393224 | tf_op jit(solution)/shard_map/ppermute | solution.py:326
  56.7 23.1 %all-to-all-start.1 = ((f32[128,8,128]{2,1,0:T(8,128)}), f32[128,8,128]{2,1,0:T(8,128)S(1)}, u32[]{:S(2)}, u32[]{:S(2)}) async-start(f32[128,8,128]{2,1,0:T(8,128)} %shard_map.74), calls=%async_computation.1 | async-start | bytes 1048576 | tf_op jit(solution)/shard_map/all_to_all | solution.py:402
  65.6 11.5 %collective-permute-start.10 = (f32[64,128]{1,0:T(8,128)S(1)}, f32[64,128]{1,0:T(8,128)S(1)}, u32[]{:S(2)}, u32[]{:S(2)}) collective-permute-start(f32[64,128]{1,0:T(8,128)S(1)} %get-tuple-element.23), channel_id=1, source_target_pairs={{0,16},{16,32},{32,48},{48,64},{64,80},{80,96},{96,112},{112,0},{1... | collective-permute-start | bytes 98312 | tf_op jit(solution)/shard_map/ppermute | solution.py:326
  68.6 8.5 %collective-permute-start.11 = (f32[64,128]{1,0:T(8,128)S(1)}, f32[64,128]{1,0:T(8,128)S(1)}, u32[]{:S(2)}, u32[]{:S(2)}) collective-permute-start(f32[64,128]{1,0:T(8,128)S(1)} %get-tuple-element.24), channel_id=1, source_target_pairs={{0,112},{16,0},{32,16},{48,32},{64,48},{80,64},{96,80},{112,96},{1... | collective-permute-start | bytes 98312 | tf_op jit(solution)/shard_map/ppermute | solution.py:326

commit v6 on v5

--- a/solution.py
+++ b/solution.py
@@ -396,11 +396,9 @@
     rim_from_east = moved(west_rim, "col", -1)
     from_south = moved(north_rim, "row", -1)
     from_north = moved(south_rim, "row", 1)
-    share = call(share_kernel, f32(*parts.shape), 5)(
-        parts, rim_from_west, rim_from_east, from_north, from_south
-    )
+    share = call(share_kernel, f32(*parts.shape), 1)(parts)
     total = lax.all_to_all(share, BOTH, 0, 0, tiled=True)
-    to_north, to_south = call(rim_corner_kernel, [f32(2 * HALO, LANES)] * 2, 2)(rim_from_west, rim_from_east)
+    to_north, to_south = call(rim_corner_kernel, [f32(2 * HALO, LANES)] * 2, 2, us=20)(rim_from_west, rim_from_east)
     south_corners = moved(to_north, "row", -1)
     north_corners = moved(to_south, "row", 1)
     object_grad = call(object_kernel, f32(PLANES, rows, cols), 7)(

time: 81.2 us -> 73.1 us (0.900)
  starting transfers between devices: 39.2 us -> 34.7 us
  waiting for transfers between devices: 26.5 us -> 22.9 us
    ppermute x12, waiting for transfers between devices: 25.1 us -> 14.1 us  [moved(): lax.ppermute(block, axis, [(i, (i + distance) % count) for i in range(cou...]
    all_to_all x1, waiting for transfers between devices: 0.01 us -> 7.41 us  [on_device(): lax.all_to_all(probe_grad.reshape(devices, -1, LANES), BOTH, 0, 0, tiled=...]
    all_to_all x1, starting transfers between devices: 8.92 us -> 4.29 us  [on_device(): total = lax.all_to_all(share, BOTH, 0, 0, tiled=True)]
  transfers between devices with their start and end apart: 14 -> 14, of which waited for: 7 -> 6; matrix products, arithmetic and copies ran while one was open for 0% -> 0% of each run, Pallas kernels for 2% -> 4%
where the time goes in v6:
time: 73.1 us; the launch traced here: 72.8 us
  starting transfers between devices  34.7 us (47%)
  waiting for transfers between devices  22.9 us (31%)
  Pallas kernels  12.2 us (17%)
  local copies, waits for them, and re-layouts  2.24 us (3%)
  between operations  0.76 us (1%)
    ppermute x12, starting transfers between devices, moved(): lax.ppermute(block, axis, [(i, (i + distance) % count) for i in range(cou...  21.9 us
    ppermute x12, waiting for transfers between devices, moved(): lax.ppermute(block, axis, [(i, (i + distance) % count) for i in range(cou...  14.1 us
    all_to_all x1, starting transfers between devices, on_device(): lax.all_to_all(probe_grad.reshape(devices, -1, LANES), BOTH, 0, 0, tiled=...  8.5 us
    pallas_call x1, Pallas kernels, main_call(): return lambda *args: run(*args)[:6]  8.33 us
    all_to_all x1, waiting for transfers between devices, on_device(): lax.all_to_all(probe_grad.reshape(devices, -1, LANES), BOTH, 0, 0, tiled=...  7.41 us
    all_to_all x1, starting transfers between devices, on_device(): total = lax.all_to_all(share, BOTH, 0, 0, tiled=True)  4.29 us
  transfers between devices with their start and end apart: 14, of which 6 were waited for; matrix products, arithmetic and copies ran while one was open for 0% of the time, Pallas kernels for 4%

profile of v6, /device:TPU:1, one launch (start us, length us, event | category | flops | bytes accessed | tf_op | source)
XLA Modules:
  0.0 72.8 jit_solution(342141155142061994)
XLA Ops:
  0.6 1.0 %fusion = (f32[4,32,256]{2,1,0:T(8,128)S(1)}, f32[4,32,256]{2,1,0:T(8,128)S(1)}) fusion(f32[4,256,256]{2,1,0:T(8,128)} %bitcast.12), kind=kLoop, calls=%fused_computation | loop fusion | bytes 524288 | tf_op jit(solution)/shard_map/slice | solution.py:381
  1.6 6.1 %collective-permute-start.1 = (f32[4,32,256]{2,1,0:T(8,128)S(1)}, f32[4,32,256]{2,1,0:T(8,128)S(1)}, u32[]{:S(2)}, u32[]{:S(2)}) collective-permute-start(f32[4,32,256]{2,1,0:T(8,128)S(1)} %get-tuple-element.26), channel_id=1, source_target_pairs={{0,112},{16,0},{32,16},{48,32},{64,48},{80,64},{96,80},{112,96},{1... | collective-permute-start | bytes 393224 | tf_op jit(solution)/shard_map/ppermute | solution.py:326
  7.7 0.0 collective-permute-start
  7.7 0.0 copy-start.1
  7.7 1.2 %copy-done.1 = f32[2,2,256,256]{3,2,1,0:T(8,128)S(1)} copy-done((f32[2,2,256,256]{3,2,1,0:T(8,128)S(1)}, f32[2,2,256,256]{3,2,1,0:T(8,128)}, u32[]{:S(2)}) %copy-start.1) | copy-done | bytes 1048600
  8.9 0.3 shard_map.69
  9.2 0.0 copy-start.2
  9.2 1.2 %collective-permute-start.2 = (f32[256,128]{1,0:T(8,128)S(1)}, f32[256,128]{1,0:T(8,128)S(1)}, u32[]{:S(2)}, u32[]{:S(2)}) collective-permute-start(f32[256,128]{1,0:T(8,128)S(1)} %get-tuple-element.14), channel_id=1, source_target_pairs={{0,1},{1,2},{2,3},{3,4},{4,5},{5,6},{6,7},{7,8},{8,9},{9,10},{10,1... | collective-permute-start | bytes 393224 | tf_op jit(solution)/shard_map/ppermute | solution.py:326
  10.5 0.0 collective-permute-start.3
  10.5 0.0 collective-permute-done.1.south_ref
  10.5 4.7 %collective-permute-done.north_ref = f32[4,32,256]{2,1,0:T(8,128)S(1)} collective-permute-done((f32[4,32,256]{2,1,0:T(8,128)S(1)}, f32[4,32,256]{2,1,0:T(8,128)S(1)}, u32[]{:S(2)}, u32[]{:S(2)}) %collective-permute-start) | collective-permute-done | bytes 131104 | tf_op jit(solution)/shard_map/ppermute | solution.py:326
  15.2 0.1 shard_map.70
  15.3 2.4 %collective-permute-start.4 = (f32[64,128]{1,0:T(8,128)S(1)}, f32[64,128]{1,0:T(8,128)S(1)}, u32[]{:S(2)}, u32[]{:S(2)}) collective-permute-start(f32[64,128]{1,0:T(8,128)S(1)} %get-tuple-element.16), channel_id=1, source_target_pairs={{0,1},{1,2},{2,3},{3,4},{4,5},{5,6},{6,7},{7,8},{8,9},{9,10},{10,1... | collective-permute-start | bytes 98312 | tf_op jit(solution)/shard_map/ppermute | solution.py:326
  17.6 0.0 copy-start
  17.6 0.0 copy-start.3
  17.7 0.0 copy-start.4
  17.7 0.0 copy-start.5
  17.7 0.1 collective-permute-start.5
  17.7 0.0 copy-done.2
  17.8 0.1 shard_map.68.ext_in
  17.8 0.0 collective-permute-done.2.from_west_ref
  17.9 0.0 collective-permute-done.3.from_east_ref
  17.9 0.8 %collective-permute-done.4.west_corners_ref = f32[64,128]{1,0:T(8,128)S(1)} collective-permute-done((f32[64,128]{1,0:T(8,128)S(1)}, f32[64,128]{1,0:T(8,128)S(1)}, u32[]{:S(2)}, u32[]{:S(2)}) %collective-permute-start.4) | collective-permute-done | bytes 32800 | tf_op jit(solution)/shard_map/ppermute | solution.py:326
  18.7 2.4 %collective-permute-done.5.east_corners_ref = f32[64,128]{1,0:T(8,128)S(1)} collective-permute-done((f32[64,128]{1,0:T(8,128)S(1)}, f32[64,128]{1,0:T(8,128)S(1)}, u32[]{:S(2)}, u32[]{:S(2)}) %collective-permute-start.5) | collective-permute-done | bytes 32800 | tf_op jit(solution)/shard_map/ppermute | solution.py:326
  21.1 0.0 copy-done
  21.1 0.0 copy-done.3
  21.1 0.0 copy-done.4
  21.1 0.0 copy-done.5
  21.1 8.3 %shard_map.71 = (f32[2,4,128,128]{3,2,1,0:T(8,128)}, f32[4,256,256]{2,1,0:T(8,128)S(1)}, f32[4,32,256]{2,1,0:T(8,128)S(1)}, f32[4,32,256]{2,1,0:T(8,128)S(1)}, f...) custom-call(s32[2,3]{1,0:T(2,128)S(1)} %bitcast.16, ...), custom_call_target="tpu_custom_call", output_to_operand_aliasing={{6}: (1, {})} | custom-call | flops 12000000000 | bytes 36000000 | tf_op jit(solution)/shard_map/pallas_call | solution.py:366
  29.4 8.5 %all-to-all-start = ((f32[128,8,128]{2,1,0:T(8,128)}), f32[128,8,128]{2,1,0:T(8,128)S(1)}, u32[]{:S(2)}, u32[]{:S(2)}) async-start(f32[128,8,128]{2,1,0:T(8,128)} %bitcast.5), calls=%async_computation | async-start | bytes 1048576 | tf_op jit(solution)/shard_map/all_to_all | solution.py:394
  37.9 1.7 %collective-permute-start.8 = (f32[320,128]{1,0:T(8,128)S(1)}, f32[320,128]{1,0:T(8,128)S(1)}, u32[]{:S(2)}, u32[]{:S(2)}) collective-permute-start(f32[320,128]{1,0:T(8,128)S(1)} %get-tuple-element.21), channel_id=1, source_target_pairs={{0,1},{1,2},{2,3},{3,4},{4,5},{5,6},{6,7},{7,8},{8,9},{9,10},{10,1... | collective-permute-start | bytes 491528 | tf_op jit(solution)/shard_map/ppermute | solution.py:326
  39.6 0.0 collective-permute-start.9
  39.6 2.4 %collective-permute-start.6 = (f32[4,32,256]{2,1,0:T(8,128)S(1)}, f32[4,32,256]{2,1,0:T(8,128)S(1)}, u32[]{:S(2)}, u32[]{:S(2)}) collective-permute-start(f32[4,32,256]{2,1,0:T(8,128)S(1)} %get-tuple-element.19), channel_id=1, source_target_pairs={{0,16},{16,32},{32,48},{48,64},{64,80},{80,96},{96,112},{112,0},{1... | collective-permute-start | bytes 393224 | tf_op jit(solution)/shard_map/ppermute | solution.py:326
  42.0 2.7 %collective-permute-start.7 = (f32[4,32,256]{2,1,0:T(8,128)S(1)}, f32[4,32,256]{2,1,0:T(8,128)S(1)}, u32[]{:S(2)}, u32[]{:S(2)}) collective-permute-start(f32[4,32,256]{2,1,0:T(8,128)S(1)} %get-tuple-element.20), channel_id=1, source_target_pairs={{0,112},{16,0},{32,16},{48,32},{64,48},{80,64},{96,80},{112,96},{1... | collective-permute-start | bytes 393224 | tf_op jit(solution)/shard_map/ppermute | solution.py:326
  44.7 7.4 %all-to-all-done.parts_ref = f32[128,8,128]{2,1,0:T(8,128)S(1)} async-done(((f32[128,8,128]{2,1,0:T(8,128)}), f32[128,8,128]{2,1,0:T(8,128)S(1)}, u32[]{:S(2)}, u32[]{:S(2)}) %all-to-all-start) | async-done | bytes 524320 | tf_op jit(solution)/shard_map/all_to_all | solution.py:394
  52.1 1.0 %shard_map.74 = f32[128,8,128]{2,1,0:T(8,128)} custom-call(f32[128,8,128]{2,1,0:T(8,128)S(1)} %all-to-all-done.parts_ref), custom_call_target="tpu_custom_call" | custom-call | tf_op jit(solution)/shard_map/pallas_call | solution.py:399
  53.1 4.3 %all-to-all-start.1 = ((f32[128,8,128]{2,1,0:T(8,128)}), f32[128,8,128]{2,1,0:T(8,128)S(1)}, u32[]{:S(2)}, u32[]{:S(2)}) async-start(f32[128,8,128]{2,1,0:T(8,128)} %shard_map.74), calls=%async_computation.1 | async-start | bytes 1048576 | tf_op jit(solution)/shard_map/all_to_all | solution.py:400
  57.4 0.0 collective-permute-done.8.from_west_ref
  57.4 0.0 collective-permute-done.9.from_east_ref
  57.4 3.0 %collective-permute-start.10 = (f32[64,128]{1,0:T(8,128)S(1)}, f32[64,128]{1,0:T(8,128)S(1)}, u32[]{:S(2)}, u32[]{:S(2)}) collective-permute-start(f32[64,128]{1,0:T(8,128)S(1)} %get-tuple-element.23), channel_id=1, source_target_pairs={{0,16},{16,32},{32,48},{48,64},{64,80},{80,96},{96,112},{112,0},{1... | collective-permute-start | bytes 98312 | tf_op jit(solution)/shard_map/ppermute | solution.py:326
  60.4 2.4 %collective-permute-start.11 = (f32[64,128]{1,0:T(8,128)S(1)}, f32[64,128]{1,0:T(8,128)S(1)}, u32[]{:S(2)}, u32[]{:S(2)}) collective-permute-start(f32[64,128]{1,0:T(8,128)S(1)} %get-tuple-element.24), channel_id=1, source_target_pairs={{0,112},{16,0},{32,16},{48,32},{64,48},{80,64},{96,80},{112,96},{1... | collective-permute-start | bytes 98312 | tf_op jit(solution)/shard_map/ppermute | solution.py:326
  62.8 0.0 collective-permute-done.6.from_north_ref
  62.8 0.0 collective-permute-done.7.from_south_ref
  62.8 6.2 %collective-permute-done.10.north_corners_ref = f32[64,128]{1,0:T(8,128)S(1)} collective-permute-done((f32[64,128]{1,0:T(8,128)S(1)}, f32[64,128]{1,0:T(8,128)S(1)}, u32[]{:S(2)}, u32[]{:S(2)}) %collective-permute-start.10) | collective-permute-done | bytes 32800 | tf_op jit(solution)/shard_map/ppermute | solution.py:326
  69.0 0.0 collective-permute-done.11.south_corners_ref
  69.0 1.3 %shard_map.73 = f32[4,256,256]{2,1,0:T(8,128)} custom-call(f32[4,256,256]{2,1,0:T(8,128)S(1)} %get-tuple-element.18.center_ref, f32[4,32,256]{2,1,0:T(8,128)S(1)} %collective-permute-done.6.from_north_ref, f32[4,32,256]{2,1,0:T(8,128)S(1)} %collective-permute-done.7.from_south_ref, f32[320,128]{1,0:T(8,128)S(1)} %collective-permute-done.8.from_west_ref, ...), custom_call_target="tpu_custom_call" | custom-call | tf_op jit(solution)/shard_map/pallas_call | solution.py:404
  70.3 1.4 %all-to-all-done.1 = f32[128,8,128]{2,1,0:T(8,128)S(1)} async-done(((f32[128,8,128]{2,1,0:T(8,128)}), f32[128,8,128]{2,1,0:T(8,128)S(1)}, u32[]{:S(2)}, u32[]{:S(2)}) %all-to-all-start.1) | async-done | bytes 524320 | tf_op jit(solution)/shard_map/all_to_all | solution.py:400
  71.7 1.1 %shard_map.75 = f32[1024,128]{1,0:T(8,128)} custom-call(f32[1024,128]{1,0:T(8,128)S(1)} %bitcast.10, f32[1024,128]{1,0:T(8,128)S(1)} %bitcast.11), custom_call_target="tpu_custom_call" | custom-call | tf_op jit(solution)/shard_map/pallas_call | solution.py:407
  (1 shorter events, 0.0 us)
Async XLA Ops:
  1.6 8.8 %collective-permute-start.1 = (f32[4,32,256]{2,1,0:T(8,128)S(1)}, f32[4,32,256]{2,1,0:T(8,128)S(1)}, u32[]{:S(2)}, u32[]{:S(2)}) collective-permute-start(f32[4,32,256]{2,1,0:T(8,128)S(1)} %get-tuple-element.26), channel_id=1, source_target_pairs={{0,112},{16,0},{32,16},{48,32},{64,48},{80,64},{96,80},{112,96},{1... | collective-permute-start | bytes 393224 | tf_op jit(solution)/shard_map/ppermute | solution.py:326
  7.7 7.4 %collective-permute-start = (f32[4,32,256]{2,1,0:T(8,128)S(1)}, f32[4,32,256]{2,1,0:T(8,128)S(1)}, u32[]{:S(2)}, u32[]{:S(2)}) collective-permute-start(f32[4,32,256]{2,1,0:T(8,128)S(1)} %get-tuple-element.27), channel_id=1, source_target_pairs={{0,16},{16,32},{32,48},{48,64},{64,80},{80,96},{96,112},{112,0},{1... | collective-permute-start | bytes 393224 | tf_op jit(solution)/shard_map/ppermute | solution.py:326
  7.7 1.2 %copy-start.1 = (f32[2,2,256,256]{3,2,1,0:T(8,128)S(1)}, f32[2,2,256,256]{3,2,1,0:T(8,128)}, u32[]{:S(2)}) copy-start(f32[2,2,256,256]{3,2,1,0:T(8,128)} %param.5) | copy-start | bytes 3145732
  9.2 8.5 %copy-start.2 = (f32[2,2,256,256]{3,2,1,0:T(8,128)S(1)}, f32[2,2,256,256]{3,2,1,0:T(8,128)}, u32[]{:S(2)}) copy-start(f32[2,2,256,256]{3,2,1,0:T(8,128)} %param.5) | copy-start | bytes 3145732
  9.2 8.6 %collective-permute-start.2 = (f32[256,128]{1,0:T(8,128)S(1)}, f32[256,128]{1,0:T(8,128)S(1)}, u32[]{:S(2)}, u32[]{:S(2)}) collective-permute-start(f32[256,128]{1,0:T(8,128)S(1)} %get-tuple-element.14), channel_id=1, source_target_pairs={{0,1},{1,2},{2,3},{3,4},{4,5},{5,6},{6,7},{7,8},{8,9},{9,10},{10,1... | collective-permute-start | bytes 393224 | tf_op jit(solution)/shard_map/ppermute | solution.py:326
  10.5 7.4 %collective-permute-start.3 = (f32[256,128]{1,0:T(8,128)S(1)}, f32[256,128]{1,0:T(8,128)S(1)}, u32[]{:S(2)}, u32[]{:S(2)}) collective-permute-start(f32[256,128]{1,0:T(8,128)S(1)} %get-tuple-element.15), channel_id=1, source_target_pairs={{0,15},{1,0},{2,1},{3,2},{4,3},{5,4},{6,5},{7,6},{8,7},{9,8},{10,9... | collective-permute-start | bytes 393224 | tf_op jit(solution)/shard_map/ppermute | solution.py:326
  15.3 3.4 %collective-permute-start.4 = (f32[64,128]{1,0:T(8,128)S(1)}, f32[64,128]{1,0:T(8,128)S(1)}, u32[]{:S(2)}, u32[]{:S(2)}) collective-permute-start(f32[64,128]{1,0:T(8,128)S(1)} %get-tuple-element.16), channel_id=1, source_target_pairs={{0,1},{1,2},{2,3},{3,4},{4,5},{5,6},{6,7},{7,8},{8,9},{9,10},{10,1... | collective-permute-start | bytes 98312 | tf_op jit(solution)/shard_map/ppermute | solution.py:326
  17.6 3.4 %copy-start = (f32[2,4,128,128]{3,2,1,0:T(8,128)S(1)}, f32[2,4,128,128]{3,2,1,0:T(8,128)}, u32[]{:S(2)}) copy-start(f32[2,4,128,128]{3,2,1,0:T(8,128)} %probe_ref.1) | copy-start | bytes 1572868
  17.6 3.4 %copy-start.3 = (f32[1,1,3,128,128]{4,3,2,1,0:T(8,128)S(1)}, f32[1,1,3,128,128]{4,3,2,1,0:T(8,128)}, u32[]{:S(2)}) copy-start(f32[1,1,3,128,128]{4,3,2,1,0:T(8,128)} %param.8) | copy-start | bytes 589828
  17.7 3.4 %copy-start.4 = (s32[1,1,3,2]{2,3,1,0:T(2,128)S(1)}, s32[1,1,3,2]{2,3,1,0:T(2,128)}, u32[]{:S(2)}) copy-start(s32[1,1,3,2]{2,3,1,0:T(2,128)} %param.7) | copy-start | bytes 76
  17.7 3.4 %copy-start.5 = (bf16[4,2,256,256]{3,2,1,0:T(8,128)(2,1)S(1)}, bf16[4,2,256,256]{3,2,1,0:T(8,128)(2,1)}, u32[]{:S(2)}) copy-start(bf16[4,2,256,256]{3,2,1,0:T(8,128)(2,1)} %constant.2.clone.mat_ref) | copy-start | bytes 3145732
  17.7 3.4 %collective-permute-start.5 = (f32[64,128]{1,0:T(8,128)S(1)}, f32[64,128]{1,0:T(8,128)S(1)}, u32[]{:S(2)}, u32[]{:S(2)}) collective-permute-start(f32[64,128]{1,0:T(8,128)S(1)} %get-tuple-element.17), channel_id=1, source_target_pairs={{0,15},{1,0},{2,1},{3,2},{4,3},{5,4},{6,5},{7,6},{8,7},{9,8},{10,9... | collective-permute-start | bytes 98312 | tf_op jit(solution)/shard_map/ppermute | solution.py:326
  29.4 22.7 %all-to-all-start = ((f32[128,8,128]{2,1,0:T(8,128)}), f32[128,8,128]{2,1,0:T(8,128)S(1)}, u32[]{:S(2)}, u32[]{:S(2)}) async-start(f32[128,8,128]{2,1,0:T(8,128)} %bitcast.5), calls=%async_computation | async-start | bytes 1048576 | tf_op jit(solution)/shard_map/all_to_all | solution.py:394
  37.9 19.5 %collective-permute-start.8 = (f32[320,128]{1,0:T(8,128)S(1)}, f32[320,128]{1,0:T(8,128)S(1)}, u32[]{:S(2)}, u32[]{:S(2)}) collective-permute-start(f32[320,128]{1,0:T(8,128)S(1)} %get-tuple-element.21), channel_id=1, source_target_pairs={{0,1},{1,2},{2,3},{3,4},{4,5},{5,6},{6,7},{7,8},{8,9},{9,10},{10,1... | collective-permute-start | bytes 491528 | tf_op jit(solution)/shard_map/ppermute | solution.py:326
  39.6 17.8 %collective-permute-start.9 = (f32[320,128]{1,0:T(8,128)S(1)}, f32[320,128]{1,0:T(8,128)S(1)}, u32[]{:S(2)}, u32[]{:S(2)}) collective-permute-start(f32[320,128]{1,0:T(8,128)S(1)} %get-tuple-element.22), channel_id=1, source_target_pairs={{0,15},{1,0},{2,1},{3,2},{4,3},{5,4},{6,5},{7,6},{8,7},{9,8},{10,9... | collective-permute-start | bytes 491528 | tf_op jit(solution)/shard_map/ppermute | solution.py:326
  39.6 23.2 %collective-permute-start.6 = (f32[4,32,256]{2,1,0:T(8,128)S(1)}, f32[4,32,256]{2,1,0:T(8,128)S(1)}, u32[]{:S(2)}, u32[]{:S(2)}) collective-permute-start(f32[4,32,256]{2,1,0:T(8,128)S(1)} %get-tuple-element.19), channel_id=1, source_target_pairs={{0,16},{16,32},{32,48},{48,64},{64,80},{80,96},{96,112},{112,0},{1... | collective-permute-start | bytes 393224 | tf_op jit(solution)/shard_map/ppermute | solution.py:326
  42.0 20.8 %collective-permute-start.7 = (f32[4,32,256]{2,1,0:T(8,128)S(1)}, f32[4,32,256]{2,1,0:T(8,128)S(1)}, u32[]{:S(2)}, u32[]{:S(2)}) collective-permute-start(f32[4,32,256]{2,1,0:T(8,128)S(1)} %get-tuple-element.20), channel_id=1, source_target_pairs={{0,112},{16,0},{32,16},{48,32},{64,48},{80,64},{96,80},{112,96},{1... | collective-permute-start | bytes 393224 | tf_op jit(solution)/shard_map/ppermute | solution.py:326
  53.1 18.6 %all-to-all-start.1 = ((f32[128,8,128]{2,1,0:T(8,128)}), f32[128,8,128]{2,1,0:T(8,128)S(1)}, u32[]{:S(2)}, u32[]{:S(2)}) async-start(f32[128,8,128]{2,1,0:T(8,128)} %shard_map.74), calls=%async_computation.1 | async-start | bytes 1048576 | tf_op jit(solution)/shard_map/all_to_all | solution.py:400
  57.4 11.6 %collective-permute-start.10 = (f32[64,128]{1,0:T(8,128)S(1)}, f32[64,128]{1,0:T(8,128)S(1)}, u32[]{:S(2)}, u32[]{:S(2)}) collective-permute-start(f32[64,128]{1,0:T(8,128)S(1)} %get-tuple-element.23), channel_id=1, source_target_pairs={{0,16},{16,32},{32,48},{48,64},{64,80},{80,96},{96,112},{112,0},{1... | collective-permute-start | bytes 98312 | tf_op jit(solution)/shard_map/ppermute | solution.py:326
  60.4 8.6 %collective-permute-start.11 = (f32[64,128]{1,0:T(8,128)S(1)}, f32[64,128]{1,0:T(8,128)S(1)}, u32[]{:S(2)}, u32[]{:S(2)}) collective-permute-start(f32[64,128]{1,0:T(8,128)S(1)} %get-tuple-element.24), channel_id=1, source_target_pairs={{0,112},{16,0},{32,16},{48,32},{64,48},{80,64},{96,80},{112,96},{1... | collective-permute-start | bytes 98312 | tf_op jit(solution)/shard_map/ppermute | solution.py:326

commit v7 on v6

--- a/solution.py
+++ b/solution.py
@@ -35,6 +35,7 @@
 C, C_CONJ, G, G_CONJ = range(4)
 BLOCKS = 2
 ROWS = 2 * WIN // BLOCKS
+CHUNKS = 4
 
 
 def lane_iota(rows):
@@ -281,36 +282,56 @@
     share_ref[...] = jnp.broadcast_to(jnp.sum(parts_ref[...], axis=0)[None], share_ref.shape)
 
 
+def from_sides(left, right, p):
+    lane = lane_iota(left.shape[0])
+    return (
+        jnp.where(lane < HALO, turned(left, -p * HALO), 0.0),
+        jnp.where(lane >= LANES - HALO, turned(right, (3 - p) * HALO), 0.0),
+    )
+
+
 def object_kernel(
-    center_ref, from_north_ref, from_south_ref, from_west_ref, from_east_ref, north_corners_ref, south_corners_ref,
-    object_ref,
+    center_ref, from_north_ref, from_south_ref, from_west_ref, from_east_ref, object_ref, north_ref, south_ref
 ):
     rows = center_ref.shape[1]
-
-    def rim(left, right, p):
-        lane = lane_iota(left.shape[0])
-        return (
-            jnp.where(lane < HALO, turned(left, -p * HALO), 0.0),
-            jnp.where(lane >= LANES - HALO, turned(right, (3 - p) * HALO), 0.0),
-        )
-
     for p in range(PLANES):
-        sides = rim(from_west_ref[HALO : HALO + rows, :], from_east_ref[HALO : HALO + rows, :], p)
-        north = rim(north_corners_ref[0:HALO, :], north_corners_ref[HALO:, :], p)
-        south = rim(south_corners_ref[0:HALO, :], south_corners_ref[HALO:, :], p)
+        sides = from_sides(from_west_ref[HALO : HALO + rows, :], from_east_ref[HALO : HALO + rows, :], p)
         for q in range(2):
             cols = slice(q * LANES, (q + 1) * LANES)
             whole = center_ref[p, :, cols] + sides[q]
-            object_ref[p, 0:HALO, cols] = whole[0:HALO] + from_north_ref[p, :, cols] + north[q]
-            object_ref[p, HALO : rows - HALO, cols] = whole[HALO : rows - HALO]
-            object_ref[p, rows - HALO :, cols] = whole[rows - HALO :] + from_south_ref[p, :, cols] + south[q]
-
-
-def probe_kernel(total_ref, probe_ref, probe_new_ref):
+            object_ref[p, :, cols] = whole
+            north_ref[p, :, cols] = whole[0:HALO] + from_north_ref[p, :, cols]
+            south_ref[p, :, cols] = whole[rows - HALO :] + from_south_ref[p, :, cols]
+
+
+def final_kernel(
+    object_in, north_ref, south_ref, north_corners_ref, south_corners_ref, total_ref, probe_ref,
+    object_ref, probe_new_ref, strips, steps, sem,
+):
+    del object_in
+    rows = object_ref.shape[1]
+    copies = []
+    for k, (edge_ref, corners_ref) in enumerate(((north_ref, north_corners_ref), (south_ref, south_corners_ref))):
+        for p in range(PLANES):
+            corners = from_sides(corners_ref[0:HALO, :], corners_ref[HALO:, :], p)
+            for q in range(2):
+                cols = slice(q * LANES, (q + 1) * LANES)
+                strips[k, p, :, cols] = edge_ref[p, :, cols] + corners[q]
+        place_at = slice(0, HALO) if k == 0 else slice(rows - HALO, rows)
+        copies.append(pltpu.make_async_copy(strips.at[k], object_ref.at[:, place_at, :], sem.at[k]))
+        copies[-1].start()
     total = total_ref[...]
     squares = jnp.sum(total * total, axis=0, keepdims=True)
     mean = jnp.sum(squares, axis=1, keepdims=True) / (total.shape[0] * total.shape[1])
-    probe_new_ref[...] = probe_ref[...] - total * (STEP_SIZE / jnp.sqrt(mean + EPSILON))
+    scale = STEP_SIZE / jnp.sqrt(mean + EPSILON)
+    chunk = total.shape[0] // CHUNKS
+    for k in range(CHUNKS):
+        part = slice(k * chunk, (k + 1) * chunk)
+        steps[part, :] = probe_ref[part, :] - total_ref[part, :] * scale
+        copies.append(pltpu.make_async_copy(steps.at[part, :], probe_new_ref.at[part, :], sem.at[2 + k]))
+        copies[-1].start()
+    for copy in copies:
+        copy.wait()
 
 
 def vmem(count):
@@ -401,10 +422,26 @@
     to_north, to_south = call(rim_corner_kernel, [f32(2 * HALO, LANES)] * 2, 2, us=20)(rim_from_west, rim_from_east)
     south_corners = moved(to_north, "row", -1)
     north_corners = moved(to_south, "row", 1)
-    object_grad = call(object_kernel, f32(PLANES, rows, cols), 7)(
-        center, from_north, from_south, rim_from_west, rim_from_east, north_corners, south_corners
-    )
-    probe_new = call(probe_kernel, f32(*flat), 2)(total.reshape(flat), probe_modes.reshape(flat))
+    edge = f32(PLANES, HALO, cols)
+    bulk, north_edge, south_edge = call(object_kernel, [f32(PLANES, rows, cols), edge, edge], 5)(
+        center, from_north, from_south, rim_from_west, rim_from_east
+    )
+    anywhere = pl.BlockSpec(memory_space=pl.ANY)
+    object_grad, probe_new = pl.pallas_call(
+        final_kernel,
+        out_shape=[f32(PLANES, rows, cols), f32(*flat)],
+        in_specs=[anywhere] + vmem(6),
+        out_specs=[anywhere] * 2,
+        scratch_shapes=[
+            pltpu.VMEM((2, PLANES, HALO, cols), jnp.float32),
+            pltpu.VMEM(flat, jnp.float32),
+            pltpu.SemaphoreType.DMA((2 + CHUNKS,)),
+        ],
+        input_output_aliases={0: 0},
+        compiler_params=pltpu.CompilerParams(vmem_limit_bytes=2 * 2**20),
+    )(
+        bulk, north_edge, south_edge, north_corners, south_corners, total.reshape(flat), probe_modes.reshape(flat)
+    )
     return object_grad.reshape(object_tiles.shape), probe_new.reshape(probe_modes.shape)
 
 

time: 73.1 us -> 73.1 us (level)
    all_to_all x1, waiting for transfers between devices: 1.39 us -> 2.68 us  [on_device(): total = lax.all_to_all(share, BOTH, 0, 0, tiled=True)]
    ppermute x12, waiting for transfers between devices: 14.1 us -> 12.9 us  [moved(): lax.ppermute(block, axis, [(i, (i + distance) % count) for i in range(cou...]
where the time goes in v7:
time: 73.1 us; the launch traced here: 72.8 us
  starting transfers between devices  34.7 us (47%)
  waiting for transfers between devices  23 us (31%)
  Pallas kernels  12.1 us (17%)
  local copies, waits for them, and re-layouts  2.24 us (3%)
  between operations  0.76 us (1%)
    ppermute x12, starting transfers between devices, moved(): lax.ppermute(block, axis, [(i, (i + distance) % count) for i in range(cou...  21.9 us
    ppermute x12, waiting for transfers between devices, moved(): lax.ppermute(block, axis, [(i, (i + distance) % count) for i in range(cou...  12.9 us
    all_to_all x1, starting transfers between devices, on_device(): lax.all_to_all(probe_grad.reshape(devices, -1, LANES), BOTH, 0, 0, tiled=...  8.52 us
    pallas_call x1, Pallas kernels, main_call(): return lambda *args: run(*args)[:6]  8.33 us
    all_to_all x1, waiting for transfers between devices, on_device(): lax.all_to_all(probe_grad.reshape(devices, -1, LANES), BOTH, 0, 0, tiled=...  7.41 us
    all_to_all x1, starting transfers between devices, on_device(): total = lax.all_to_all(share, BOTH, 0, 0, tiled=True)  4.29 us
    all_to_all x1, waiting for transfers between devices, on_device(): total = lax.all_to_all(share, BOTH, 0, 0, tiled=True)  2.68 us
  transfers between devices with their start and end apart: 14, of which 6 were waited for; matrix products, arithmetic and copies ran while one was open for 0% of the time, Pallas kernels for 4%

profile of v7, /device:TPU:1, one launch (start us, length us, event | category | flops | bytes accessed | tf_op | source)
XLA Modules:
  0.0 72.8 jit_solution(7944110847188864715)
XLA Ops:
  0.6 1.0 %fusion = (f32[4,32,256]{2,1,0:T(8,128)S(1)}, f32[4,32,256]{2,1,0:T(8,128)S(1)}) fusion(f32[4,256,256]{2,1,0:T(8,128)} %bitcast.12), kind=kLoop, calls=%fused_computation | loop fusion | bytes 524288 | tf_op jit(solution)/shard_map/slice | solution.py:402
  1.6 6.1 %collective-permute-start.1 = (f32[4,32,256]{2,1,0:T(8,128)S(1)}, f32[4,32,256]{2,1,0:T(8,128)S(1)}, u32[]{:S(2)}, u32[]{:S(2)}) collective-permute-start(f32[4,32,256]{2,1,0:T(8,128)S(1)} %get-tuple-element.36), channel_id=1, source_target_pairs={{0,112},{16,0},{32,16},{48,32},{64,48},{80,64},{96,80},{112,96},{1... | collective-permute-start | bytes 393224 | tf_op jit(solution)/shard_map/ppermute | solution.py:347
  7.7 0.0 collective-permute-start
  7.7 0.0 copy-start.1
  7.7 1.2 %copy-done.1 = f32[2,2,256,256]{3,2,1,0:T(8,128)S(1)} copy-done((f32[2,2,256,256]{3,2,1,0:T(8,128)S(1)}, f32[2,2,256,256]{3,2,1,0:T(8,128)}, u32[]{:S(2)}) %copy-start.1) | copy-done | bytes 1048600
  8.9 0.3 shard_map.69
  9.2 0.0 copy-start.2
  9.2 1.2 %collective-permute-start.2 = (f32[256,128]{1,0:T(8,128)S(1)}, f32[256,128]{1,0:T(8,128)S(1)}, u32[]{:S(2)}, u32[]{:S(2)}) collective-permute-start(f32[256,128]{1,0:T(8,128)S(1)} %get-tuple-element.19), channel_id=1, source_target_pairs={{0,1},{1,2},{2,3},{3,4},{4,5},{5,6},{6,7},{7,8},{8,9},{9,10},{10,1... | collective-permute-start | bytes 393224 | tf_op jit(solution)/shard_map/ppermute | solution.py:347
  10.5 0.0 collective-permute-start.3
  10.5 0.0 collective-permute-done.1.south_ref
  10.5 4.7 %collective-permute-done.north_ref = f32[4,32,256]{2,1,0:T(8,128)S(1)} collective-permute-done((f32[4,32,256]{2,1,0:T(8,128)S(1)}, f32[4,32,256]{2,1,0:T(8,128)S(1)}, u32[]{:S(2)}, u32[]{:S(2)}) %collective-permute-start) | collective-permute-done | bytes 131104 | tf_op jit(solution)/shard_map/ppermute | solution.py:347
  15.2 0.1 shard_map.70
  15.3 2.4 %collective-permute-start.4 = (f32[64,128]{1,0:T(8,128)S(1)}, f32[64,128]{1,0:T(8,128)S(1)}, u32[]{:S(2)}, u32[]{:S(2)}) collective-permute-start(f32[64,128]{1,0:T(8,128)S(1)} %get-tuple-element.21), channel_id=1, source_target_pairs={{0,1},{1,2},{2,3},{3,4},{4,5},{5,6},{6,7},{7,8},{8,9},{9,10},{10,1... | collective-permute-start | bytes 98312 | tf_op jit(solution)/shard_map/ppermute | solution.py:347
  17.6 0.0 copy-start
  17.6 0.0 copy-start.3
  17.7 0.0 copy-start.4
  17.7 0.0 copy-start.5
  17.7 0.1 collective-permute-start.5
  17.7 0.0 copy-done.2
  17.8 0.1 shard_map.68.ext_in
  17.8 0.0 collective-permute-done.2.from_west_ref
  17.9 0.0 collective-permute-done.3.from_east_ref
  17.9 0.8 %collective-permute-done.4.west_corners_ref = f32[64,128]{1,0:T(8,128)S(1)} collective-permute-done((f32[64,128]{1,0:T(8,128)S(1)}, f32[64,128]{1,0:T(8,128)S(1)}, u32[]{:S(2)}, u32[]{:S(2)}) %collective-permute-start.4) | collective-permute-done | bytes 32800 | tf_op jit(solution)/shard_map/ppermute | solution.py:347
  18.7 2.4 %collective-permute-done.5.east_corners_ref = f32[64,128]{1,0:T(8,128)S(1)} collective-permute-done((f32[64,128]{1,0:T(8,128)S(1)}, f32[64,128]{1,0:T(8,128)S(1)}, u32[]{:S(2)}, u32[]{:S(2)}) %collective-permute-start.5) | collective-permute-done | bytes 32800 | tf_op jit(solution)/shard_map/ppermute | solution.py:347
  21.1 0.0 copy-done
  21.1 0.0 copy-done.3
  21.1 0.0 copy-done.4
  21.1 0.0 copy-done.5
  21.1 8.3 %shard_map.71 = (f32[2,4,128,128]{3,2,1,0:T(8,128)}, f32[4,256,256]{2,1,0:T(8,128)S(1)}, f32[4,32,256]{2,1,0:T(8,128)S(1)}, f32[4,32,256]{2,1,0:T(8,128)S(1)}, f...) custom-call(s32[2,3]{1,0:T(2,128)S(1)} %bitcast.16, ...), custom_call_target="tpu_custom_call", output_to_operand_aliasing={{6}: (1, {})} | custom-call | flops 12000000000 | bytes 36000000 | tf_op jit(solution)/shard_map/pallas_call | solution.py:387
  29.4 8.5 %all-to-all-start = ((f32[128,8,128]{2,1,0:T(8,128)}), f32[128,8,128]{2,1,0:T(8,128)S(1)}, u32[]{:S(2)}, u32[]{:S(2)}) async-start(f32[128,8,128]{2,1,0:T(8,128)} %bitcast.4), calls=%async_computation | async-start | bytes 1048576 | tf_op jit(solution)/shard_map/all_to_all | solution.py:415
  37.9 1.7 %collective-permute-start.8 = (f32[320,128]{1,0:T(8,128)S(1)}, f32[320,128]{1,0:T(8,128)S(1)}, u32[]{:S(2)}, u32[]{:S(2)}) collective-permute-start(f32[320,128]{1,0:T(8,128)S(1)} %get-tuple-element.26), channel_id=1, source_target_pairs={{0,1},{1,2},{2,3},{3,4},{4,5},{5,6},{6,7},{7,8},{8,9},{9,10},{10,1... | collective-permute-start | bytes 491528 | tf_op jit(solution)/shard_map/ppermute | solution.py:347
  39.6 0.0 collective-permute-start.9
  39.7 2.4 %collective-permute-start.6 = (f32[4,32,256]{2,1,0:T(8,128)S(1)}, f32[4,32,256]{2,1,0:T(8,128)S(1)}, u32[]{:S(2)}, u32[]{:S(2)}) collective-permute-start(f32[4,32,256]{2,1,0:T(8,128)S(1)} %get-tuple-element.24), channel_id=1, source_target_pairs={{0,16},{16,32},{32,48},{48,64},{64,80},{80,96},{96,112},{112,0},{1... | collective-permute-start | bytes 393224 | tf_op jit(solution)/shard_map/ppermute | solution.py:347
  42.0 2.7 %collective-permute-start.7 = (f32[4,32,256]{2,1,0:T(8,128)S(1)}, f32[4,32,256]{2,1,0:T(8,128)S(1)}, u32[]{:S(2)}, u32[]{:S(2)}) collective-permute-start(f32[4,32,256]{2,1,0:T(8,128)S(1)} %get-tuple-element.25), channel_id=1, source_target_pairs={{0,112},{16,0},{32,16},{48,32},{64,48},{80,64},{96,80},{112,96},{1... | collective-permute-start | bytes 393224 | tf_op jit(solution)/shard_map/ppermute | solution.py:347
  44.7 7.4 %all-to-all-done.parts_ref = f32[128,8,128]{2,1,0:T(8,128)S(1)} async-done(((f32[128,8,128]{2,1,0:T(8,128)}), f32[128,8,128]{2,1,0:T(8,128)S(1)}, u32[]{:S(2)}, u32[]{:S(2)}) %all-to-all-start) | async-done | bytes 524320 | tf_op jit(solution)/shard_map/all_to_all | solution.py:415
  52.1 1.0 %shard_map.74 = f32[128,8,128]{2,1,0:T(8,128)} custom-call(f32[128,8,128]{2,1,0:T(8,128)S(1)} %all-to-all-done.parts_ref), custom_call_target="tpu_custom_call" | custom-call | tf_op jit(solution)/shard_map/pallas_call | solution.py:420
  53.1 4.3 %all-to-all-start.1 = ((f32[128,8,128]{2,1,0:T(8,128)}), f32[128,8,128]{2,1,0:T(8,128)S(1)}, u32[]{:S(2)}, u32[]{:S(2)}) async-start(f32[128,8,128]{2,1,0:T(8,128)} %shard_map.74), calls=%async_computation.1 | async-start | bytes 1048576 | tf_op jit(solution)/shard_map/all_to_all | solution.py:421
  57.4 0.0 collective-permute-done.8.from_west_ref
  57.4 0.0 collective-permute-done.9.from_east_ref
  57.4 3.0 %collective-permute-start.10 = (f32[64,128]{1,0:T(8,128)S(1)}, f32[64,128]{1,0:T(8,128)S(1)}, u32[]{:S(2)}, u32[]{:S(2)}) collective-permute-start(f32[64,128]{1,0:T(8,128)S(1)} %get-tuple-element.31), channel_id=1, source_target_pairs={{0,16},{16,32},{32,48},{48,64},{64,80},{80,96},{96,112},{112,0},{1... | collective-permute-start | bytes 98312 | tf_op jit(solution)/shard_map/ppermute | solution.py:347
  60.4 2.4 %collective-permute-start.11 = (f32[64,128]{1,0:T(8,128)S(1)}, f32[64,128]{1,0:T(8,128)S(1)}, u32[]{:S(2)}, u32[]{:S(2)}) collective-permute-start(f32[64,128]{1,0:T(8,128)S(1)} %get-tuple-element.32), channel_id=1, source_target_pairs={{0,112},{16,0},{32,16},{48,32},{64,48},{80,64},{96,80},{112,96},{1... | collective-permute-start | bytes 98312 | tf_op jit(solution)/shard_map/ppermute | solution.py:347
  62.8 0.0 collective-permute-done.6.from_north_ref
  62.8 0.0 collective-permute-done.7.from_south_ref
  62.8 1.2 %shard_map.72 = (f32[4,256,256]{2,1,0:T(8,128)}, f32[4,32,256]{2,1,0:T(8,128)S(1)}, f32[4,32,256]{2,1,0:T(8,128)S(1)}) custom-call(f32[4,256,256]{2,1,0:T(8,128)S(1)} %get-tuple-element.23.center_ref, f32[4,32,256]{2,1,0:T(8,128)S(1)} %collective-permute-done.6.from_north_ref, f32[4,32,256]{2,1,0:T(8,128)S(1)} %collective-permute-done.7.from_south_ref, ...), custom_call_target="tpu_custom_call" | custom-call | tf_op jit(solution)/shard_map/pallas_call | solution.py:426
  64.1 5.0 %collective-permute-done.10.north_corners_ref = f32[64,128]{1,0:T(8,128)S(1)} collective-permute-done((f32[64,128]{1,0:T(8,128)S(1)}, f32[64,128]{1,0:T(8,128)S(1)}, u32[]{:S(2)}, u32[]{:S(2)}) %collective-permute-start.10) | collective-permute-done | bytes 32800 | tf_op jit(solution)/shard_map/ppermute | solution.py:347
  69.1 0.0 collective-permute-done.11.south_corners_ref
  69.1 2.7 %all-to-all-done.1 = f32[128,8,128]{2,1,0:T(8,128)S(1)} async-done(((f32[128,8,128]{2,1,0:T(8,128)}), f32[128,8,128]{2,1,0:T(8,128)S(1)}, u32[]{:S(2)}, u32[]{:S(2)}) %all-to-all-start.1) | async-done | bytes 524320 | tf_op jit(solution)/shard_map/all_to_all | solution.py:421
  71.7 1.1 %shard_map.75 = (f32[4,256,256]{2,1,0:T(8,128)}, f32[1024,128]{1,0:T(8,128)}) custom-call(f32[4,256,256]{2,1,0:T(8,128)} %get-tuple-element.28.object_in, f32[4,32,256]{2,1,0:T(8,128)S(1)} %get-tuple-element.29.north_ref, f32[4,32,256]{2,1,0:T(8,128)S(1)} %get-tuple-element.30.south_ref, ...), custom_call_target="tpu_custom_call", output_to_operand_aliasing={{0}: (0, {})} | custom-call | tf_op jit(solution)/shard_map/pallas_call | solution.py:430
  (1 shorter events, 0.0 us)
Async XLA Ops:
  1.6 8.8 %collective-permute-start.1 = (f32[4,32,256]{2,1,0:T(8,128)S(1)}, f32[4,32,256]{2,1,0:T(8,128)S(1)}, u32[]{:S(2)}, u32[]{:S(2)}) collective-permute-start(f32[4,32,256]{2,1,0:T(8,128)S(1)} %get-tuple-element.36), channel_id=1, source_target_pairs={{0,112},{16,0},{32,16},{48,32},{64,48},{80,64},{96,80},{112,96},{1... | collective-permute-start | bytes 393224 | tf_op jit(solution)/shard_map/ppermute | solution.py:347
  7.7 7.4 %collective-permute-start = (f32[4,32,256]{2,1,0:T(8,128)S(1)}, f32[4,32,256]{2,1,0:T(8,128)S(1)}, u32[]{:S(2)}, u32[]{:S(2)}) collective-permute-start(f32[4,32,256]{2,1,0:T(8,128)S(1)} %get-tuple-element.37), channel_id=1, source_target_pairs={{0,16},{16,32},{32,48},{48,64},{64,80},{80,96},{96,112},{112,0},{1... | collective-permute-start | bytes 393224 | tf_op jit(solution)/shard_map/ppermute | solution.py:347
  7.7 1.2 %copy-start.1 = (f32[2,2,256,256]{3,2,1,0:T(8,128)S(1)}, f32[2,2,256,256]{3,2,1,0:T(8,128)}, u32[]{:S(2)}) copy-start(f32[2,2,256,256]{3,2,1,0:T(8,128)} %param.5) | copy-start | bytes 3145732
  9.2 8.5 %copy-start.2 = (f32[2,2,256,256]{3,2,1,0:T(8,128)S(1)}, f32[2,2,256,256]{3,2,1,0:T(8,128)}, u32[]{:S(2)}) copy-start(f32[2,2,256,256]{3,2,1,0:T(8,128)} %param.5) | copy-start | bytes 3145732
  9.2 8.6 %collective-permute-start.2 = (f32[256,128]{1,0:T(8,128)S(1)}, f32[256,128]{1,0:T(8,128)S(1)}, u32[]{:S(2)}, u32[]{:S(2)}) collective-permute-start(f32[256,128]{1,0:T(8,128)S(1)} %get-tuple-element.19), channel_id=1, source_target_pairs={{0,1},{1,2},{2,3},{3,4},{4,5},{5,6},{6,7},{7,8},{8,9},{9,10},{10,1... | collective-permute-start | bytes 393224 | tf_op jit(solution)/shard_map/ppermute | solution.py:347
  10.5 7.4 %collective-permute-start.3 = (f32[256,128]{1,0:T(8,128)S(1)}, f32[256,128]{1,0:T(8,128)S(1)}, u32[]{:S(2)}, u32[]{:S(2)}) collective-permute-start(f32[256,128]{1,0:T(8,128)S(1)} %get-tuple-element.20), channel_id=1, source_target_pairs={{0,15},{1,0},{2,1},{3,2},{4,3},{5,4},{6,5},{7,6},{8,7},{9,8},{10,9... | collective-permute-start | bytes 393224 | tf_op jit(solution)/shard_map/ppermute | solution.py:347
  15.3 3.4 %collective-permute-start.4 = (f32[64,128]{1,0:T(8,128)S(1)}, f32[64,128]{1,0:T(8,128)S(1)}, u32[]{:S(2)}, u32[]{:S(2)}) collective-permute-start(f32[64,128]{1,0:T(8,128)S(1)} %get-tuple-element.21), channel_id=1, source_target_pairs={{0,1},{1,2},{2,3},{3,4},{4,5},{5,6},{6,7},{7,8},{8,9},{9,10},{10,1... | collective-permute-start | bytes 98312 | tf_op jit(solution)/shard_map/ppermute | solution.py:347
  17.6 3.4 %copy-start = (f32[2,4,128,128]{3,2,1,0:T(8,128)S(1)}, f32[2,4,128,128]{3,2,1,0:T(8,128)}, u32[]{:S(2)}) copy-start(f32[2,4,128,128]{3,2,1,0:T(8,128)} %probe_ref.1) | copy-start | bytes 1572868
  17.6 3.4 %copy-start.3 = (f32[1,1,3,128,128]{4,3,2,1,0:T(8,128)S(1)}, f32[1,1,3,128,128]{4,3,2,1,0:T(8,128)}, u32[]{:S(2)}) copy-start(f32[1,1,3,128,128]{4,3,2,1,0:T(8,128)} %param.8) | copy-start | bytes 589828
  17.7 3.4 %copy-start.4 = (s32[1,1,3,2]{2,3,1,0:T(2,128)S(1)}, s32[1,1,3,2]{2,3,1,0:T(2,128)}, u32[]{:S(2)}) copy-start(s32[1,1,3,2]{2,3,1,0:T(2,128)} %param.7) | copy-start | bytes 76
  17.7 3.4 %copy-start.5 = (bf16[4,2,256,256]{3,2,1,0:T(8,128)(2,1)S(1)}, bf16[4,2,256,256]{3,2,1,0:T(8,128)(2,1)}, u32[]{:S(2)}) copy-start(bf16[4,2,256,256]{3,2,1,0:T(8,128)(2,1)} %constant.2.clone.mat_ref) | copy-start | bytes 3145732
  17.7 3.4 %collective-permute-start.5 = (f32[64,128]{1,0:T(8,128)S(1)}, f32[64,128]{1,0:T(8,128)S(1)}, u32[]{:S(2)}, u32[]{:S(2)}) collective-permute-start(f32[64,128]{1,0:T(8,128)S(1)} %get-tuple-element.22), channel_id=1, source_target_pairs={{0,15},{1,0},{2,1},{3,2},{4,3},{5,4},{6,5},{7,6},{8,7},{9,8},{10,9... | collective-permute-start | bytes 98312 | tf_op jit(solution)/shard_map/ppermute | solution.py:347
  29.4 22.7 %all-to-all-start = ((f32[128,8,128]{2,1,0:T(8,128)}), f32[128,8,128]{2,1,0:T(8,128)S(1)}, u32[]{:S(2)}, u32[]{:S(2)}) async-start(f32[128,8,128]{2,1,0:T(8,128)} %bitcast.4), calls=%async_computation | async-start | bytes 1048576 | tf_op jit(solution)/shard_map/all_to_all | solution.py:415
  37.9 19.5 %collective-permute-start.8 = (f32[320,128]{1,0:T(8,128)S(1)}, f32[320,128]{1,0:T(8,128)S(1)}, u32[]{:S(2)}, u32[]{:S(2)}) collective-permute-start(f32[320,128]{1,0:T(8,128)S(1)} %get-tuple-element.26), channel_id=1, source_target_pairs={{0,1},{1,2},{2,3},{3,4},{4,5},{5,6},{6,7},{7,8},{8,9},{9,10},{10,1... | collective-permute-start | bytes 491528 | tf_op jit(solution)/shard_map/ppermute | solution.py:347
  39.6 17.8 %collective-permute-start.9 = (f32[320,128]{1,0:T(8,128)S(1)}, f32[320,128]{1,0:T(8,128)S(1)}, u32[]{:S(2)}, u32[]{:S(2)}) collective-permute-start(f32[320,128]{1,0:T(8,128)S(1)} %get-tuple-element.27), channel_id=1, source_target_pairs={{0,15},{1,0},{2,1},{3,2},{4,3},{5,4},{6,5},{7,6},{8,7},{9,8},{10,9... | collective-permute-start | bytes 491528 | tf_op jit(solution)/shard_map/ppermute | solution.py:347
  39.7 23.2 %collective-permute-start.6 = (f32[4,32,256]{2,1,0:T(8,128)S(1)}, f32[4,32,256]{2,1,0:T(8,128)S(1)}, u32[]{:S(2)}, u32[]{:S(2)}) collective-permute-start(f32[4,32,256]{2,1,0:T(8,128)S(1)} %get-tuple-element.24), channel_id=1, source_target_pairs={{0,16},{16,32},{32,48},{48,64},{64,80},{80,96},{96,112},{112,0},{1... | collective-permute-start | bytes 393224 | tf_op jit(solution)/shard_map/ppermute | solution.py:347
  42.0 20.8 %collective-permute-start.7 = (f32[4,32,256]{2,1,0:T(8,128)S(1)}, f32[4,32,256]{2,1,0:T(8,128)S(1)}, u32[]{:S(2)}, u32[]{:S(2)}) collective-permute-start(f32[4,32,256]{2,1,0:T(8,128)S(1)} %get-tuple-element.25), channel_id=1, source_target_pairs={{0,112},{16,0},{32,16},{48,32},{64,48},{80,64},{96,80},{112,96},{1... | collective-permute-start | bytes 393224 | tf_op jit(solution)/shard_map/ppermute | solution.py:347
  53.1 18.6 %all-to-all-start.1 = ((f32[128,8,128]{2,1,0:T(8,128)}), f32[128,8,128]{2,1,0:T(8,128)S(1)}, u32[]{:S(2)}, u32[]{:S(2)}) async-start(f32[128,8,128]{2,1,0:T(8,128)} %shard_map.74), calls=%async_computation.1 | async-start | bytes 1048576 | tf_op jit(solution)/shard_map/all_to_all | solution.py:421
  57.4 11.6 %collective-permute-start.10 = (f32[64,128]{1,0:T(8,128)S(1)}, f32[64,128]{1,0:T(8,128)S(1)}, u32[]{:S(2)}, u32[]{:S(2)}) collective-permute-start(f32[64,128]{1,0:T(8,128)S(1)} %get-tuple-element.31), channel_id=1, source_target_pairs={{0,16},{16,32},{32,48},{48,64},{64,80},{80,96},{96,112},{112,0},{1... | collective-permute-start | bytes 98312 | tf_op jit(solution)/shard_map/ppermute | solution.py:347
  60.4 8.6 %collective-permute-start.11 = (f32[64,128]{1,0:T(8,128)S(1)}, f32[64,128]{1,0:T(8,128)S(1)}, u32[]{:S(2)}, u32[]{:S(2)}) collective-permute-start(f32[64,128]{1,0:T(8,128)S(1)} %get-tuple-element.32), channel_id=1, source_target_pairs={{0,112},{16,0},{32,16},{48,32},{64,48},{80,64},{96,80},{112,96},{1... | collective-permute-start | bytes 98312 | tf_op jit(solution)/shard_map/ppermute | solution.py:347

commit v8 on v7

--- a/solution.py
+++ b/solution.py
@@ -1,3 +1,5 @@
+import math
+
 import jax
 import jax.numpy as jnp
 import numpy as np
@@ -15,7 +17,9 @@
 SHIFT_AMP = 0.5
 STEP_SIZE = 0.5
 EPSILON = 1e-06
-BOTH = ("row", "col")
+COL = ("pair", "core")
+PEERS = ("row", "pair")
+SWAP = [(0, 1), (1, 0)]
 
 
 def matrices():
@@ -92,9 +96,9 @@
 
 
 def main_kernel(
-    offsets_ref, ext_in, from_west_ref, from_east_ref, west_corners_ref, east_corners_ref, amp_ref, probe_ref, mat_ref,
-    probe_grad_ref, center_ref, north_rim_ref, south_rim_ref, east_rim_ref, west_rim_ref, ext,
-    rh, rl, lh, ll, field, d_keep, win, factor, grad,
+    offsets_ref, core_ref, ext_in, from_west_ref, from_east_ref, west_corners_ref, east_corners_ref, amp_ref, probe_ref, mat_ref,
+    keep_ref, send_ref, center_ref, north_rim_ref, south_rim_ref, east_rim_ref, west_rim_ref, ext,
+    rh, rl, lh, ll, field, d_keep, win, factor, grad, probe_grad_ref,
 ):
     del ext_in
     ext_rows = ext.shape[2]
@@ -254,6 +258,8 @@
         run, *[pltpu.ACC(c)((ROWS, 2 * WIN), jnp.float32) for _ in scans for c in chains for _ in range(BLOCKS)]
     )
 
+    keep_ref[...] = probe_grad_ref[core_ref[0]]
+    send_ref[...] = probe_grad_ref[1 - core_ref[0]]
     lane_all = lane_iota(ext_rows)
     east = jnp.zeros((ext_rows, LANES), jnp.float32)
     west = jnp.zeros((ext_rows, LANES), jnp.float32)
@@ -277,6 +283,10 @@
         to_south_ref[k * HALO : (k + 1) * HALO, :] = ref[ref.shape[0] - HALO :, :]
 
 
+def add_kernel(left_ref, right_ref, out_ref):
+    out_ref[...] = left_ref[...] + right_ref[...]
+
+
 def share_kernel(parts_ref, *refs):
     share_ref = refs[-1]
     share_ref[...] = jnp.broadcast_to(jnp.sum(parts_ref[...], axis=0)[None], share_ref.shape)
@@ -305,7 +315,7 @@
 
 
 def final_kernel(
-    object_in, north_ref, south_ref, north_corners_ref, south_corners_ref, total_ref, probe_ref,
+    object_in, north_ref, south_ref, north_corners_ref, south_corners_ref, mine_ref, other_ref, probe_ref, core_ref,
     object_ref, probe_new_ref, strips, steps, sem,
 ):
     del object_in
@@ -320,15 +330,16 @@
         place_at = slice(0, HALO) if k == 0 else slice(rows - HALO, rows)
         copies.append(pltpu.make_async_copy(strips.at[k], object_ref.at[:, place_at, :], sem.at[k]))
         copies[-1].start()
-    total = total_ref[...]
-    squares = jnp.sum(total * total, axis=0, keepdims=True)
-    mean = jnp.sum(squares, axis=1, keepdims=True) / (total.shape[0] * total.shape[1])
+    squares = jnp.sum(mine_ref[...] * mine_ref[...] + other_ref[...] * other_ref[...], axis=0, keepdims=True)
+    mean = jnp.sum(squares, axis=1, keepdims=True) / (2 * mine_ref.shape[0] * mine_ref.shape[1])
     scale = STEP_SIZE / jnp.sqrt(mean + EPSILON)
-    chunk = total.shape[0] // CHUNKS
+    core = core_ref[0]
+    chunk = mine_ref.shape[0] // CHUNKS
     for k in range(CHUNKS):
         part = slice(k * chunk, (k + 1) * chunk)
-        steps[part, :] = probe_ref[part, :] - total_ref[part, :] * scale
-        copies.append(pltpu.make_async_copy(steps.at[part, :], probe_new_ref.at[part, :], sem.at[2 + k]))
+        steps[core, part, :] = probe_ref[core, part, :] - mine_ref[part, :] * scale
+        steps[1 - core, part, :] = probe_ref[1 - core, part, :] - other_ref[part, :] * scale
+        copies.append(pltpu.make_async_copy(steps.at[:, part, :], probe_new_ref.at[:, part, :], sem.at[2 + k]))
         copies[-1].start()
     for copy in copies:
         copy.wait()
@@ -342,8 +353,12 @@
     return jax.ShapeDtypeStruct(shape, jnp.float32)
 
 
+def axis_count(axes):
+    return math.prod(lax.axis_size(a) for a in ((axes,) if isinstance(axes, str) else axes))
+
+
 def moved(block, axis, distance):
-    count = lax.axis_size(axis)
+    count = axis_count(axis)
     return lax.ppermute(block, axis, [(i, (i + distance) % count) for i in range(count)])
 
 
@@ -367,24 +382,25 @@
     ext_rows = rows + 2 * HALO
     pair = pltpu.VMEM((scans, MODES // 2, 2 * WIN, 2 * WIN), jnp.bfloat16)
     modes = pltpu.VMEM((scans, 2, MODES, WIN, WIN), jnp.float32)
-    outs = [f32(2, MODES, WIN, WIN), f32(PLANES, rows, cols)]
+    outs = [f32(MODES, WIN, WIN), f32(MODES, WIN, WIN), f32(PLANES, rows, cols)]
     outs += [f32(PLANES, HALO, cols)] * 2 + [f32(ext_rows, LANES)] * 2 + [f32(PLANES, 3, ext_rows, LANES)]
     run = pl.pallas_call(
         main_kernel,
         out_shape=outs,
-        in_specs=[pl.BlockSpec(memory_space=pltpu.SMEM)] + vmem(8),
+        in_specs=[pl.BlockSpec(memory_space=pltpu.SMEM)] * 2 + vmem(8),
         out_specs=vmem(len(outs)),
         scratch_shapes=[
             pair, pair, pair, pair, modes, modes,
             pltpu.VMEM((scans, PLANES, WIN, WIN), jnp.float32),
             pltpu.VMEM((scans, WIN, WIN), jnp.float32),
             pltpu.VMEM((PLANES, 3, ext_rows, LANES), jnp.float32),
+            pltpu.VMEM((2, MODES, WIN, WIN), jnp.float32),
         ],
-        input_output_aliases={1: 6},
+        input_output_aliases={2: 7},
         compiler_params=pltpu.CompilerParams(vmem_limit_bytes=24 * 2**20),
         cost_estimate=cost(12),
     )
-    return lambda *args: run(*args)[:6]
+    return lambda *args: run(*args)[:7]
 
 
 def on_device(object_tiles, probe_modes, offsets, amplitude):
@@ -392,45 +408,48 @@
     ext_rows = rows + 2 * HALO
     scans = offsets.shape[2]
     tile = object_tiles.reshape(PLANES, rows, cols)
+    core = lax.axis_index("core").astype(jnp.int32).reshape(1)
     offset_pairs = jnp.swapaxes(offsets, 2, 3).reshape(2, scans)
     amp = amplitude.reshape(scans, WIN, WIN)
-    flat = (2 * MODES * WIN, WIN)
+    flat = (2, MODES * WIN, WIN)
     mats = jnp.asarray(matrices())
-    devices = lax.axis_size("row") * lax.axis_size("col")
 
     north = moved(tile[:, rows - HALO :], "row", 1)
     south = moved(tile[:, :HALO], "row", -1)
     east_send, west_send = call(pack_kernel, [f32(rows, LANES)] * 2, 1, us=1)(tile)
-    from_west = moved(east_send, "col", 1)
-    from_east = moved(west_send, "col", -1)
+    from_west = moved(east_send, COL, 1)
+    from_east = moved(west_send, COL, -1)
     east_send, west_send = call(corner_kernel, [f32(2 * HALO, LANES)] * 2, 2, us=1)(north, south)
-    west_corners = moved(east_send, "col", 1)
-    east_corners = moved(west_send, "col", -1)
+    west_corners = moved(east_send, COL, 1)
+    east_corners = moved(west_send, COL, -1)
 
     ext = call(assemble_kernel, f32(PLANES, 3, ext_rows, LANES), 3, us=4)(tile, north, south)
-    probe_grad, center, north_rim, south_rim, east_rim, west_rim = main_call(scans, rows, cols)(
-        offset_pairs, ext, from_west, from_east, west_corners, east_corners, amp, probe_modes, mats
-    )
-
-    parts = lax.all_to_all(probe_grad.reshape(devices, -1, LANES), BOTH, 0, 0, tiled=True)
-    rim_from_west = moved(east_rim, "col", 1)
-    rim_from_east = moved(west_rim, "col", -1)
+    keep, send, center, north_rim, south_rim, east_rim, west_rim = main_call(scans, rows, cols)(
+        offset_pairs, core, ext, from_west, from_east, west_corners, east_corners, amp, probe_modes, mats
+    )
+
+    got = lax.ppermute(send, "core", SWAP)
+    half_sum = call(add_kernel, f32(MODES, WIN, WIN), 2)(keep, got)
+    parts = lax.all_to_all(half_sum.reshape(axis_count(PEERS), -1, LANES), PEERS, 0, 0, tiled=True)
+    rim_from_west = moved(east_rim, COL, 1)
+    rim_from_east = moved(west_rim, COL, -1)
     from_south = moved(north_rim, "row", -1)
     from_north = moved(south_rim, "row", 1)
     share = call(share_kernel, f32(*parts.shape), 1)(parts)
-    total = lax.all_to_all(share, BOTH, 0, 0, tiled=True)
-    to_north, to_south = call(rim_corner_kernel, [f32(2 * HALO, LANES)] * 2, 2, us=20)(rim_from_west, rim_from_east)
+    mine = lax.all_to_all(share, PEERS, 0, 0, tiled=True).reshape(MODES * WIN, WIN)
+    other = lax.ppermute(mine, "core", SWAP)
+    to_north, to_south = call(rim_corner_kernel, [f32(2 * HALO, LANES)] * 2, 2, us=80)(rim_from_west, rim_from_east)
     south_corners = moved(to_north, "row", -1)
     north_corners = moved(to_south, "row", 1)
     edge = f32(PLANES, HALO, cols)
-    bulk, north_edge, south_edge = call(object_kernel, [f32(PLANES, rows, cols), edge, edge], 5)(
+    bulk, north_edge, south_edge = call(object_kernel, [f32(PLANES, rows, cols), edge, edge], 5, us=80)(
         center, from_north, from_south, rim_from_west, rim_from_east
     )
     anywhere = pl.BlockSpec(memory_space=pl.ANY)
     object_grad, probe_new = pl.pallas_call(
         final_kernel,
         out_shape=[f32(PLANES, rows, cols), f32(*flat)],
-        in_specs=[anywhere] + vmem(6),
+        in_specs=[anywhere] + vmem(7) + [pl.BlockSpec(memory_space=pltpu.SMEM)],
         out_specs=[anywhere] * 2,
         scratch_shapes=[
             pltpu.VMEM((2, PLANES, HALO, cols), jnp.float32),
@@ -440,22 +459,24 @@
         input_output_aliases={0: 0},
         compiler_params=pltpu.CompilerParams(vmem_limit_bytes=2 * 2**20),
     )(
-        bulk, north_edge, south_edge, north_corners, south_corners, total.reshape(flat), probe_modes.reshape(flat)
+        bulk, north_edge, south_edge, north_corners, south_corners, mine, other, probe_modes.reshape(flat), core
     )
     return object_grad.reshape(object_tiles.shape), probe_new.reshape(probe_modes.shape)
 
 
 def solution(mesh):
+    names = ("row",) + COL
+    split_mesh = jax.sharding.Mesh(mesh.devices.reshape(mesh.shape["row"], -1, 2), names)
     placed = (
-        P(None, None, "row", "col"),
+        P(None, None, "row", COL),
         P(),
-        P("row", "col", None, None),
-        P("row", "col", None, None, None),
+        P("row", COL, None, None),
+        P("row", COL, None, None, None),
     )
     return jax.shard_map(
         on_device,
-        mesh=mesh,
+        mesh=split_mesh,
         in_specs=placed,
-        out_specs=(P(None, None, "row", "col"), P()),
+        out_specs=(P(None, None, "row", COL), P()),
         check_vma=False,
     )

time: 73.1 us -> 72.6 us (level)
  waiting for transfers between devices: 23 us -> 16.2 us
  starting transfers between devices: 34.7 us -> 40.5 us
    ppermute x0 -> x2, starting transfers between devices: none -> 6.17 us  [the longest x1 4.16 us: on_device(): other = lax.ppermute(mine, 'core', SWAP)]
    ppermute x12, waiting for transfers between devices: 12.9 us -> 7.91 us  [moved(): lax.ppermute(block, axis, [(i, (i + distance) % count) for i in range(cou...]
    all_to_all x2, waiting for transfers between devices: 10.1 us -> 7.1 us  [the longest x1 4.16 us: on_device(): lax.all_to_all(share, PEERS, 0, 0, tiled=True).reshape(MODES * WIN, WIN)]
    ppermute x0 -> x2, waiting for transfers between devices: none -> 1.16 us  [the longest x1 1.16 us: on_device(): got = lax.ppermute(send, 'core', SWAP)]
    pallas_call x3 -> x4, Pallas kernels: 9.58 us -> 10.1 us  [the longest x1 8.08 us: main_call(): return lambda *args: run(*args)[:7]]
  transfers between devices with their start and end apart: 14 -> 16, of which waited for: 6 -> 6; matrix products, arithmetic and copies ran while one was open for 0% -> 0% of each run, Pallas kernels for 4% -> 3%
where the time goes in v8:
time: 72.6 us; the launch traced here: 72.3 us
  starting transfers between devices  40.5 us (56%)
  waiting for transfers between devices  16.2 us (22%)
  Pallas kernels  12.4 us (17%)
  local copies, waits for them, and re-layouts  2.24 us (3%)
  between operations  0.95 us (1%)
    ppermute x12, starting transfers between devices, moved(): lax.ppermute(block, axis, [(i, (i + distance) % count) for i in range(cou...  21.7 us
    pallas_call x1, Pallas kernels, main_call(): return lambda *args: run(*args)[:7]  8.08 us
    all_to_all x1, starting transfers between devices, on_device(): lax.all_to_all(half_sum.reshape(axis_count(PEERS), -1, LANES), PEERS, 0,...  8.02 us
    ppermute x12, waiting for transfers between devices, moved(): lax.ppermute(block, axis, [(i, (i + distance) % count) for i in range(cou...  7.91 us
    all_to_all x1, starting transfers between devices, on_device(): lax.all_to_all(share, PEERS, 0, 0, tiled=True).reshape(MODES * WIN, WIN)  4.64 us
    ppermute x1, starting transfers between devices, on_device(): other = lax.ppermute(mine, 'core', SWAP)  4.16 us
    all_to_all x1, waiting for transfers between devices, on_device(): lax.all_to_all(share, PEERS, 0, 0, tiled=True).reshape(MODES * WIN, WIN)  4.16 us
    all_to_all x1, waiting for transfers between devices, on_device(): lax.all_to_all(half_sum.reshape(axis_count(PEERS), -1, LANES), PEERS, 0,...  2.95 us
  transfers between devices with their start and end apart: 16, of which 6 were waited for; matrix products, arithmetic and copies ran while one was open for 0% of the time, Pallas kernels for 3%

profile of v8, /device:TPU:1, one launch (start us, length us, event | category | flops | bytes accessed | tf_op | source)
XLA Modules:
  0.0 72.3 jit_solution(861316683437971398)
XLA Ops:
  0.6 1.0 %fusion = (f32[4,32,256]{2,1,0:T(8,128)S(1)}, f32[4,32,256]{2,1,0:T(8,128)S(1)}) fusion(f32[4,256,256]{2,1,0:T(8,128)} %bitcast.14), kind=kLoop, calls=%fused_computation | loop fusion | bytes 524288 | tf_op jit(solution)/shard_map/slice | solution.py:418
  1.6 6.1 %collective-permute-start.1 = (f32[4,32,256]{2,1,0:T(8,128)S(1)}, f32[4,32,256]{2,1,0:T(8,128)S(1)}, u32[]{:S(2)}, u32[]{:S(2)}) collective-permute-start(f32[4,32,256]{2,1,0:T(8,128)S(1)} %get-tuple-element.38), channel_id=1, source_target_pairs={{0,112},{16,0},{32,16},{48,32},{64,48},{80,64},{96,80},{112,96},{1... | collective-permute-start | bytes 393224 | tf_op jit(solution)/shard_map/ppermute | solution.py:362
  7.7 0.0 collective-permute-start
  7.7 0.0 copy-start.2
  7.7 1.2 %copy-done.2 = f32[2,2,256,256]{3,2,1,0:T(8,128)S(1)} copy-done((f32[2,2,256,256]{3,2,1,0:T(8,128)S(1)}, f32[2,2,256,256]{3,2,1,0:T(8,128)}, u32[]{:S(2)}) %copy-start.2) | copy-done | bytes 1048600
  8.9 0.3 shard_map.69
  9.2 0.0 copy-start.3
  9.2 1.2 %collective-permute-start.2 = (f32[256,128]{1,0:T(8,128)S(1)}, f32[256,128]{1,0:T(8,128)S(1)}, u32[]{:S(2)}, u32[]{:S(2)}) collective-permute-start(f32[256,128]{1,0:T(8,128)S(1)} %get-tuple-element.20), channel_id=1, source_target_pairs={{0,1},{1,2},{2,3},{3,4},{4,5},{5,6},{6,7},{7,8},{8,9},{9,10},{10,1... | collective-permute-start | bytes 393224 | tf_op jit(solution)/shard_map/ppermute | solution.py:362
  10.5 0.0 collective-permute-start.3
  10.5 0.0 collective-permute-done.1.south_ref
  10.5 4.7 %collective-permute-done.north_ref = f32[4,32,256]{2,1,0:T(8,128)S(1)} collective-permute-done((f32[4,32,256]{2,1,0:T(8,128)S(1)}, f32[4,32,256]{2,1,0:T(8,128)S(1)}, u32[]{:S(2)}, u32[]{:S(2)}) %collective-permute-start) | collective-permute-done | bytes 131104 | tf_op jit(solution)/shard_map/ppermute | solution.py:362
  15.2 0.1 shard_map.70
  15.3 2.4 %collective-permute-start.4 = (f32[64,128]{1,0:T(8,128)S(1)}, f32[64,128]{1,0:T(8,128)S(1)}, u32[]{:S(2)}, u32[]{:S(2)}) collective-permute-start(f32[64,128]{1,0:T(8,128)S(1)} %get-tuple-element.22), channel_id=1, source_target_pairs={{0,1},{1,2},{2,3},{3,4},{4,5},{5,6},{6,7},{7,8},{8,9},{9,10},{10,1... | collective-permute-start | bytes 98312 | tf_op jit(solution)/shard_map/ppermute | solution.py:362
  17.6 0.0 copy-start
  17.6 0.0 copy-start.4
  17.7 0.0 copy-start.5
  17.7 0.0 copy-start.6
  17.7 0.1 collective-permute-start.5
  17.7 0.0 copy-done.3
  17.8 0.1 shard_map.68.ext_in
  17.8 0.0 collective-permute-done.2.from_west_ref
  17.9 0.0 collective-permute-done.3.from_east_ref
  17.9 0.8 %collective-permute-done.4.west_corners_ref = f32[64,128]{1,0:T(8,128)S(1)} collective-permute-done((f32[64,128]{1,0:T(8,128)S(1)}, f32[64,128]{1,0:T(8,128)S(1)}, u32[]{:S(2)}, u32[]{:S(2)}) %collective-permute-start.4) | collective-permute-done | bytes 32800 | tf_op jit(solution)/shard_map/ppermute | solution.py:362
  18.7 2.4 %collective-permute-done.5.east_corners_ref = f32[64,128]{1,0:T(8,128)S(1)} collective-permute-done((f32[64,128]{1,0:T(8,128)S(1)}, f32[64,128]{1,0:T(8,128)S(1)}, u32[]{:S(2)}, u32[]{:S(2)}) %collective-permute-start.5) | collective-permute-done | bytes 32800 | tf_op jit(solution)/shard_map/ppermute | solution.py:362
  21.1 0.0 copy-done
  21.1 0.0 copy-done.4
  21.1 0.0 copy-done.5
  21.1 0.0 copy-done.6
  21.1 8.1 %shard_map.71 = (f32[4,128,128]{2,1,0:T(8,128)S(1)}, f32[4,128,128]{2,1,0:T(8,128)S(1)}, f32[4,256,256]{2,1,0:T(8,128)S(1)}, f32[4,32,256]{2,1,0:T(8,128)S(1)}, ...) custom-call(s32[2,3]{1,0:T(2,128)S(1)} %bitcast.18, ...), custom_call_target="tpu_custom_call", output_to_operand_aliasing={{7}: (2, {})} | custom-call | flops 12000000000 | bytes 36000000 | tf_op jit(solution)/shard_map/pallas_call | solution.py:403
  29.2 2.0 %collective-permute-start.12 = (f32[4,128,128]{2,1,0:T(8,128)S(1)}, f32[4,128,128]{2,1,0:T(8,128)S(1)}, u32[]{:S(2)}, u32[]{:S(2)}) collective-permute-start(f32[4,128,128]{2,1,0:T(8,128)S(1)} %get-tuple-element.35), channel_id=1, source_target_pairs={{0,1},{1,0},{2,3},{3,2},{4,5},{5,4},{6,7},{7,6},{8,9},{9,8},{10,11... | collective-permute-start | bytes 786440 | tf_op jit(solution)/shard_map/ppermute | solution.py:431
  31.2 1.2 %collective-permute-done.12.right_ref = f32[4,128,128]{2,1,0:T(8,128)S(1)} collective-permute-done((f32[4,128,128]{2,1,0:T(8,128)S(1)}, f32[4,128,128]{2,1,0:T(8,128)S(1)}, u32[]{:S(2)}, u32[]{:S(2)}) %collective-permute-start.12) | collective-permute-done | bytes 262176 | tf_op jit(solution)/shard_map/ppermute | solution.py:431
  32.3 0.7 %shard_map.74 = f32[4,128,128]{2,1,0:T(8,128)} custom-call(f32[4,128,128]{2,1,0:T(8,128)S(1)} %get-tuple-element.34.left_ref, f32[4,128,128]{2,1,0:T(8,128)S(1)} %collective-permute-done.12.right_ref), custom_call_target="tpu_custom_call" | custom-call | tf_op jit(solution)/shard_map/pallas_call | solution.py:432
  33.1 8.0 %all-to-all-start = ((f32[64,8,128]{2,1,0:T(8,128)}), f32[64,8,128]{2,1,0:T(8,128)S(1)}, u32[]{:S(2)}, u32[]{:S(2)}) async-start(f32[64,8,128]{2,1,0:T(8,128)} %bitcast.5), calls=%async_computation | async-start | bytes 524288 | tf_op jit(solution)/shard_map/all_to_all | solution.py:433
  41.1 1.7 %collective-permute-start.8 = (f32[320,128]{1,0:T(8,128)S(1)}, f32[320,128]{1,0:T(8,128)S(1)}, u32[]{:S(2)}, u32[]{:S(2)}) collective-permute-start(f32[320,128]{1,0:T(8,128)S(1)} %get-tuple-element.27), channel_id=1, source_target_pairs={{0,1},{1,2},{2,3},{3,4},{4,5},{5,6},{6,7},{7,8},{8,9},{9,10},{10,1... | collective-permute-start | bytes 491528 | tf_op jit(solution)/shard_map/ppermute | solution.py:362
  42.8 0.0 collective-permute-start.9
  42.8 2.4 %collective-permute-start.6 = (f32[4,32,256]{2,1,0:T(8,128)S(1)}, f32[4,32,256]{2,1,0:T(8,128)S(1)}, u32[]{:S(2)}, u32[]{:S(2)}) collective-permute-start(f32[4,32,256]{2,1,0:T(8,128)S(1)} %get-tuple-element.25), channel_id=1, source_target_pairs={{0,16},{16,32},{32,48},{48,64},{64,80},{80,96},{96,112},{112,0},{1... | collective-permute-start | bytes 393224 | tf_op jit(solution)/shard_map/ppermute | solution.py:362
  45.2 2.7 %collective-permute-start.7 = (f32[4,32,256]{2,1,0:T(8,128)S(1)}, f32[4,32,256]{2,1,0:T(8,128)S(1)}, u32[]{:S(2)}, u32[]{:S(2)}) collective-permute-start(f32[4,32,256]{2,1,0:T(8,128)S(1)} %get-tuple-element.26), channel_id=1, source_target_pairs={{0,112},{16,0},{32,16},{48,32},{64,48},{80,64},{96,80},{112,96},{1... | collective-permute-start | bytes 393224 | tf_op jit(solution)/shard_map/ppermute | solution.py:362
  47.9 2.9 %all-to-all-done.parts_ref = f32[64,8,128]{2,1,0:T(8,128)S(1)} async-done(((f32[64,8,128]{2,1,0:T(8,128)}), f32[64,8,128]{2,1,0:T(8,128)S(1)}, u32[]{:S(2)}, u32[]{:S(2)}) %all-to-all-start) | async-done | bytes 262176 | tf_op jit(solution)/shard_map/all_to_all | solution.py:433
  50.8 0.8 %shard_map.75 = f32[64,8,128]{2,1,0:T(8,128)} custom-call(f32[64,8,128]{2,1,0:T(8,128)S(1)} %all-to-all-done.parts_ref), custom_call_target="tpu_custom_call" | custom-call | tf_op jit(solution)/shard_map/pallas_call | solution.py:438
  51.6 4.6 %all-to-all-start.1 = ((f32[64,8,128]{2,1,0:T(8,128)}), f32[64,8,128]{2,1,0:T(8,128)S(1)}, u32[]{:S(2)}, u32[]{:S(2)}) async-start(f32[64,8,128]{2,1,0:T(8,128)} %shard_map.75), calls=%async_computation.1 | async-start | bytes 524288 | tf_op jit(solution)/shard_map/all_to_all | solution.py:439
  56.3 0.0 collective-permute-done.8.from_west_ref
  56.3 0.0 collective-permute-done.9.from_east_ref
  56.3 2.6 %collective-permute-start.10 = (f32[64,128]{1,0:T(8,128)S(1)}, f32[64,128]{1,0:T(8,128)S(1)}, u32[]{:S(2)}, u32[]{:S(2)}) collective-permute-start(f32[64,128]{1,0:T(8,128)S(1)} %get-tuple-element.32), channel_id=1, source_target_pairs={{0,16},{16,32},{32,48},{48,64},{64,80},{80,96},{96,112},{112,0},{1... | collective-permute-start | bytes 98312 | tf_op jit(solution)/shard_map/ppermute | solution.py:362
  58.9 2.6 %collective-permute-start.11 = (f32[64,128]{1,0:T(8,128)S(1)}, f32[64,128]{1,0:T(8,128)S(1)}, u32[]{:S(2)}, u32[]{:S(2)}) collective-permute-start(f32[64,128]{1,0:T(8,128)S(1)} %get-tuple-element.33), channel_id=1, source_target_pairs={{0,112},{16,0},{32,16},{48,32},{64,48},{80,64},{96,80},{112,96},{1... | collective-permute-start | bytes 98312 | tf_op jit(solution)/shard_map/ppermute | solution.py:362
  61.4 4.2 %all-to-all-done.1 = f32[64,8,128]{2,1,0:T(8,128)S(1)} async-done(((f32[64,8,128]{2,1,0:T(8,128)}), f32[64,8,128]{2,1,0:T(8,128)S(1)}, u32[]{:S(2)}, u32[]{:S(2)}) %all-to-all-start.1) | async-done | bytes 262176 | tf_op jit(solution)/shard_map/all_to_all | solution.py:439
  65.6 4.2 %collective-permute-start.13 = (f32[512,128]{1,0:T(8,128)S(1)}, f32[512,128]{1,0:T(8,128)S(1)}, u32[]{:S(2)}, u32[]{:S(2)}) collective-permute-start(f32[512,128]{1,0:T(8,128)S(1)} %bitcast.11), channel_id=1, source_target_pairs={{0,1},{1,0},{2,3},{3,2},{4,5},{5,4},{6,7},{7,6},{8,9},{9,8},{10,11... | collective-permute-start | bytes 786440 | tf_op jit(solution)/shard_map/ppermute | solution.py:440
  69.8 0.0 collective-permute-done.6.from_north_ref
  69.8 0.0 collective-permute-done.7.from_south_ref
  69.8 0.0 copy-start.1
  69.8 1.2 %shard_map.72 = (f32[4,256,256]{2,1,0:T(8,128)}, f32[4,32,256]{2,1,0:T(8,128)S(1)}, f32[4,32,256]{2,1,0:T(8,128)S(1)}) custom-call(f32[4,256,256]{2,1,0:T(8,128)S(1)} %get-tuple-element.24.center_ref, f32[4,32,256]{2,1,0:T(8,128)S(1)} %collective-permute-done.6.from_north_ref, f32[4,32,256]{2,1,0:T(8,128)S(1)} %collective-permute-done.7.from_south_ref, ...), custom_call_target="tpu_custom_call" | custom-call | flops 80000000000 | bytes 240000000 | tf_op jit(solution)/shard_map/pallas_call | solution.py:445
  71.0 0.0 collective-permute-done.10.north_corners_ref
  71.0 0.0 collective-permute-done.11.south_corners_ref
  71.0 0.0 collective-permute-done.13.other_ref
  71.0 0.0 copy-done.1
  71.0 1.1 %shard_map.76 = (f32[4,256,256]{2,1,0:T(8,128)}, f32[2,512,128]{2,1,0:T(8,128)}) custom-call(f32[4,256,256]{2,1,0:T(8,128)} %get-tuple-element.29.object_in, f32[4,32,256]{2,1,0:T(8,128)S(1)} %get-tuple-element.30.north_ref, f32[4,32,256]{2,1,0:T(8,128)S(1)} %get-tuple-element.31.south_ref, ...), custom_call_target="tpu_custom_call", output_to_operand_aliasing={{0}: (0, {})} | custom-call | tf_op jit(solution)/shard_map/pallas_call | solution.py:449
  (1 shorter events, 0.0 us)
Async XLA Ops:
  1.6 8.8 %collective-permute-start.1 = (f32[4,32,256]{2,1,0:T(8,128)S(1)}, f32[4,32,256]{2,1,0:T(8,128)S(1)}, u32[]{:S(2)}, u32[]{:S(2)}) collective-permute-start(f32[4,32,256]{2,1,0:T(8,128)S(1)} %get-tuple-element.38), channel_id=1, source_target_pairs={{0,112},{16,0},{32,16},{48,32},{64,48},{80,64},{96,80},{112,96},{1... | collective-permute-start | bytes 393224 | tf_op jit(solution)/shard_map/ppermute | solution.py:362
  7.7 7.4 %collective-permute-start = (f32[4,32,256]{2,1,0:T(8,128)S(1)}, f32[4,32,256]{2,1,0:T(8,128)S(1)}, u32[]{:S(2)}, u32[]{:S(2)}) collective-permute-start(f32[4,32,256]{2,1,0:T(8,128)S(1)} %get-tuple-element.39), channel_id=1, source_target_pairs={{0,16},{16,32},{32,48},{48,64},{64,80},{80,96},{96,112},{112,0},{1... | collective-permute-start | bytes 393224 | tf_op jit(solution)/shard_map/ppermute | solution.py:362
  7.7 1.2 %copy-start.2 = (f32[2,2,256,256]{3,2,1,0:T(8,128)S(1)}, f32[2,2,256,256]{3,2,1,0:T(8,128)}, u32[]{:S(2)}) copy-start(f32[2,2,256,256]{3,2,1,0:T(8,128)} %param.5) | copy-start | bytes 3145732
  9.2 8.5 %copy-start.3 = (f32[2,2,256,256]{3,2,1,0:T(8,128)S(1)}, f32[2,2,256,256]{3,2,1,0:T(8,128)}, u32[]{:S(2)}) copy-start(f32[2,2,256,256]{3,2,1,0:T(8,128)} %param.5) | copy-start | bytes 3145732
  9.2 8.6 %collective-permute-start.2 = (f32[256,128]{1,0:T(8,128)S(1)}, f32[256,128]{1,0:T(8,128)S(1)}, u32[]{:S(2)}, u32[]{:S(2)}) collective-permute-start(f32[256,128]{1,0:T(8,128)S(1)} %get-tuple-element.20), channel_id=1, source_target_pairs={{0,1},{1,2},{2,3},{3,4},{4,5},{5,6},{6,7},{7,8},{8,9},{9,10},{10,1... | collective-permute-start | bytes 393224 | tf_op jit(solution)/shard_map/ppermute | solution.py:362
  10.5 7.4 %collective-permute-start.3 = (f32[256,128]{1,0:T(8,128)S(1)}, f32[256,128]{1,0:T(8,128)S(1)}, u32[]{:S(2)}, u32[]{:S(2)}) collective-permute-start(f32[256,128]{1,0:T(8,128)S(1)} %get-tuple-element.21), channel_id=1, source_target_pairs={{0,15},{1,0},{2,1},{3,2},{4,3},{5,4},{6,5},{7,6},{8,7},{9,8},{10,9... | collective-permute-start | bytes 393224 | tf_op jit(solution)/shard_map/ppermute | solution.py:362
  15.3 3.4 %collective-permute-start.4 = (f32[64,128]{1,0:T(8,128)S(1)}, f32[64,128]{1,0:T(8,128)S(1)}, u32[]{:S(2)}, u32[]{:S(2)}) collective-permute-start(f32[64,128]{1,0:T(8,128)S(1)} %get-tuple-element.22), channel_id=1, source_target_pairs={{0,1},{1,2},{2,3},{3,4},{4,5},{5,6},{6,7},{7,8},{8,9},{9,10},{10,1... | collective-permute-start | bytes 98312 | tf_op jit(solution)/shard_map/ppermute | solution.py:362
  17.6 3.4 %copy-start = (f32[2,4,128,128]{3,2,1,0:T(8,128)S(1)}, f32[2,4,128,128]{3,2,1,0:T(8,128)}, u32[]{:S(2)}) copy-start(f32[2,4,128,128]{3,2,1,0:T(8,128)} %probe_ref.1) | copy-start | bytes 1572868
  17.6 3.4 %copy-start.4 = (f32[1,1,3,128,128]{4,3,2,1,0:T(8,128)S(1)}, f32[1,1,3,128,128]{4,3,2,1,0:T(8,128)}, u32[]{:S(2)}) copy-start(f32[1,1,3,128,128]{4,3,2,1,0:T(8,128)} %param.8) | copy-start | bytes 589828
  17.7 3.4 %copy-start.5 = (s32[1,1,3,2]{2,3,1,0:T(2,128)S(1)}, s32[1,1,3,2]{2,3,1,0:T(2,128)}, u32[]{:S(2)}) copy-start(s32[1,1,3,2]{2,3,1,0:T(2,128)} %param.7) | copy-start | bytes 76
  17.7 3.4 %copy-start.6 = (bf16[4,2,256,256]{3,2,1,0:T(8,128)(2,1)S(1)}, bf16[4,2,256,256]{3,2,1,0:T(8,128)(2,1)}, u32[]{:S(2)}) copy-start(bf16[4,2,256,256]{3,2,1,0:T(8,128)(2,1)} %constant.6.clone.mat_ref) | copy-start | bytes 3145732
  17.7 3.4 %collective-permute-start.5 = (f32[64,128]{1,0:T(8,128)S(1)}, f32[64,128]{1,0:T(8,128)S(1)}, u32[]{:S(2)}, u32[]{:S(2)}) collective-permute-start(f32[64,128]{1,0:T(8,128)S(1)} %get-tuple-element.23), channel_id=1, source_target_pairs={{0,15},{1,0},{2,1},{3,2},{4,3},{5,4},{6,5},{7,6},{8,7},{9,8},{10,9... | collective-permute-start | bytes 98312 | tf_op jit(solution)/shard_map/ppermute | solution.py:362
  29.2 3.2 %collective-permute-start.12 = (f32[4,128,128]{2,1,0:T(8,128)S(1)}, f32[4,128,128]{2,1,0:T(8,128)S(1)}, u32[]{:S(2)}, u32[]{:S(2)}) collective-permute-start(f32[4,128,128]{2,1,0:T(8,128)S(1)} %get-tuple-element.35), channel_id=1, source_target_pairs={{0,1},{1,0},{2,3},{3,2},{4,5},{5,4},{6,7},{7,6},{8,9},{9,8},{10,11... | collective-permute-start | bytes 786440 | tf_op jit(solution)/shard_map/ppermute | solution.py:431
  33.1 17.7 %all-to-all-start = ((f32[64,8,128]{2,1,0:T(8,128)}), f32[64,8,128]{2,1,0:T(8,128)S(1)}, u32[]{:S(2)}, u32[]{:S(2)}) async-start(f32[64,8,128]{2,1,0:T(8,128)} %bitcast.5), calls=%async_computation | async-start | bytes 524288 | tf_op jit(solution)/shard_map/all_to_all | solution.py:433
  41.1 15.1 %collective-permute-start.8 = (f32[320,128]{1,0:T(8,128)S(1)}, f32[320,128]{1,0:T(8,128)S(1)}, u32[]{:S(2)}, u32[]{:S(2)}) collective-permute-start(f32[320,128]{1,0:T(8,128)S(1)} %get-tuple-element.27), channel_id=1, source_target_pairs={{0,1},{1,2},{2,3},{3,4},{4,5},{5,6},{6,7},{7,8},{8,9},{9,10},{10,1... | collective-permute-start | bytes 491528 | tf_op jit(solution)/shard_map/ppermute | solution.py:362
  42.8 13.5 %collective-permute-start.9 = (f32[320,128]{1,0:T(8,128)S(1)}, f32[320,128]{1,0:T(8,128)S(1)}, u32[]{:S(2)}, u32[]{:S(2)}) collective-permute-start(f32[320,128]{1,0:T(8,128)S(1)} %get-tuple-element.28), channel_id=1, source_target_pairs={{0,15},{1,0},{2,1},{3,2},{4,3},{5,4},{6,5},{7,6},{8,7},{9,8},{10,9... | collective-permute-start | bytes 491528 | tf_op jit(solution)/shard_map/ppermute | solution.py:362
  42.8 27.0 %collective-permute-start.6 = (f32[4,32,256]{2,1,0:T(8,128)S(1)}, f32[4,32,256]{2,1,0:T(8,128)S(1)}, u32[]{:S(2)}, u32[]{:S(2)}) collective-permute-start(f32[4,32,256]{2,1,0:T(8,128)S(1)} %get-tuple-element.25), channel_id=1, source_target_pairs={{0,16},{16,32},{32,48},{48,64},{64,80},{80,96},{96,112},{112,0},{1... | collective-permute-start | bytes 393224 | tf_op jit(solution)/shard_map/ppermute | solution.py:362
  45.2 24.6 %collective-permute-start.7 = (f32[4,32,256]{2,1,0:T(8,128)S(1)}, f32[4,32,256]{2,1,0:T(8,128)S(1)}, u32[]{:S(2)}, u32[]{:S(2)}) collective-permute-start(f32[4,32,256]{2,1,0:T(8,128)S(1)} %get-tuple-element.26), channel_id=1, source_target_pairs={{0,112},{16,0},{32,16},{48,32},{64,48},{80,64},{96,80},{112,96},{1... | collective-permute-start | bytes 393224 | tf_op jit(solution)/shard_map/ppermute | solution.py:362
  51.6 14.0 %all-to-all-start.1 = ((f32[64,8,128]{2,1,0:T(8,128)}), f32[64,8,128]{2,1,0:T(8,128)S(1)}, u32[]{:S(2)}, u32[]{:S(2)}) async-start(f32[64,8,128]{2,1,0:T(8,128)} %shard_map.75), calls=%async_computation.1 | async-start | bytes 524288 | tf_op jit(solution)/shard_map/all_to_all | solution.py:439
  56.3 14.7 %collective-permute-start.10 = (f32[64,128]{1,0:T(8,128)S(1)}, f32[64,128]{1,0:T(8,128)S(1)}, u32[]{:S(2)}, u32[]{:S(2)}) collective-permute-start(f32[64,128]{1,0:T(8,128)S(1)} %get-tuple-element.32), channel_id=1, source_target_pairs={{0,16},{16,32},{32,48},{48,64},{64,80},{80,96},{96,112},{112,0},{1... | collective-permute-start | bytes 98312 | tf_op jit(solution)/shard_map/ppermute | solution.py:362
  58.9 12.1 %collective-permute-start.11 = (f32[64,128]{1,0:T(8,128)S(1)}, f32[64,128]{1,0:T(8,128)S(1)}, u32[]{:S(2)}, u32[]{:S(2)}) collective-permute-start(f32[64,128]{1,0:T(8,128)S(1)} %get-tuple-element.33), channel_id=1, source_target_pairs={{0,112},{16,0},{32,16},{48,32},{64,48},{80,64},{96,80},{112,96},{1... | collective-permute-start | bytes 98312 | tf_op jit(solution)/shard_map/ppermute | solution.py:362
  65.6 5.4 %collective-permute-start.13 = (f32[512,128]{1,0:T(8,128)S(1)}, f32[512,128]{1,0:T(8,128)S(1)}, u32[]{:S(2)}, u32[]{:S(2)}) collective-permute-start(f32[512,128]{1,0:T(8,128)S(1)} %bitcast.11), channel_id=1, source_target_pairs={{0,1},{1,0},{2,3},{3,2},{4,5},{5,4},{6,7},{7,6},{8,9},{9,8},{10,11... | collective-permute-start | bytes 786440 | tf_op jit(solution)/shard_map/ppermute | solution.py:440
  69.8 1.3 %copy-start.1 = (f32[2,4,128,128]{3,2,1,0:T(8,128)S(1)}, f32[2,4,128,128]{3,2,1,0:T(8,128)}, u32[]{:S(2)}) copy-start(f32[2,4,128,128]{3,2,1,0:T(8,128)} %probe_ref.1) | copy-start | bytes 1572868

commit v9 on v7

--- a/solution.py
+++ b/solution.py
@@ -93,8 +93,8 @@
 
 def main_kernel(
     offsets_ref, ext_in, from_west_ref, from_east_ref, west_corners_ref, east_corners_ref, amp_ref, probe_ref, mat_ref,
-    probe_grad_ref, center_ref, north_rim_ref, south_rim_ref, east_rim_ref, west_rim_ref, ext,
-    rh, rl, lh, ll, field, d_keep, win, factor, grad,
+    probe_out_ref, center_ref, north_rim_ref, south_rim_ref, east_rim_ref, west_rim_ref, ext,
+    rh, rl, lh, ll, field, d_keep, win, factor, grad, probe_grad_ref, sem,
 ):
     del ext_in
     ext_rows = ext.shape[2]
@@ -115,6 +115,9 @@
 
     def put(high, low, at, value):
         high[at], low[at] = split(value)
+
+    def write(part, m):
+        return pltpu.make_async_copy(probe_grad_ref.at[part, m], probe_out_ref.at[part, m], sem.at[part * MODES + m])
 
     def run(*accs):
         def blocks(s, c):
@@ -243,6 +246,9 @@
                 grad_i = first_r * imag - first_i * real
                 probe_grad_ref[0, m] = grad_r if s == 0 else probe_grad_ref[0, m] + grad_r
                 probe_grad_ref[1, m] = grad_i if s == 0 else probe_grad_ref[1, m] + grad_i
+                if s == scans[-1]:
+                    for part in range(2):
+                        write(part, m).start()
             scatter(0, sum_r)
             scatter(2, sum_i)
 
@@ -269,6 +275,9 @@
         west = jnp.where(here, turned(third, (p - 3) * HALO), west)
     east_rim_ref[...] = east
     west_rim_ref[...] = west
+    for part in range(2):
+        for m in range(MODES):
+            write(part, m).wait()
 
 
 def rim_corner_kernel(from_west_ref, from_east_ref, to_north_ref, to_south_ref):
@@ -277,9 +286,17 @@
         to_south_ref[k * HALO : (k + 1) * HALO, :] = ref[ref.shape[0] - HALO :, :]
 
 
-def share_kernel(parts_ref, *refs):
-    share_ref = refs[-1]
-    share_ref[...] = jnp.broadcast_to(jnp.sum(parts_ref[...], axis=0)[None], share_ref.shape)
+def share_kernel(parts_ref, share_ref, block, sem):
+    repeats = block.shape[0]
+    block[...] = jnp.broadcast_to(jnp.sum(parts_ref[...], axis=0)[None], block.shape)
+    copies = [
+        pltpu.make_async_copy(block, share_ref.at[k * repeats : (k + 1) * repeats], sem.at[k])
+        for k in range(share_ref.shape[0] // repeats)
+    ]
+    for copy in copies:
+        copy.start()
+    for copy in copies:
+        copy.wait()
 
 
 def from_sides(left, right, p):
@@ -373,12 +390,14 @@
         main_kernel,
         out_shape=outs,
         in_specs=[pl.BlockSpec(memory_space=pltpu.SMEM)] + vmem(8),
-        out_specs=vmem(len(outs)),
+        out_specs=[pl.BlockSpec(memory_space=pl.ANY)] + vmem(len(outs) - 1),
         scratch_shapes=[
             pair, pair, pair, pair, modes, modes,
             pltpu.VMEM((scans, PLANES, WIN, WIN), jnp.float32),
             pltpu.VMEM((scans, WIN, WIN), jnp.float32),
             pltpu.VMEM((PLANES, 3, ext_rows, LANES), jnp.float32),
+            pltpu.VMEM((2, MODES, WIN, WIN), jnp.float32),
+            pltpu.SemaphoreType.DMA((2 * MODES,)),
         ],
         input_output_aliases={1: 6},
         compiler_params=pltpu.CompilerParams(vmem_limit_bytes=24 * 2**20),
@@ -398,6 +417,7 @@
     mats = jnp.asarray(matrices())
     devices = lax.axis_size("row") * lax.axis_size("col")
 
+    anywhere = pl.BlockSpec(memory_space=pl.ANY)
     north = moved(tile[:, rows - HALO :], "row", 1)
     south = moved(tile[:, :HALO], "row", -1)
     east_send, west_send = call(pack_kernel, [f32(rows, LANES)] * 2, 1, us=1)(tile)
@@ -417,7 +437,17 @@
     rim_from_east = moved(west_rim, "col", -1)
     from_south = moved(north_rim, "row", -1)
     from_north = moved(south_rim, "row", 1)
-    share = call(share_kernel, f32(*parts.shape), 1)(parts)
+    share = pl.pallas_call(
+        share_kernel,
+        out_shape=f32(*parts.shape),
+        in_specs=vmem(1),
+        out_specs=anywhere,
+        scratch_shapes=[
+            pltpu.VMEM((devices // CHUNKS, *parts.shape[1:]), jnp.float32),
+            pltpu.SemaphoreType.DMA((CHUNKS,)),
+        ],
+        compiler_params=pltpu.CompilerParams(vmem_limit_bytes=2 * 2**20),
+    )(parts)
     total = lax.all_to_all(share, BOTH, 0, 0, tiled=True)
     to_north, to_south = call(rim_corner_kernel, [f32(2 * HALO, LANES)] * 2, 2, us=20)(rim_from_west, rim_from_east)
     south_corners = moved(to_north, "row", -1)
@@ -426,7 +456,6 @@
     bulk, north_edge, south_edge = call(object_kernel, [f32(PLANES, rows, cols), edge, edge], 5)(
         center, from_north, from_south, rim_from_west, rim_from_east
     )
-    anywhere = pl.BlockSpec(memory_space=pl.ANY)
     object_grad, probe_new = pl.pallas_call(
         final_kernel,
         out_shape=[f32(PLANES, rows, cols), f32(*flat)],

time: 73.1 us -> 73.2 us (level)
  no operation moved by 1% of the time
where the time goes in v9:
time: 73.2 us; the launch traced here: 72.9 us
  starting transfers between devices  34.8 us (48%)
  waiting for transfers between devices  23 us (31%)
  Pallas kernels  12.1 us (17%)
  local copies, waits for them, and re-layouts  2.24 us (3%)
  between operations  0.78 us (1%)
    ppermute x12, starting transfers between devices, moved(): lax.ppermute(block, axis, [(i, (i + distance) % count) for i in range(cou...  21.9 us
    ppermute x12, waiting for transfers between devices, moved(): lax.ppermute(block, axis, [(i, (i + distance) % count) for i in range(cou...  12.9 us
    all_to_all x1, starting transfers between devices, on_device(): lax.all_to_all(probe_grad.reshape(devices, -1, LANES), BOTH, 0, 0, tiled=...  8.54 us
    pallas_call x1, Pallas kernels, main_call(): return lambda *args: run(*args)[:6]  8.34 us
    all_to_all x1, waiting for transfers between devices, on_device(): lax.all_to_all(probe_grad.reshape(devices, -1, LANES), BOTH, 0, 0, tiled=...  7.41 us
    all_to_all x1, starting transfers between devices, on_device(): total = lax.all_to_all(share, BOTH, 0, 0, tiled=True)  4.31 us
    all_to_all x1, waiting for transfers between devices, on_device(): total = lax.all_to_all(share, BOTH, 0, 0, tiled=True)  2.68 us
  transfers between devices with their start and end apart: 14, of which 6 were waited for; matrix products, arithmetic and copies ran while one was open for 0% of the time, Pallas kernels for 4%

profile of v9, /device:TPU:1, one launch (start us, length us, event | category | flops | bytes accessed | tf_op | source)
XLA Modules:
  0.0 72.9 jit_solution(17508931024231764719)
XLA Ops:
  0.6 1.0 %fusion = (f32[4,32,256]{2,1,0:T(8,128)S(1)}, f32[4,32,256]{2,1,0:T(8,128)S(1)}) fusion(f32[4,256,256]{2,1,0:T(8,128)} %bitcast.12), kind=kLoop, calls=%fused_computation | loop fusion | bytes 524288 | tf_op jit(solution)/shard_map/slice | solution.py:422
  1.6 6.1 %collective-permute-start.1 = (f32[4,32,256]{2,1,0:T(8,128)S(1)}, f32[4,32,256]{2,1,0:T(8,128)S(1)}, u32[]{:S(2)}, u32[]{:S(2)}) collective-permute-start(f32[4,32,256]{2,1,0:T(8,128)S(1)} %get-tuple-element.36), channel_id=1, source_target_pairs={{0,112},{16,0},{32,16},{48,32},{64,48},{80,64},{96,80},{112,96},{1... | collective-permute-start | bytes 393224 | tf_op jit(solution)/shard_map/ppermute | solution.py:364
  7.7 0.0 collective-permute-start
  7.7 0.0 copy-start.1
  7.7 1.2 %copy-done.1 = f32[2,2,256,256]{3,2,1,0:T(8,128)S(1)} copy-done((f32[2,2,256,256]{3,2,1,0:T(8,128)S(1)}, f32[2,2,256,256]{3,2,1,0:T(8,128)}, u32[]{:S(2)}) %copy-start.1) | copy-done | bytes 1048600
  8.9 0.3 shard_map.69
  9.2 0.0 copy-start.2
  9.2 1.2 %collective-permute-start.2 = (f32[256,128]{1,0:T(8,128)S(1)}, f32[256,128]{1,0:T(8,128)S(1)}, u32[]{:S(2)}, u32[]{:S(2)}) collective-permute-start(f32[256,128]{1,0:T(8,128)S(1)} %get-tuple-element.19), channel_id=1, source_target_pairs={{0,1},{1,2},{2,3},{3,4},{4,5},{5,6},{6,7},{7,8},{8,9},{9,10},{10,1... | collective-permute-start | bytes 393224 | tf_op jit(solution)/shard_map/ppermute | solution.py:364
  10.5 0.0 collective-permute-start.3
  10.5 0.0 collective-permute-done.1.south_ref
  10.5 4.7 %collective-permute-done.north_ref = f32[4,32,256]{2,1,0:T(8,128)S(1)} collective-permute-done((f32[4,32,256]{2,1,0:T(8,128)S(1)}, f32[4,32,256]{2,1,0:T(8,128)S(1)}, u32[]{:S(2)}, u32[]{:S(2)}) %collective-permute-start) | collective-permute-done | bytes 131104 | tf_op jit(solution)/shard_map/ppermute | solution.py:364
  15.2 0.1 shard_map.70
  15.3 2.4 %collective-permute-start.4 = (f32[64,128]{1,0:T(8,128)S(1)}, f32[64,128]{1,0:T(8,128)S(1)}, u32[]{:S(2)}, u32[]{:S(2)}) collective-permute-start(f32[64,128]{1,0:T(8,128)S(1)} %get-tuple-element.21), channel_id=1, source_target_pairs={{0,1},{1,2},{2,3},{3,4},{4,5},{5,6},{6,7},{7,8},{8,9},{9,10},{10,1... | collective-permute-start | bytes 98312 | tf_op jit(solution)/shard_map/ppermute | solution.py:364
  17.6 0.0 copy-start
  17.6 0.0 copy-start.3
  17.7 0.0 copy-start.4
  17.7 0.0 copy-start.5
  17.7 0.1 collective-permute-start.5
  17.7 0.0 copy-done.2
  17.8 0.1 shard_map.68.ext_in
  17.8 0.0 collective-permute-done.2.from_west_ref
  17.9 0.0 collective-permute-done.3.from_east_ref
  17.9 0.8 %collective-permute-done.4.west_corners_ref = f32[64,128]{1,0:T(8,128)S(1)} collective-permute-done((f32[64,128]{1,0:T(8,128)S(1)}, f32[64,128]{1,0:T(8,128)S(1)}, u32[]{:S(2)}, u32[]{:S(2)}) %collective-permute-start.4) | collective-permute-done | bytes 32800 | tf_op jit(solution)/shard_map/ppermute | solution.py:364
  18.7 2.4 %collective-permute-done.5.east_corners_ref = f32[64,128]{1,0:T(8,128)S(1)} collective-permute-done((f32[64,128]{1,0:T(8,128)S(1)}, f32[64,128]{1,0:T(8,128)S(1)}, u32[]{:S(2)}, u32[]{:S(2)}) %collective-permute-start.5) | collective-permute-done | bytes 32800 | tf_op jit(solution)/shard_map/ppermute | solution.py:364
  21.1 0.0 copy-done
  21.1 0.0 copy-done.3
  21.1 0.0 copy-done.4
  21.1 0.0 copy-done.5
  21.1 8.3 %shard_map.71 = (f32[2,4,128,128]{3,2,1,0:T(8,128)}, f32[4,256,256]{2,1,0:T(8,128)S(1)}, f32[4,32,256]{2,1,0:T(8,128)S(1)}, f32[4,32,256]{2,1,0:T(8,128)S(1)}, f...) custom-call(s32[2,3]{1,0:T(2,128)S(1)} %bitcast.16, ...), custom_call_target="tpu_custom_call", output_to_operand_aliasing={{6}: (1, {})} | custom-call | flops 12000000000 | bytes 36000000 | tf_op jit(solution)/shard_map/pallas_call | solution.py:406
  29.4 8.5 %all-to-all-start = ((f32[128,8,128]{2,1,0:T(8,128)}), f32[128,8,128]{2,1,0:T(8,128)S(1)}, u32[]{:S(2)}, u32[]{:S(2)}) async-start(f32[128,8,128]{2,1,0:T(8,128)} %bitcast.4), calls=%async_computation | async-start | bytes 1048576 | tf_op jit(solution)/shard_map/all_to_all | solution.py:435
  38.0 1.7 %collective-permute-start.8 = (f32[320,128]{1,0:T(8,128)S(1)}, f32[320,128]{1,0:T(8,128)S(1)}, u32[]{:S(2)}, u32[]{:S(2)}) collective-permute-start(f32[320,128]{1,0:T(8,128)S(1)} %get-tuple-element.26), channel_id=1, source_target_pairs={{0,1},{1,2},{2,3},{3,4},{4,5},{5,6},{6,7},{7,8},{8,9},{9,10},{10,1... | collective-permute-start | bytes 491528 | tf_op jit(solution)/shard_map/ppermute | solution.py:364
  39.7 0.0 collective-permute-start.9
  39.7 2.4 %collective-permute-start.6 = (f32[4,32,256]{2,1,0:T(8,128)S(1)}, f32[4,32,256]{2,1,0:T(8,128)S(1)}, u32[]{:S(2)}, u32[]{:S(2)}) collective-permute-start(f32[4,32,256]{2,1,0:T(8,128)S(1)} %get-tuple-element.24), channel_id=1, source_target_pairs={{0,16},{16,32},{32,48},{48,64},{64,80},{80,96},{96,112},{112,0},{1... | collective-permute-start | bytes 393224 | tf_op jit(solution)/shard_map/ppermute | solution.py:364
  42.1 2.7 %collective-permute-start.7 = (f32[4,32,256]{2,1,0:T(8,128)S(1)}, f32[4,32,256]{2,1,0:T(8,128)S(1)}, u32[]{:S(2)}, u32[]{:S(2)}) collective-permute-start(f32[4,32,256]{2,1,0:T(8,128)S(1)} %get-tuple-element.25), channel_id=1, source_target_pairs={{0,112},{16,0},{32,16},{48,32},{64,48},{80,64},{96,80},{112,96},{1... | collective-permute-start | bytes 393224 | tf_op jit(solution)/shard_map/ppermute | solution.py:364
  44.8 7.4 %all-to-all-done.parts_ref = f32[128,8,128]{2,1,0:T(8,128)S(1)} async-done(((f32[128,8,128]{2,1,0:T(8,128)}), f32[128,8,128]{2,1,0:T(8,128)S(1)}, u32[]{:S(2)}, u32[]{:S(2)}) %all-to-all-start) | async-done | bytes 524320 | tf_op jit(solution)/shard_map/all_to_all | solution.py:435
  52.2 1.0 %shard_map.74 = f32[128,8,128]{2,1,0:T(8,128)} custom-call(f32[128,8,128]{2,1,0:T(8,128)S(1)} %all-to-all-done.parts_ref), custom_call_target="tpu_custom_call" | custom-call | tf_op jit(solution)/shard_map/pallas_call | solution.py:440
  53.1 4.3 %all-to-all-start.1 = ((f32[128,8,128]{2,1,0:T(8,128)}), f32[128,8,128]{2,1,0:T(8,128)S(1)}, u32[]{:S(2)}, u32[]{:S(2)}) async-start(f32[128,8,128]{2,1,0:T(8,128)} %shard_map.74), calls=%async_computation.1 | async-start | bytes 1048576 | tf_op jit(solution)/shard_map/all_to_all | solution.py:451
  57.5 0.0 collective-permute-done.8.from_west_ref
  57.5 0.0 collective-permute-done.9.from_east_ref
  57.5 3.0 %collective-permute-start.10 = (f32[64,128]{1,0:T(8,128)S(1)}, f32[64,128]{1,0:T(8,128)S(1)}, u32[]{:S(2)}, u32[]{:S(2)}) collective-permute-start(f32[64,128]{1,0:T(8,128)S(1)} %get-tuple-element.31), channel_id=1, source_target_pairs={{0,16},{16,32},{32,48},{48,64},{64,80},{80,96},{96,112},{112,0},{1... | collective-permute-start | bytes 98312 | tf_op jit(solution)/shard_map/ppermute | solution.py:364
  60.5 2.4 %collective-permute-start.11 = (f32[64,128]{1,0:T(8,128)S(1)}, f32[64,128]{1,0:T(8,128)S(1)}, u32[]{:S(2)}, u32[]{:S(2)}) collective-permute-start(f32[64,128]{1,0:T(8,128)S(1)} %get-tuple-element.32), channel_id=1, source_target_pairs={{0,112},{16,0},{32,16},{48,32},{64,48},{80,64},{96,80},{112,96},{1... | collective-permute-start | bytes 98312 | tf_op jit(solution)/shard_map/ppermute | solution.py:364
  62.9 0.0 collective-permute-done.6.from_north_ref
  62.9 0.0 collective-permute-done.7.from_south_ref
  62.9 1.2 %shard_map.72 = (f32[4,256,256]{2,1,0:T(8,128)}, f32[4,32,256]{2,1,0:T(8,128)S(1)}, f32[4,32,256]{2,1,0:T(8,128)S(1)}) custom-call(f32[4,256,256]{2,1,0:T(8,128)S(1)} %get-tuple-element.23.center_ref, f32[4,32,256]{2,1,0:T(8,128)S(1)} %collective-permute-done.6.from_north_ref, f32[4,32,256]{2,1,0:T(8,128)S(1)} %collective-permute-done.7.from_south_ref, ...), custom_call_target="tpu_custom_call" | custom-call | tf_op jit(solution)/shard_map/pallas_call | solution.py:456
  64.1 5.0 %collective-permute-done.10.north_corners_ref = f32[64,128]{1,0:T(8,128)S(1)} collective-permute-done((f32[64,128]{1,0:T(8,128)S(1)}, f32[64,128]{1,0:T(8,128)S(1)}, u32[]{:S(2)}, u32[]{:S(2)}) %collective-permute-start.10) | collective-permute-done | bytes 32800 | tf_op jit(solution)/shard_map/ppermute | solution.py:364
  69.1 0.0 collective-permute-done.11.south_corners_ref
  69.1 2.7 %all-to-all-done.1 = f32[128,8,128]{2,1,0:T(8,128)S(1)} async-done(((f32[128,8,128]{2,1,0:T(8,128)}), f32[128,8,128]{2,1,0:T(8,128)S(1)}, u32[]{:S(2)}, u32[]{:S(2)}) %all-to-all-start.1) | async-done | bytes 524320 | tf_op jit(solution)/shard_map/all_to_all | solution.py:451
  71.8 1.1 %shard_map.75 = (f32[4,256,256]{2,1,0:T(8,128)}, f32[1024,128]{1,0:T(8,128)}) custom-call(f32[4,256,256]{2,1,0:T(8,128)} %get-tuple-element.28.object_in, f32[4,32,256]{2,1,0:T(8,128)S(1)} %get-tuple-element.29.north_ref, f32[4,32,256]{2,1,0:T(8,128)S(1)} %get-tuple-element.30.south_ref, ...), custom_call_target="tpu_custom_call", output_to_operand_aliasing={{0}: (0, {})} | custom-call | tf_op jit(solution)/shard_map/pallas_call | solution.py:459
  (1 shorter events, 0.0 us)
Async XLA Ops:
  1.6 8.8 %collective-permute-start.1 = (f32[4,32,256]{2,1,0:T(8,128)S(1)}, f32[4,32,256]{2,1,0:T(8,128)S(1)}, u32[]{:S(2)}, u32[]{:S(2)}) collective-permute-start(f32[4,32,256]{2,1,0:T(8,128)S(1)} %get-tuple-element.36), channel_id=1, source_target_pairs={{0,112},{16,0},{32,16},{48,32},{64,48},{80,64},{96,80},{112,96},{1... | collective-permute-start | bytes 393224 | tf_op jit(solution)/shard_map/ppermute | solution.py:364
  7.7 7.4 %collective-permute-start = (f32[4,32,256]{2,1,0:T(8,128)S(1)}, f32[4,32,256]{2,1,0:T(8,128)S(1)}, u32[]{:S(2)}, u32[]{:S(2)}) collective-permute-start(f32[4,32,256]{2,1,0:T(8,128)S(1)} %get-tuple-element.37), channel_id=1, source_target_pairs={{0,16},{16,32},{32,48},{48,64},{64,80},{80,96},{96,112},{112,0},{1... | collective-permute-start | bytes 393224 | tf_op jit(solution)/shard_map/ppermute | solution.py:364
  7.7 1.2 %copy-start.1 = (f32[2,2,256,256]{3,2,1,0:T(8,128)S(1)}, f32[2,2,256,256]{3,2,1,0:T(8,128)}, u32[]{:S(2)}) copy-start(f32[2,2,256,256]{3,2,1,0:T(8,128)} %param.5) | copy-start | bytes 3145732
  9.2 8.5 %copy-start.2 = (f32[2,2,256,256]{3,2,1,0:T(8,128)S(1)}, f32[2,2,256,256]{3,2,1,0:T(8,128)}, u32[]{:S(2)}) copy-start(f32[2,2,256,256]{3,2,1,0:T(8,128)} %param.5) | copy-start | bytes 3145732
  9.2 8.6 %collective-permute-start.2 = (f32[256,128]{1,0:T(8,128)S(1)}, f32[256,128]{1,0:T(8,128)S(1)}, u32[]{:S(2)}, u32[]{:S(2)}) collective-permute-start(f32[256,128]{1,0:T(8,128)S(1)} %get-tuple-element.19), channel_id=1, source_target_pairs={{0,1},{1,2},{2,3},{3,4},{4,5},{5,6},{6,7},{7,8},{8,9},{9,10},{10,1... | collective-permute-start | bytes 393224 | tf_op jit(solution)/shard_map/ppermute | solution.py:364
  10.5 7.4 %collective-permute-start.3 = (f32[256,128]{1,0:T(8,128)S(1)}, f32[256,128]{1,0:T(8,128)S(1)}, u32[]{:S(2)}, u32[]{:S(2)}) collective-permute-start(f32[256,128]{1,0:T(8,128)S(1)} %get-tuple-element.20), channel_id=1, source_target_pairs={{0,15},{1,0},{2,1},{3,2},{4,3},{5,4},{6,5},{7,6},{8,7},{9,8},{10,9... | collective-permute-start | bytes 393224 | tf_op jit(solution)/shard_map/ppermute | solution.py:364
  15.3 3.4 %collective-permute-start.4 = (f32[64,128]{1,0:T(8,128)S(1)}, f32[64,128]{1,0:T(8,128)S(1)}, u32[]{:S(2)}, u32[]{:S(2)}) collective-permute-start(f32[64,128]{1,0:T(8,128)S(1)} %get-tuple-element.21), channel_id=1, source_target_pairs={{0,1},{1,2},{2,3},{3,4},{4,5},{5,6},{6,7},{7,8},{8,9},{9,10},{10,1... | collective-permute-start | bytes 98312 | tf_op jit(solution)/shard_map/ppermute | solution.py:364
  17.6 3.4 %copy-start = (f32[2,4,128,128]{3,2,1,0:T(8,128)S(1)}, f32[2,4,128,128]{3,2,1,0:T(8,128)}, u32[]{:S(2)}) copy-start(f32[2,4,128,128]{3,2,1,0:T(8,128)} %probe_ref.1) | copy-start | bytes 1572868
  17.6 3.4 %copy-start.3 = (f32[1,1,3,128,128]{4,3,2,1,0:T(8,128)S(1)}, f32[1,1,3,128,128]{4,3,2,1,0:T(8,128)}, u32[]{:S(2)}) copy-start(f32[1,1,3,128,128]{4,3,2,1,0:T(8,128)} %param.8) | copy-start | bytes 589828
  17.7 3.4 %copy-start.4 = (s32[1,1,3,2]{2,3,1,0:T(2,128)S(1)}, s32[1,1,3,2]{2,3,1,0:T(2,128)}, u32[]{:S(2)}) copy-start(s32[1,1,3,2]{2,3,1,0:T(2,128)} %param.7) | copy-start | bytes 76
  17.7 3.4 %copy-start.5 = (bf16[4,2,256,256]{3,2,1,0:T(8,128)(2,1)S(1)}, bf16[4,2,256,256]{3,2,1,0:T(8,128)(2,1)}, u32[]{:S(2)}) copy-start(bf16[4,2,256,256]{3,2,1,0:T(8,128)(2,1)} %constant.2.clone.mat_ref) | copy-start | bytes 3145732
  17.7 3.4 %collective-permute-start.5 = (f32[64,128]{1,0:T(8,128)S(1)}, f32[64,128]{1,0:T(8,128)S(1)}, u32[]{:S(2)}, u32[]{:S(2)}) collective-permute-start(f32[64,128]{1,0:T(8,128)S(1)} %get-tuple-element.22), channel_id=1, source_target_pairs={{0,15},{1,0},{2,1},{3,2},{4,3},{5,4},{6,5},{7,6},{8,7},{9,8},{10,9... | collective-permute-start | bytes 98312 | tf_op jit(solution)/shard_map/ppermute | solution.py:364
  29.4 22.7 %all-to-all-start = ((f32[128,8,128]{2,1,0:T(8,128)}), f32[128,8,128]{2,1,0:T(8,128)S(1)}, u32[]{:S(2)}, u32[]{:S(2)}) async-start(f32[128,8,128]{2,1,0:T(8,128)} %bitcast.4), calls=%async_computation | async-start | bytes 1048576 | tf_op jit(solution)/shard_map/all_to_all | solution.py:435
  38.0 19.5 %collective-permute-start.8 = (f32[320,128]{1,0:T(8,128)S(1)}, f32[320,128]{1,0:T(8,128)S(1)}, u32[]{:S(2)}, u32[]{:S(2)}) collective-permute-start(f32[320,128]{1,0:T(8,128)S(1)} %get-tuple-element.26), channel_id=1, source_target_pairs={{0,1},{1,2},{2,3},{3,4},{4,5},{5,6},{6,7},{7,8},{8,9},{9,10},{10,1... | collective-permute-start | bytes 491528 | tf_op jit(solution)/shard_map/ppermute | solution.py:364
  39.7 17.8 %collective-permute-start.9 = (f32[320,128]{1,0:T(8,128)S(1)}, f32[320,128]{1,0:T(8,128)S(1)}, u32[]{:S(2)}, u32[]{:S(2)}) collective-permute-start(f32[320,128]{1,0:T(8,128)S(1)} %get-tuple-element.27), channel_id=1, source_target_pairs={{0,15},{1,0},{2,1},{3,2},{4,3},{5,4},{6,5},{7,6},{8,7},{9,8},{10,9... | collective-permute-start | bytes 491528 | tf_op jit(solution)/shard_map/ppermute | solution.py:364
  39.7 23.2 %collective-permute-start.6 = (f32[4,32,256]{2,1,0:T(8,128)S(1)}, f32[4,32,256]{2,1,0:T(8,128)S(1)}, u32[]{:S(2)}, u32[]{:S(2)}) collective-permute-start(f32[4,32,256]{2,1,0:T(8,128)S(1)} %get-tuple-element.24), channel_id=1, source_target_pairs={{0,16},{16,32},{32,48},{48,64},{64,80},{80,96},{96,112},{112,0},{1... | collective-permute-start | bytes 393224 | tf_op jit(solution)/shard_map/ppermute | solution.py:364
  42.1 20.8 %collective-permute-start.7 = (f32[4,32,256]{2,1,0:T(8,128)S(1)}, f32[4,32,256]{2,1,0:T(8,128)S(1)}, u32[]{:S(2)}, u32[]{:S(2)}) collective-permute-start(f32[4,32,256]{2,1,0:T(8,128)S(1)} %get-tuple-element.25), channel_id=1, source_target_pairs={{0,112},{16,0},{32,16},{48,32},{64,48},{80,64},{96,80},{112,96},{1... | collective-permute-start | bytes 393224 | tf_op jit(solution)/shard_map/ppermute | solution.py:364
  53.1 18.7 %all-to-all-start.1 = ((f32[128,8,128]{2,1,0:T(8,128)}), f32[128,8,128]{2,1,0:T(8,128)S(1)}, u32[]{:S(2)}, u32[]{:S(2)}) async-start(f32[128,8,128]{2,1,0:T(8,128)} %shard_map.74), calls=%async_computation.1 | async-start | bytes 1048576 | tf_op jit(solution)/shard_map/all_to_all | solution.py:451
  57.5 11.6 %collective-permute-start.10 = (f32[64,128]{1,0:T(8,128)S(1)}, f32[64,128]{1,0:T(8,128)S(1)}, u32[]{:S(2)}, u32[]{:S(2)}) collective-permute-start(f32[64,128]{1,0:T(8,128)S(1)} %get-tuple-element.31), channel_id=1, source_target_pairs={{0,16},{16,32},{32,48},{48,64},{64,80},{80,96},{96,112},{112,0},{1... | collective-permute-start | bytes 98312 | tf_op jit(solution)/shard_map/ppermute | solution.py:364
  60.5 8.6 %collective-permute-start.11 = (f32[64,128]{1,0:T(8,128)S(1)}, f32[64,128]{1,0:T(8,128)S(1)}, u32[]{:S(2)}, u32[]{:S(2)}) collective-permute-start(f32[64,128]{1,0:T(8,128)S(1)} %get-tuple-element.32), channel_id=1, source_target_pairs={{0,112},{16,0},{32,16},{48,32},{64,48},{80,64},{96,80},{112,96},{1... | collective-permute-start | bytes 98312 | tf_op jit(solution)/shard_map/ppermute | solution.py:364

commit v10 on v8

--- a/solution.py
+++ b/solution.py
@@ -281,15 +281,6 @@
     for k, ref in enumerate((from_west_ref, from_east_ref)):
         to_north_ref[k * HALO : (k + 1) * HALO, :] = ref[0:HALO, :]
         to_south_ref[k * HALO : (k + 1) * HALO, :] = ref[ref.shape[0] - HALO :, :]
-
-
-def add_kernel(left_ref, right_ref, out_ref):
-    out_ref[...] = left_ref[...] + right_ref[...]
-
-
-def share_kernel(parts_ref, *refs):
-    share_ref = refs[-1]
-    share_ref[...] = jnp.broadcast_to(jnp.sum(parts_ref[...], axis=0)[None], share_ref.shape)
 
 
 def from_sides(left, right, p):
@@ -429,13 +420,13 @@
     )
 
     got = lax.ppermute(send, "core", SWAP)
-    half_sum = call(add_kernel, f32(MODES, WIN, WIN), 2)(keep, got)
+    half_sum = keep + got
     parts = lax.all_to_all(half_sum.reshape(axis_count(PEERS), -1, LANES), PEERS, 0, 0, tiled=True)
     rim_from_west = moved(east_rim, COL, 1)
     rim_from_east = moved(west_rim, COL, -1)
     from_south = moved(north_rim, "row", -1)
     from_north = moved(south_rim, "row", 1)
-    share = call(share_kernel, f32(*parts.shape), 1)(parts)
+    share = jnp.broadcast_to(jnp.sum(parts, axis=0)[None], parts.shape)
     mine = lax.all_to_all(share, PEERS, 0, 0, tiled=True).reshape(MODES * WIN, WIN)
     other = lax.ppermute(mine, "core", SWAP)
     to_north, to_south = call(rim_corner_kernel, [f32(2 * HALO, LANES)] * 2, 2, us=80)(rim_from_west, rim_from_east)

time: 72.6 us -> 72.6 us (level)
  Pallas kernels: 12.4 us -> 10.9 us
  other arithmetic: 0 us -> 0.81 us
  local copies, waits for them, and re-layouts: 2.24 us -> 2.97 us
    pallas_call x2 -> x0, Pallas kernels: 1.52 us -> none  [the longest x1 0.79 us: on_device(): share = call(share_kernel, f32(*parts.shape), 1)(parts)]
    add x0 -> x1, other arithmetic: none -> 0.74 us  [on_device(): half_sum = keep + got]
  transfers between devices with their start and end apart: 16 -> 16, of which waited for: 6 -> 6; matrix products, arithmetic and copies ran while one was open for 0% -> 1% of each run, Pallas kernels for 3% -> 2%
where the time goes in v10:
time: 72.6 us; the launch traced here: 72.3 us
  starting transfers between devices  40.5 us (56%)
  waiting for transfers between devices  16.2 us (22%)
  Pallas kernels  10.9 us (15%)
  local copies, waits for them, and re-layouts  2.97 us (4%)
  between operations  0.95 us (1%)
  other arithmetic  0.81 us (1%)
    ppermute x12, starting transfers between devices, moved(): lax.ppermute(block, axis, [(i, (i + distance) % count) for i in range(cou...  21.7 us
    pallas_call x1, Pallas kernels, main_call(): return lambda *args: run(*args)[:7]  8.1 us
    all_to_all x1, starting transfers between devices, on_device(): lax.all_to_all(half_sum.reshape(axis_count(PEERS), -1, LANES), PEERS, 0,...  8.01 us
    ppermute x12, waiting for transfers between devices, moved(): lax.ppermute(block, axis, [(i, (i + distance) % count) for i in range(cou...  7.91 us
    all_to_all x1, starting transfers between devices, on_device(): lax.all_to_all(share, PEERS, 0, 0, tiled=True).reshape(MODES * WIN, WIN)  4.65 us
    ppermute x1, starting transfers between devices, on_device(): other = lax.ppermute(mine, 'core', SWAP)  4.16 us
    all_to_all x1, waiting for transfers between devices, on_device(): lax.all_to_all(share, PEERS, 0, 0, tiled=True).reshape(MODES * WIN, WIN)  4.16 us
    all_to_all x1, waiting for transfers between devices, on_device(): lax.all_to_all(half_sum.reshape(axis_count(PEERS), -1, LANES), PEERS, 0,...  2.95 us
  transfers between devices with their start and end apart: 16, of which 6 were waited for; matrix products, arithmetic and copies ran while one was open for 1% of the time, Pallas kernels for 2%

profile of v10, /device:TPU:1, one launch (start us, length us, event | category | flops | bytes accessed | tf_op | source)
XLA Modules:
  0.0 72.3 jit_solution(10895215368035341638)
XLA Ops:
  0.6 1.0 %fusion = (f32[4,32,256]{2,1,0:T(8,128)S(1)}, f32[4,32,256]{2,1,0:T(8,128)S(1)}) fusion(f32[4,256,256]{2,1,0:T(8,128)} %bitcast.14), kind=kLoop, calls=%fused_computation | loop fusion | bytes 524288 | tf_op jit(solution)/shard_map/slice | solution.py:409
  1.6 6.1 %collective-permute-start.1 = (f32[4,32,256]{2,1,0:T(8,128)S(1)}, f32[4,32,256]{2,1,0:T(8,128)S(1)}, u32[]{:S(2)}, u32[]{:S(2)}) collective-permute-start(f32[4,32,256]{2,1,0:T(8,128)S(1)} %get-tuple-element.38), channel_id=1, source_target_pairs={{0,112},{16,0},{32,16},{48,32},{64,48},{80,64},{96,80},{112,96},{1... | collective-permute-start | bytes 393224 | tf_op jit(solution)/shard_map/ppermute | solution.py:353
  7.7 0.0 collective-permute-start
  7.7 0.0 copy-start.2
  7.7 1.2 %copy-done.2 = f32[2,2,256,256]{3,2,1,0:T(8,128)S(1)} copy-done((f32[2,2,256,256]{3,2,1,0:T(8,128)S(1)}, f32[2,2,256,256]{3,2,1,0:T(8,128)}, u32[]{:S(2)}) %copy-start.2) | copy-done | bytes 1048600
  8.9 0.3 shard_map.69
  9.2 0.0 copy-start.3
  9.2 1.2 %collective-permute-start.2 = (f32[256,128]{1,0:T(8,128)S(1)}, f32[256,128]{1,0:T(8,128)S(1)}, u32[]{:S(2)}, u32[]{:S(2)}) collective-permute-start(f32[256,128]{1,0:T(8,128)S(1)} %get-tuple-element.20), channel_id=1, source_target_pairs={{0,1},{1,2},{2,3},{3,4},{4,5},{5,6},{6,7},{7,8},{8,9},{9,10},{10,1... | collective-permute-start | bytes 393224 | tf_op jit(solution)/shard_map/ppermute | solution.py:353
  10.5 0.0 collective-permute-start.3
  10.5 0.0 collective-permute-done.1.south_ref
  10.5 4.7 %collective-permute-done.north_ref = f32[4,32,256]{2,1,0:T(8,128)S(1)} collective-permute-done((f32[4,32,256]{2,1,0:T(8,128)S(1)}, f32[4,32,256]{2,1,0:T(8,128)S(1)}, u32[]{:S(2)}, u32[]{:S(2)}) %collective-permute-start) | collective-permute-done | bytes 131104 | tf_op jit(solution)/shard_map/ppermute | solution.py:353
  15.2 0.1 shard_map.70
  15.3 2.4 %collective-permute-start.4 = (f32[64,128]{1,0:T(8,128)S(1)}, f32[64,128]{1,0:T(8,128)S(1)}, u32[]{:S(2)}, u32[]{:S(2)}) collective-permute-start(f32[64,128]{1,0:T(8,128)S(1)} %get-tuple-element.22), channel_id=1, source_target_pairs={{0,1},{1,2},{2,3},{3,4},{4,5},{5,6},{6,7},{7,8},{8,9},{9,10},{10,1... | collective-permute-start | bytes 98312 | tf_op jit(solution)/shard_map/ppermute | solution.py:353
  17.6 0.0 copy-start
  17.6 0.0 copy-start.4
  17.7 0.0 copy-start.5
  17.7 0.0 copy-start.6
  17.7 0.1 collective-permute-start.5
  17.7 0.0 copy-done.3
  17.8 0.1 shard_map.68.ext_in
  17.8 0.0 collective-permute-done.2.from_west_ref
  17.9 0.0 collective-permute-done.3.from_east_ref
  17.9 0.8 %collective-permute-done.4.west_corners_ref = f32[64,128]{1,0:T(8,128)S(1)} collective-permute-done((f32[64,128]{1,0:T(8,128)S(1)}, f32[64,128]{1,0:T(8,128)S(1)}, u32[]{:S(2)}, u32[]{:S(2)}) %collective-permute-start.4) | collective-permute-done | bytes 32800 | tf_op jit(solution)/shard_map/ppermute | solution.py:353
  18.7 2.4 %collective-permute-done.5.east_corners_ref = f32[64,128]{1,0:T(8,128)S(1)} collective-permute-done((f32[64,128]{1,0:T(8,128)S(1)}, f32[64,128]{1,0:T(8,128)S(1)}, u32[]{:S(2)}, u32[]{:S(2)}) %collective-permute-start.5) | collective-permute-done | bytes 32800 | tf_op jit(solution)/shard_map/ppermute | solution.py:353
  21.1 0.0 copy-done
  21.1 0.0 copy-done.4
  21.1 0.0 copy-done.5
  21.1 0.0 copy-done.6
  21.1 8.1 %shard_map.71 = (f32[4,128,128]{2,1,0:T(8,128)S(1)}, f32[4,128,128]{2,1,0:T(8,128)S(1)}, f32[4,256,256]{2,1,0:T(8,128)S(1)}, f32[4,32,256]{2,1,0:T(8,128)S(1)}, ...) custom-call(s32[2,3]{1,0:T(2,128)S(1)} %bitcast.18, ...), custom_call_target="tpu_custom_call", output_to_operand_aliasing={{7}: (2, {})} | custom-call | flops 12000000000 | bytes 36000000 | tf_op jit(solution)/shard_map/pallas_call | solution.py:394
  29.2 2.0 %collective-permute-start.12 = (f32[4,128,128]{2,1,0:T(8,128)S(1)}, f32[4,128,128]{2,1,0:T(8,128)S(1)}, u32[]{:S(2)}, u32[]{:S(2)}) collective-permute-start(f32[4,128,128]{2,1,0:T(8,128)S(1)} %get-tuple-element.35), channel_id=1, source_target_pairs={{0,1},{1,0},{2,3},{3,2},{4,5},{5,4},{6,7},{7,6},{8,9},{9,8},{10,11... | collective-permute-start | bytes 786440 | tf_op jit(solution)/shard_map/ppermute | solution.py:422
  31.2 1.2 %collective-permute-done.12 = f32[4,128,128]{2,1,0:T(8,128)S(1)} collective-permute-done((f32[4,128,128]{2,1,0:T(8,128)S(1)}, f32[4,128,128]{2,1,0:T(8,128)S(1)}, u32[]{:S(2)}, u32[]{:S(2)}) %collective-permute-start.12) | collective-permute-done | bytes 262176 | tf_op jit(solution)/shard_map/ppermute | solution.py:422
  32.3 0.7 %add.3 = f32[4,128,128]{2,1,0:T(8,128)} add(f32[4,128,128]{2,1,0:T(8,128)S(1)} %get-tuple-element.34, f32[4,128,128]{2,1,0:T(8,128)S(1)} %collective-permute-done.12) | non-fusion elementwise | flops 65536 | bytes 786432 | tf_op jit(solution)/shard_map/add | solution.py:423
  33.1 8.0 %all-to-all-start = ((f32[64,8,128]{2,1,0:T(8,128)}), f32[64,8,128]{2,1,0:T(8,128)S(1)}, u32[]{:S(2)}, u32[]{:S(2)}) async-start(f32[64,8,128]{2,1,0:T(8,128)} %bitcast.5), calls=%async_computation | async-start | bytes 524288 | tf_op jit(solution)/shard_map/all_to_all | solution.py:424
  41.1 1.7 %collective-permute-start.8 = (f32[320,128]{1,0:T(8,128)S(1)}, f32[320,128]{1,0:T(8,128)S(1)}, u32[]{:S(2)}, u32[]{:S(2)}) collective-permute-start(f32[320,128]{1,0:T(8,128)S(1)} %get-tuple-element.27), channel_id=1, source_target_pairs={{0,1},{1,2},{2,3},{3,4},{4,5},{5,6},{6,7},{7,8},{8,9},{9,10},{10,1... | collective-permute-start | bytes 491528 | tf_op jit(solution)/shard_map/ppermute | solution.py:353
  42.8 0.0 collective-permute-start.9
  42.8 2.4 %collective-permute-start.6 = (f32[4,32,256]{2,1,0:T(8,128)S(1)}, f32[4,32,256]{2,1,0:T(8,128)S(1)}, u32[]{:S(2)}, u32[]{:S(2)}) collective-permute-start(f32[4,32,256]{2,1,0:T(8,128)S(1)} %get-tuple-element.25), channel_id=1, source_target_pairs={{0,16},{16,32},{32,48},{48,64},{64,80},{80,96},{96,112},{112,0},{1... | collective-permute-start | bytes 393224 | tf_op jit(solution)/shard_map/ppermute | solution.py:353
  45.2 2.7 %collective-permute-start.7 = (f32[4,32,256]{2,1,0:T(8,128)S(1)}, f32[4,32,256]{2,1,0:T(8,128)S(1)}, u32[]{:S(2)}, u32[]{:S(2)}) collective-permute-start(f32[4,32,256]{2,1,0:T(8,128)S(1)} %get-tuple-element.26), channel_id=1, source_target_pairs={{0,112},{16,0},{32,16},{48,32},{64,48},{80,64},{96,80},{112,96},{1... | collective-permute-start | bytes 393224 | tf_op jit(solution)/shard_map/ppermute | solution.py:353
  47.8 2.9 %all-to-all-done = f32[64,8,128]{2,1,0:T(8,128)S(1)} async-done(((f32[64,8,128]{2,1,0:T(8,128)}), f32[64,8,128]{2,1,0:T(8,128)S(1)}, u32[]{:S(2)}, u32[]{:S(2)}) %all-to-all-start) | async-done | bytes 262176 | tf_op jit(solution)/shard_map/all_to_all | solution.py:424
  50.8 0.1 reduce_sum.9
  50.9 0.7 %broadcast_in_dim.2 = f32[64,8,128]{2,1,0:T(8,128)} broadcast(f32[8,128]{1,0:T(8,128)S(1)} %reduce_sum.9), dimensions={1,2} | broadcast | bytes 266240 | tf_op jit(solution)/shard_map/broadcast_in_dim | solution.py:429
  51.6 4.6 %all-to-all-start.1 = ((f32[64,8,128]{2,1,0:T(8,128)}), f32[64,8,128]{2,1,0:T(8,128)S(1)}, u32[]{:S(2)}, u32[]{:S(2)}) async-start(f32[64,8,128]{2,1,0:T(8,128)} %broadcast_in_dim.2), calls=%async_computation.1 | async-start | bytes 524288 | tf_op jit(solution)/shard_map/all_to_all | solution.py:430
  56.2 0.0 collective-permute-done.8.from_west_ref
  56.3 0.0 collective-permute-done.9.from_east_ref
  56.3 2.6 %collective-permute-start.10 = (f32[64,128]{1,0:T(8,128)S(1)}, f32[64,128]{1,0:T(8,128)S(1)}, u32[]{:S(2)}, u32[]{:S(2)}) collective-permute-start(f32[64,128]{1,0:T(8,128)S(1)} %get-tuple-element.32), channel_id=1, source_target_pairs={{0,16},{16,32},{32,48},{48,64},{64,80},{80,96},{96,112},{112,0},{1... | collective-permute-start | bytes 98312 | tf_op jit(solution)/shard_map/ppermute | solution.py:353
  58.9 2.6 %collective-permute-start.11 = (f32[64,128]{1,0:T(8,128)S(1)}, f32[64,128]{1,0:T(8,128)S(1)}, u32[]{:S(2)}, u32[]{:S(2)}) collective-permute-start(f32[64,128]{1,0:T(8,128)S(1)} %get-tuple-element.33), channel_id=1, source_target_pairs={{0,112},{16,0},{32,16},{48,32},{64,48},{80,64},{96,80},{112,96},{1... | collective-permute-start | bytes 98312 | tf_op jit(solution)/shard_map/ppermute | solution.py:353
  61.4 4.2 %all-to-all-done.1 = f32[64,8,128]{2,1,0:T(8,128)S(1)} async-done(((f32[64,8,128]{2,1,0:T(8,128)}), f32[64,8,128]{2,1,0:T(8,128)S(1)}, u32[]{:S(2)}, u32[]{:S(2)}) %all-to-all-start.1) | async-done | bytes 262176 | tf_op jit(solution)/shard_map/all_to_all | solution.py:430
  65.6 4.2 %collective-permute-start.13 = (f32[512,128]{1,0:T(8,128)S(1)}, f32[512,128]{1,0:T(8,128)S(1)}, u32[]{:S(2)}, u32[]{:S(2)}) collective-permute-start(f32[512,128]{1,0:T(8,128)S(1)} %bitcast.11), channel_id=1, source_target_pairs={{0,1},{1,0},{2,3},{3,2},{4,5},{5,4},{6,7},{7,6},{8,9},{9,8},{10,11... | collective-permute-start | bytes 786440 | tf_op jit(solution)/shard_map/ppermute | solution.py:431
  69.8 0.0 collective-permute-done.6.from_north_ref
  69.8 0.0 collective-permute-done.7.from_south_ref
  69.8 0.0 copy-start.1
  69.8 1.2 %shard_map.72 = (f32[4,256,256]{2,1,0:T(8,128)}, f32[4,32,256]{2,1,0:T(8,128)S(1)}, f32[4,32,256]{2,1,0:T(8,128)S(1)}) custom-call(f32[4,256,256]{2,1,0:T(8,128)S(1)} %get-tuple-element.24.center_ref, f32[4,32,256]{2,1,0:T(8,128)S(1)} %collective-permute-done.6.from_north_ref, f32[4,32,256]{2,1,0:T(8,128)S(1)} %collective-permute-done.7.from_south_ref, ...), custom_call_target="tpu_custom_call" | custom-call | flops 80000000000 | bytes 240000000 | tf_op jit(solution)/shard_map/pallas_call | solution.py:436
  71.0 0.0 collective-permute-done.10.north_corners_ref
  71.0 0.0 collective-permute-done.11.south_corners_ref
  71.0 0.0 collective-permute-done.13.other_ref
  71.0 0.0 copy-done.1
  71.0 1.1 %shard_map.74 = (f32[4,256,256]{2,1,0:T(8,128)}, f32[2,512,128]{2,1,0:T(8,128)}) custom-call(f32[4,256,256]{2,1,0:T(8,128)} %get-tuple-element.29.object_in, f32[4,32,256]{2,1,0:T(8,128)S(1)} %get-tuple-element.30.north_ref, f32[4,32,256]{2,1,0:T(8,128)S(1)} %get-tuple-element.31.south_ref, ...), custom_call_target="tpu_custom_call", output_to_operand_aliasing={{0}: (0, {})} | custom-call | tf_op jit(solution)/shard_map/pallas_call | solution.py:440
  (1 shorter events, 0.0 us)
Async XLA Ops:
  1.6 8.8 %collective-permute-start.1 = (f32[4,32,256]{2,1,0:T(8,128)S(1)}, f32[4,32,256]{2,1,0:T(8,128)S(1)}, u32[]{:S(2)}, u32[]{:S(2)}) collective-permute-start(f32[4,32,256]{2,1,0:T(8,128)S(1)} %get-tuple-element.38), channel_id=1, source_target_pairs={{0,112},{16,0},{32,16},{48,32},{64,48},{80,64},{96,80},{112,96},{1... | collective-permute-start | bytes 393224 | tf_op jit(solution)/shard_map/ppermute | solution.py:353
  7.7 7.4 %collective-permute-start = (f32[4,32,256]{2,1,0:T(8,128)S(1)}, f32[4,32,256]{2,1,0:T(8,128)S(1)}, u32[]{:S(2)}, u32[]{:S(2)}) collective-permute-start(f32[4,32,256]{2,1,0:T(8,128)S(1)} %get-tuple-element.39), channel_id=1, source_target_pairs={{0,16},{16,32},{32,48},{48,64},{64,80},{80,96},{96,112},{112,0},{1... | collective-permute-start | bytes 393224 | tf_op jit(solution)/shard_map/ppermute | solution.py:353
  7.7 1.2 %copy-start.2 = (f32[2,2,256,256]{3,2,1,0:T(8,128)S(1)}, f32[2,2,256,256]{3,2,1,0:T(8,128)}, u32[]{:S(2)}) copy-start(f32[2,2,256,256]{3,2,1,0:T(8,128)} %param.5) | copy-start | bytes 3145732
  9.2 8.5 %copy-start.3 = (f32[2,2,256,256]{3,2,1,0:T(8,128)S(1)}, f32[2,2,256,256]{3,2,1,0:T(8,128)}, u32[]{:S(2)}) copy-start(f32[2,2,256,256]{3,2,1,0:T(8,128)} %param.5) | copy-start | bytes 3145732
  9.2 8.6 %collective-permute-start.2 = (f32[256,128]{1,0:T(8,128)S(1)}, f32[256,128]{1,0:T(8,128)S(1)}, u32[]{:S(2)}, u32[]{:S(2)}) collective-permute-start(f32[256,128]{1,0:T(8,128)S(1)} %get-tuple-element.20), channel_id=1, source_target_pairs={{0,1},{1,2},{2,3},{3,4},{4,5},{5,6},{6,7},{7,8},{8,9},{9,10},{10,1... | collective-permute-start | bytes 393224 | tf_op jit(solution)/shard_map/ppermute | solution.py:353
  10.5 7.4 %collective-permute-start.3 = (f32[256,128]{1,0:T(8,128)S(1)}, f32[256,128]{1,0:T(8,128)S(1)}, u32[]{:S(2)}, u32[]{:S(2)}) collective-permute-start(f32[256,128]{1,0:T(8,128)S(1)} %get-tuple-element.21), channel_id=1, source_target_pairs={{0,15},{1,0},{2,1},{3,2},{4,3},{5,4},{6,5},{7,6},{8,7},{9,8},{10,9... | collective-permute-start | bytes 393224 | tf_op jit(solution)/shard_map/ppermute | solution.py:353
  15.3 3.4 %collective-permute-start.4 = (f32[64,128]{1,0:T(8,128)S(1)}, f32[64,128]{1,0:T(8,128)S(1)}, u32[]{:S(2)}, u32[]{:S(2)}) collective-permute-start(f32[64,128]{1,0:T(8,128)S(1)} %get-tuple-element.22), channel_id=1, source_target_pairs={{0,1},{1,2},{2,3},{3,4},{4,5},{5,6},{6,7},{7,8},{8,9},{9,10},{10,1... | collective-permute-start | bytes 98312 | tf_op jit(solution)/shard_map/ppermute | solution.py:353
  17.6 3.4 %copy-start = (f32[2,4,128,128]{3,2,1,0:T(8,128)S(1)}, f32[2,4,128,128]{3,2,1,0:T(8,128)}, u32[]{:S(2)}) copy-start(f32[2,4,128,128]{3,2,1,0:T(8,128)} %probe_ref.1) | copy-start | bytes 1572868
  17.6 3.4 %copy-start.4 = (f32[1,1,3,128,128]{4,3,2,1,0:T(8,128)S(1)}, f32[1,1,3,128,128]{4,3,2,1,0:T(8,128)}, u32[]{:S(2)}) copy-start(f32[1,1,3,128,128]{4,3,2,1,0:T(8,128)} %param.8) | copy-start | bytes 589828
  17.7 3.4 %copy-start.5 = (s32[1,1,3,2]{2,3,1,0:T(2,128)S(1)}, s32[1,1,3,2]{2,3,1,0:T(2,128)}, u32[]{:S(2)}) copy-start(s32[1,1,3,2]{2,3,1,0:T(2,128)} %param.7) | copy-start | bytes 76
  17.7 3.4 %copy-start.6 = (bf16[4,2,256,256]{3,2,1,0:T(8,128)(2,1)S(1)}, bf16[4,2,256,256]{3,2,1,0:T(8,128)(2,1)}, u32[]{:S(2)}) copy-start(bf16[4,2,256,256]{3,2,1,0:T(8,128)(2,1)} %constant.8.clone.mat_ref) | copy-start | bytes 3145732
  17.7 3.4 %collective-permute-start.5 = (f32[64,128]{1,0:T(8,128)S(1)}, f32[64,128]{1,0:T(8,128)S(1)}, u32[]{:S(2)}, u32[]{:S(2)}) collective-permute-start(f32[64,128]{1,0:T(8,128)S(1)} %get-tuple-element.23), channel_id=1, source_target_pairs={{0,15},{1,0},{2,1},{3,2},{4,3},{5,4},{6,5},{7,6},{8,7},{9,8},{10,9... | collective-permute-start | bytes 98312 | tf_op jit(solution)/shard_map/ppermute | solution.py:353
  29.2 3.1 %collective-permute-start.12 = (f32[4,128,128]{2,1,0:T(8,128)S(1)}, f32[4,128,128]{2,1,0:T(8,128)S(1)}, u32[]{:S(2)}, u32[]{:S(2)}) collective-permute-start(f32[4,128,128]{2,1,0:T(8,128)S(1)} %get-tuple-element.35), channel_id=1, source_target_pairs={{0,1},{1,0},{2,3},{3,2},{4,5},{5,4},{6,7},{7,6},{8,9},{9,8},{10,11... | collective-permute-start | bytes 786440 | tf_op jit(solution)/shard_map/ppermute | solution.py:422
  33.1 17.7 %all-to-all-start = ((f32[64,8,128]{2,1,0:T(8,128)}), f32[64,8,128]{2,1,0:T(8,128)S(1)}, u32[]{:S(2)}, u32[]{:S(2)}) async-start(f32[64,8,128]{2,1,0:T(8,128)} %bitcast.5), calls=%async_computation | async-start | bytes 524288 | tf_op jit(solution)/shard_map/all_to_all | solution.py:424
  41.1 15.2 %collective-permute-start.8 = (f32[320,128]{1,0:T(8,128)S(1)}, f32[320,128]{1,0:T(8,128)S(1)}, u32[]{:S(2)}, u32[]{:S(2)}) collective-permute-start(f32[320,128]{1,0:T(8,128)S(1)} %get-tuple-element.27), channel_id=1, source_target_pairs={{0,1},{1,2},{2,3},{3,4},{4,5},{5,6},{6,7},{7,8},{8,9},{9,10},{10,1... | collective-permute-start | bytes 491528 | tf_op jit(solution)/shard_map/ppermute | solution.py:353
  42.8 13.5 %collective-permute-start.9 = (f32[320,128]{1,0:T(8,128)S(1)}, f32[320,128]{1,0:T(8,128)S(1)}, u32[]{:S(2)}, u32[]{:S(2)}) collective-permute-start(f32[320,128]{1,0:T(8,128)S(1)} %get-tuple-element.28), channel_id=1, source_target_pairs={{0,15},{1,0},{2,1},{3,2},{4,3},{5,4},{6,5},{7,6},{8,7},{9,8},{10,9... | collective-permute-start | bytes 491528 | tf_op jit(solution)/shard_map/ppermute | solution.py:353
  42.8 27.0 %collective-permute-start.6 = (f32[4,32,256]{2,1,0:T(8,128)S(1)}, f32[4,32,256]{2,1,0:T(8,128)S(1)}, u32[]{:S(2)}, u32[]{:S(2)}) collective-permute-start(f32[4,32,256]{2,1,0:T(8,128)S(1)} %get-tuple-element.25), channel_id=1, source_target_pairs={{0,16},{16,32},{32,48},{48,64},{64,80},{80,96},{96,112},{112,0},{1... | collective-permute-start | bytes 393224 | tf_op jit(solution)/shard_map/ppermute | solution.py:353
  45.2 24.6 %collective-permute-start.7 = (f32[4,32,256]{2,1,0:T(8,128)S(1)}, f32[4,32,256]{2,1,0:T(8,128)S(1)}, u32[]{:S(2)}, u32[]{:S(2)}) collective-permute-start(f32[4,32,256]{2,1,0:T(8,128)S(1)} %get-tuple-element.26), channel_id=1, source_target_pairs={{0,112},{16,0},{32,16},{48,32},{64,48},{80,64},{96,80},{112,96},{1... | collective-permute-start | bytes 393224 | tf_op jit(solution)/shard_map/ppermute | solution.py:353
  51.6 14.0 %all-to-all-start.1 = ((f32[64,8,128]{2,1,0:T(8,128)}), f32[64,8,128]{2,1,0:T(8,128)S(1)}, u32[]{:S(2)}, u32[]{:S(2)}) async-start(f32[64,8,128]{2,1,0:T(8,128)} %broadcast_in_dim.2), calls=%async_computation.1 | async-start | bytes 524288 | tf_op jit(solution)/shard_map/all_to_all | solution.py:430
  56.3 14.7 %collective-permute-start.10 = (f32[64,128]{1,0:T(8,128)S(1)}, f32[64,128]{1,0:T(8,128)S(1)}, u32[]{:S(2)}, u32[]{:S(2)}) collective-permute-start(f32[64,128]{1,0:T(8,128)S(1)} %get-tuple-element.32), channel_id=1, source_target_pairs={{0,16},{16,32},{32,48},{48,64},{64,80},{80,96},{96,112},{112,0},{1... | collective-permute-start | bytes 98312 | tf_op jit(solution)/shard_map/ppermute | solution.py:353
  58.9 12.1 %collective-permute-start.11 = (f32[64,128]{1,0:T(8,128)S(1)}, f32[64,128]{1,0:T(8,128)S(1)}, u32[]{:S(2)}, u32[]{:S(2)}) collective-permute-start(f32[64,128]{1,0:T(8,128)S(1)} %get-tuple-element.33), channel_id=1, source_target_pairs={{0,112},{16,0},{32,16},{48,32},{64,48},{80,64},{96,80},{112,96},{1... | collective-permute-start | bytes 98312 | tf_op jit(solution)/shard_map/ppermute | solution.py:353
  65.6 5.4 %collective-permute-start.13 = (f32[512,128]{1,0:T(8,128)S(1)}, f32[512,128]{1,0:T(8,128)S(1)}, u32[]{:S(2)}, u32[]{:S(2)}) collective-permute-start(f32[512,128]{1,0:T(8,128)S(1)} %bitcast.11), channel_id=1, source_target_pairs={{0,1},{1,0},{2,3},{3,2},{4,5},{5,4},{6,7},{7,6},{8,9},{9,8},{10,11... | collective-permute-start | bytes 786440 | tf_op jit(solution)/shard_map/ppermute | solution.py:431
  69.8 1.3 %copy-start.1 = (f32[2,4,128,128]{3,2,1,0:T(8,128)S(1)}, f32[2,4,128,128]{3,2,1,0:T(8,128)}, u32[]{:S(2)}) copy-start(f32[2,4,128,128]{3,2,1,0:T(8,128)} %probe_ref.1) | copy-start | bytes 1572868
